TPU v7x, 32 devices: a whole 2x2x4 slice. The times are simulated.
32 devices in a mesh: dp: 8 (over z, x), fsdp: 4 (over y, core).
Axes of the slice: x: 2, y: 2, z: 4, core: 2. Of those that a mesh axis runs over, the one named last changes fastest.
Arguments:
- tokens: bfloat16 [32768, 768], P(('dp', 'fsdp')), may hold values from -6 to 6
- counts: int32 [32], P(('dp', 'fsdp')), may hold values from 512 to 1024, as said below
- cotangent: bfloat16 [32768, 768], P(('dp', 'fsdp')), may hold values from -6 to 6
- qkv_weight: float32 [768, 2304], P('dp', 'fsdp'), may hold values from -0.21875 to 0.21875
- out_weight: float32 [768, 768], P('dp', 'fsdp'), may hold values from -1.75 to 1.75
- up_weight: float32 [768, 3072], P('dp', 'fsdp'), may hold values from -0.21875 to 0.21875
- down_weight: float32 [3072, 768], P('dp', 'fsdp'), may hold values from -0.109375 to 0.109375
- small_params: float32 [9216], replicated
- statistics: float32 [32, 2, 768, 768], P(('dp', 'fsdp')), as said below
- inverse_roots: float32 [32, 2, 768, 768], P(('dp', 'fsdp')), as said below
- owners: int32 [12], replicated, may hold values from 0 to 31, as said below
Outputs:
- layer_out: bfloat16 [32768, 768], P(('dp', 'fsdp'))
- input_grad: bfloat16 [32768, 768], P(('dp', 'fsdp'))
- grad_qkv: float32 [768, 2304], P('dp', 'fsdp')
- grad_out: float32 [768, 768], P('dp', 'fsdp')
- grad_up: float32 [768, 3072], P('dp', 'fsdp')
- grad_down: float32 [3072, 768], P('dp', 'fsdp')
- grad_small: float32 [9216], replicated
- new_statistics: float32 [32, 2, 768, 768], P(('dp', 'fsdp'))
- new_qkv: float32 [768, 2304], P('dp', 'fsdp')
- new_out: float32 [768, 768], P('dp', 'fsdp')
- new_up: float32 [768, 3072], P('dp', 'fsdp')
- new_down: float32 [3072, 768], P('dp', 'fsdp')
- new_small: float32 [9216], replicated
Inputs may be any that keep to these rules, and one draw needn't show every extreme that they name: `counts`: true patch count of each clip; 1024 is reached by one clip and 512 by another. `owners`: distinct device ranks, rank = dp index * 4 + fsdp index. `statistics`: each slot's two matrices are symmetric. `inverse_roots`: each slot's two matrices are symmetric.
All inputs are finite; a program needn't handle non-finite values.
Results may differ from a plain program's by a relative error of at most 0.017.
Values may be sent and summed in bfloat16 or wider, within the bound.
A program may use at most 320 MiB of HBM per device.

v0:
```python
from functools import partial

import jax
import jax.numpy as jnp
from jax import lax
from jax.sharding import PartitionSpec as P

D = 768
HEADS = 12
HD = 64
FF = 3072
BLOCKS = 12


masked_score = -1000000000.0
decay_rate = 0.5
step_rate = 1.0
small_rate = 0.3
highest = lax.Precision.HIGHEST


def broadcast(value, axis, source):
    kept = jnp.where(lax.axis_index(axis) == source, value, 0).astype(value.dtype)
    return lax.psum(kept, axis)


def layer_norm(values, scale_row, shift_row):
    center = values - jnp.mean(values, axis=-1, keepdims=True)
    spread = jnp.mean(center * center, axis=-1, keepdims=True)
    return center * lax.rsqrt(spread + 1e-06) * scale_row + shift_row


def unpack(small_params):
    pieces = [small_params[number * D : (number + 1) * D] for number in range(8)]
    return pieces + [small_params[8 * D : 8 * D + FF]]


def row_dot(left, right):
    return jnp.dot(left, right, preferred_element_type=jnp.float32)


def column_dot(left, right):
    return lax.dot_general(
        left, right, (((0,), (0,)), ((), ())), preferred_element_type=jnp.float32
    )


def transposed_dot(left, right):
    return lax.dot_general(
        left, right, (((1,), (1,)), ((), ())), preferred_element_type=jnp.float32
    )


def block_split(array, block_rows):
    slots = array.shape[-1]
    return array.reshape(HEADS, HD, slots // block_rows, block_rows).transpose(2, 0, 1, 3)


def block_join(array):
    return array.transpose(0, 3, 1, 2).reshape(-1, D)


def attend_clip(queries, key_rows, value_rows, length):
    slots = queries.shape[-1]
    block_rows = min(512, slots)
    score_scale = float(HD) ** (-0.5)
    visible = (jnp.arange(slots) < length)[None, None, :]

    def one_block(query_block):
        scores = (
            jnp.einsum("hdq,hdk->hqk", query_block, key_rows, preferred_element_type=jnp.float32)
            * score_scale
        )
        scores = jnp.where(visible, scores, masked_score)
        row_top = jnp.max(scores, axis=-1, keepdims=True)
        raised = jnp.exp(scores - row_top)
        row_total = jnp.sum(raised, axis=-1, keepdims=True)
        softmax_weights = (raised / row_total).astype(jnp.bfloat16)
        attended = jnp.einsum(
            "hqk,hdk->hdq", softmax_weights, value_rows, preferred_element_type=jnp.float32
        )
        return (attended.astype(jnp.bfloat16), (row_top + jnp.log(row_total))[:, :, 0])

    attended, log_totals = lax.map(one_block, block_split(queries, block_rows))
    return (block_join(attended), log_totals)


def attend_back(queries, key_rows, value_rows, length, log_totals, out_grads):
    slots = queries.shape[-1]
    block_rows = min(512, slots)
    score_scale = float(HD) ** (-0.5)
    visible = (jnp.arange(slots) < length)[None, None, :]

    def one_block(carry, pieces):
        key_grad, value_grad = carry
        query_block, grad_block, log_block = pieces
        scores = (
            jnp.einsum("hdq,hdk->hqk", query_block, key_rows, preferred_element_type=jnp.float32)
            * score_scale
        )
        scores = jnp.where(visible, scores, masked_score)
        softmax_weights = jnp.exp(scores - log_block[:, :, None])
        weight_grad = jnp.einsum(
            "hdq,hdk->hqk", grad_block, value_rows, preferred_element_type=jnp.float32
        )
        inner_sum = jnp.sum(softmax_weights * weight_grad, axis=-1, keepdims=True)
        score_grad = (softmax_weights * (weight_grad - inner_sum)).astype(jnp.bfloat16)
        query_grad = (
            jnp.einsum("hqk,hdk->hdq", score_grad, key_rows, preferred_element_type=jnp.float32)
            * score_scale
        )
        key_grad = (
            key_grad
            + jnp.einsum(
                "hqk,hdq->hdk", score_grad, query_block, preferred_element_type=jnp.float32
            )
            * score_scale
        )
        value_grad = value_grad + jnp.einsum(
            "hqk,hdq->hdk",
            softmax_weights.astype(jnp.bfloat16),
            grad_block,
            preferred_element_type=jnp.float32,
        )
        return ((key_grad, value_grad), query_grad)

    blank = jnp.zeros((HEADS, HD, slots), jnp.float32)
    (key_grad, value_grad), query_grad = lax.scan(
        one_block,
        (blank, blank),
        (block_split(queries, block_rows), block_split(out_grads, block_rows), log_totals),
    )
    key_rows_grad = key_grad.transpose(2, 0, 1).reshape(slots, D)
    value_rows_grad = value_grad.transpose(2, 0, 1).reshape(slots, D)
    return (block_join(query_grad), key_rows_grad, value_rows_grad)


def take_columns(operands, member, start):
    return lax.slice_in_dim(operands[member], start, start + D, axis=1)


def take_rows(operands, member, start):
    return lax.slice_in_dim(operands[member], start, start + D, axis=0)


def block_pickers():
    pickers = [partial(take_columns, member=0, start=column * D) for column in range(3)]
    pickers.append(partial(take_columns, member=1, start=0))
    pickers = pickers + [
        partial(take_columns, member=2, start=column * D) for column in range(FF // D)
    ]
    pickers = pickers + [
        partial(take_rows, member=3, start=column * D) for column in range(FF // D)
    ]
    return pickers


def fetch_update(update, root):
    return broadcast(update.astype(jnp.bfloat16), ("dp", "fsdp"), root).astype(update.dtype)


def band_tile(band, like, column_index):
    columns_here = like.shape[1]
    return lax.dynamic_slice_in_dim(band, column_index * columns_here, columns_here, 1)


def row_band(pieces, like, row_index):
    rows_here = like.shape[0]
    start = row_index * rows_here
    return jnp.concatenate(
        [lax.dynamic_slice_in_dim(piece, start, rows_here, 0) for piece in pieces], axis=1
    )


def stacked_band(pieces, like, row_index):
    rows_here = like.shape[0]
    start = row_index * rows_here
    owner_block = start // D
    picked = jnp.zeros((rows_here, D), jnp.float32)
    for number in range(len(pieces)):
        inside = jnp.clip(start - number * D, 0, D - rows_here)
        piece = lax.dynamic_slice_in_dim(pieces[number], inside, rows_here, 0)
        picked = jnp.where(owner_block == number, piece, picked)
    return picked


def local(
    tokens,
    counts,
    cotangent,
    qkv_weight,
    out_weight,
    up_weight,
    down_weight,
    small_params,
    statistics,
    inverse_roots,
    owners,
):
    clips_here = counts.shape[0]
    slots = tokens.shape[0] // clips_here
    qkv_low = qkv_weight.astype(jnp.bfloat16)
    out_low = out_weight.astype(jnp.bfloat16)
    up_low = up_weight.astype(jnp.bfloat16)
    down_low = down_weight.astype(jnp.bfloat16)
    qkv_cols, out_cols, up_cols, down_cols = (
        lax.all_gather(qkv_low, "fsdp", axis=1, tiled=True),
        lax.all_gather(out_low, "fsdp", axis=1, tiled=True),
        lax.all_gather(up_low, "fsdp", axis=1, tiled=True),
        lax.all_gather(down_low, "fsdp", axis=1, tiled=True),
    )
    qkv_full, out_full, up_full, down_full = (
        lax.all_gather(qkv_cols, "dp", axis=0, tiled=True),
        lax.all_gather(out_cols, "dp", axis=0, tiled=True),
        lax.all_gather(up_cols, "dp", axis=0, tiled=True),
        lax.all_gather(down_cols, "dp", axis=0, tiled=True),
    )
    (
        gain_one,
        shift_one,
        gain_two,
        shift_two,
        bias_query,
        bias_value,
        bias_out,
        bias_down,
        bias_up,
    ) = unpack(small_params)

    def heads_view(array):
        return array.reshape(clips_here, slots, HEADS, HD).transpose(0, 2, 3, 1)

    def clip_forward(clip_group):
        return attend_clip(clip_group[0], clip_group[1], clip_group[2], clip_group[3])

    def clip_backward(clip_group):
        return attend_back(
            clip_group[0], clip_group[1], clip_group[2], clip_group[3], clip_group[4], clip_group[5]
        )

    inputs = tokens.astype(jnp.float32)
    normed = layer_norm(inputs, gain_one, shift_one).astype(jnp.bfloat16)
    projected = row_dot(normed, qkv_full)
    queries = heads_view((projected[:, :D] + bias_query).astype(jnp.bfloat16))
    key_rows = heads_view(projected[:, D : 2 * D].astype(jnp.bfloat16))
    value_rows = heads_view((projected[:, 2 * D :] + bias_value).astype(jnp.bfloat16))
    attended, log_totals = lax.map(clip_forward, (queries, key_rows, value_rows, counts))
    attended = attended.reshape(-1, D)
    middle = inputs + (row_dot(attended, out_full) + bias_out)
    normed_two = layer_norm(middle, gain_two, shift_two).astype(jnp.bfloat16)
    hidden = row_dot(normed_two, up_full) + bias_up
    active = jax.nn.gelu(hidden, approximate=False).astype(jnp.bfloat16)
    layer_rows = (middle + row_dot(active, down_full) + bias_down).astype(jnp.bfloat16)
    qkv_part, out_part, up_part, down_part = (
        lax.all_gather(qkv_low, "fsdp", axis=1, tiled=True),
        lax.all_gather(out_low, "fsdp", axis=1, tiled=True),
        lax.all_gather(up_low, "fsdp", axis=1, tiled=True),
        lax.all_gather(down_low, "fsdp", axis=1, tiled=True),
    )
    qkv_back, out_back, up_back, down_back = (
        lax.all_gather(qkv_part, "dp", axis=0, tiled=True),
        lax.all_gather(out_part, "dp", axis=0, tiled=True),
        lax.all_gather(up_part, "dp", axis=0, tiled=True),
        lax.all_gather(down_part, "dp", axis=0, tiled=True),
    )
    grad_down = column_dot(active, cotangent)
    grad_bias_down = jnp.sum(cotangent.astype(jnp.float32), axis=0)
    active_grad = transposed_dot(cotangent, down_back)
    unused_value, gelu_pull = jax.vjp(partial(jax.nn.gelu, approximate=False), hidden)
    hidden_grad = gelu_pull(active_grad)[0].astype(jnp.bfloat16)
    grad_up = column_dot(normed_two, hidden_grad)
    grad_bias_up = jnp.sum(hidden_grad.astype(jnp.float32), axis=0)
    normed_two_grad = transposed_dot(hidden_grad, up_back)
    unused_norm, norm_two_pull = jax.vjp(layer_norm, middle, gain_two, shift_two)
    middle_grad, grad_gain_two, grad_shift_two = norm_two_pull(normed_two_grad)
    middle_grad = middle_grad + cotangent.astype(jnp.float32)
    branch_grad = middle_grad.astype(jnp.bfloat16)
    grad_out = column_dot(attended, branch_grad)
    grad_bias_out = jnp.sum(branch_grad.astype(jnp.float32), axis=0)
    attended_grad = transposed_dot(branch_grad, out_back).astype(jnp.bfloat16)
    query_grad, key_grad, value_grad = lax.map(
        clip_backward,
        (queries, key_rows, value_rows, counts, log_totals, heads_view(attended_grad)),
    )
    projected_grad = (
        jnp.concatenate([query_grad, key_grad, value_grad], axis=-1)
        .reshape(-1, 3 * D)
        .astype(jnp.bfloat16)
    )
    grad_qkv = column_dot(normed, projected_grad)
    grad_bias_query = jnp.sum(projected_grad[:, :D].astype(jnp.float32), axis=0)
    grad_bias_value = jnp.sum(projected_grad[:, 2 * D :].astype(jnp.float32), axis=0)
    normed_grad = transposed_dot(projected_grad, qkv_back)
    unused_first, norm_one_pull = jax.vjp(layer_norm, inputs, gain_one, shift_one)
    input_rows_grad, grad_gain_one, grad_shift_one = norm_one_pull(normed_grad)
    input_grad = (middle_grad + input_rows_grad).astype(jnp.bfloat16)
    small_grad = jnp.concatenate(
        [
            grad_gain_one,
            grad_shift_one,
            grad_gain_two,
            grad_shift_two,
            grad_bias_query,
            grad_bias_value,
            grad_bias_out,
            grad_bias_down,
            grad_bias_up,
        ]
    )
    row_qkv, row_out, row_up, row_down, row_small = (
        lax.psum_scatter(
            grad_qkv.astype(jnp.bfloat16), "dp", scatter_dimension=0, tiled=True
        ).astype(jnp.float32),
        lax.psum_scatter(
            grad_out.astype(jnp.bfloat16), "dp", scatter_dimension=0, tiled=True
        ).astype(jnp.float32),
        lax.psum_scatter(
            grad_up.astype(jnp.bfloat16), "dp", scatter_dimension=0, tiled=True
        ).astype(jnp.float32),
        lax.psum_scatter(
            grad_down.astype(jnp.bfloat16), "dp", scatter_dimension=0, tiled=True
        ).astype(jnp.float32),
        lax.psum_scatter(
            small_grad.astype(jnp.bfloat16), "dp", scatter_dimension=0, tiled=True
        ).astype(jnp.float32),
    )
    shard_qkv, shard_out, shard_up, shard_down, shard_small = (
        lax.psum_scatter(
            row_qkv.astype(jnp.bfloat16), "fsdp", scatter_dimension=1, tiled=True
        ).astype(jnp.float32),
        lax.psum_scatter(
            row_out.astype(jnp.bfloat16), "fsdp", scatter_dimension=1, tiled=True
        ).astype(jnp.float32),
        lax.psum_scatter(
            row_up.astype(jnp.bfloat16), "fsdp", scatter_dimension=1, tiled=True
        ).astype(jnp.float32),
        lax.psum_scatter(
            row_down.astype(jnp.bfloat16), "fsdp", scatter_dimension=1, tiled=True
        ).astype(jnp.float32),
        lax.psum_scatter(
            row_small.astype(jnp.bfloat16), "fsdp", scatter_dimension=0, tiled=True
        ).astype(jnp.float32),
    )
    band_qkv, band_out, band_up, band_down, band_small = (
        lax.all_gather(shard_qkv.astype(jnp.bfloat16), "fsdp", axis=1, tiled=True).astype(
            shard_qkv.dtype
        ),
        lax.all_gather(shard_out.astype(jnp.bfloat16), "fsdp", axis=1, tiled=True).astype(
            shard_out.dtype
        ),
        lax.all_gather(shard_up.astype(jnp.bfloat16), "fsdp", axis=1, tiled=True).astype(
            shard_up.dtype
        ),
        lax.all_gather(shard_down.astype(jnp.bfloat16), "fsdp", axis=1, tiled=True).astype(
            shard_down.dtype
        ),
        lax.all_gather(shard_small.astype(jnp.bfloat16), "fsdp", axis=0, tiled=True).astype(
            shard_small.dtype
        ),
    )
    rank = lax.axis_index(("dp", "fsdp"))
    row_index = lax.axis_index("dp")
    column_index = lax.axis_index("fsdp")
    numbers = jnp.arange(BLOCKS, dtype=jnp.int32)
    matches = owners == rank
    mine = jnp.sum(jnp.where(matches, numbers, 0))
    owning = jnp.any(matches)

    def update_slot(gradient):
        left_stat = decay_rate * statistics[0, 0] + (1.0 - decay_rate) * jnp.dot(
            gradient, gradient.T, precision=highest, preferred_element_type=jnp.float32
        )
        right_stat = decay_rate * statistics[0, 1] + (1.0 - decay_rate) * jnp.dot(
            gradient.T, gradient, precision=highest, preferred_element_type=jnp.float32
        )
        left_step = jnp.dot(
            inverse_roots[0, 0], gradient, precision=highest, preferred_element_type=jnp.float32
        )
        update = jnp.dot(
            left_step, inverse_roots[0, 1], precision=highest, preferred_element_type=jnp.float32
        )
        return (jnp.stack([left_stat, right_stat])[None], update)

    def keep_slot(gradient):
        return (statistics, jnp.zeros((D, D), jnp.float32))

    whole_qkv, whole_out, whole_up, whole_down, whole_small = (
        lax.all_gather(band_qkv.astype(jnp.bfloat16), "dp", axis=0, tiled=True).astype(
            band_qkv.dtype
        ),
        lax.all_gather(band_out.astype(jnp.bfloat16), "dp", axis=0, tiled=True).astype(
            band_out.dtype
        ),
        lax.all_gather(band_up.astype(jnp.bfloat16), "dp", axis=0, tiled=True).astype(
            band_up.dtype
        ),
        lax.all_gather(band_down.astype(jnp.bfloat16), "dp", axis=0, tiled=True).astype(
            band_down.dtype
        ),
        lax.all_gather(band_small.astype(jnp.bfloat16), "dp", axis=0, tiled=True).astype(
            band_small.dtype
        ),
    )
    gradient = lax.switch(mine, block_pickers(), (whole_qkv, whole_out, whole_up, whole_down))
    new_statistics, update = lax.cond(owning, update_slot, keep_slot, gradient)
    arrivals = []
    for number in range(BLOCKS):
        arrivals.append(fetch_update(update, owners[number]))
    tile_qkv = band_tile(row_band(arrivals[0:3], qkv_weight, row_index), qkv_weight, column_index)
    tile_out = band_tile(row_band(arrivals[3:4], out_weight, row_index), out_weight, column_index)
    tile_up = band_tile(
        row_band(arrivals[4 : 4 + FF // D], up_weight, row_index), up_weight, column_index
    )
    tile_down = band_tile(
        stacked_band(arrivals[4 + FF // D :], down_weight, row_index), down_weight, column_index
    )
    new_qkv = qkv_weight - step_rate * tile_qkv
    new_out = out_weight - step_rate * tile_out
    new_up = up_weight - step_rate * tile_up
    new_down = down_weight - step_rate * tile_down
    new_small = small_params - small_rate * whole_small * lax.rsqrt(
        jnp.mean(whole_small * whole_small) + 1e-06
    )
    return (
        layer_rows,
        input_grad,
        shard_qkv,
        shard_out,
        shard_up,
        shard_down,
        whole_small,
        new_statistics,
        new_qkv,
        new_out,
        new_up,
        new_down,
        new_small,
    )


def solution(mesh):
    placed = (
        P(("dp", "fsdp"), None),
        P(("dp", "fsdp")),
        P(("dp", "fsdp"), None),
        P("dp", "fsdp"),
        P("dp", "fsdp"),
        P("dp", "fsdp"),
        P("dp", "fsdp"),
        P(),
        P(("dp", "fsdp"), None, None, None),
        P(("dp", "fsdp"), None, None, None),
        P(),
    )
    return jax.shard_map(
        local,
        mesh=mesh,
        in_specs=placed,
        out_specs=(
            P(("dp", "fsdp"), None),
            P(("dp", "fsdp"), None),
            P("dp", "fsdp"),
            P("dp", "fsdp"),
            P("dp", "fsdp"),
            P("dp", "fsdp"),
            P(),
            P(("dp", "fsdp"), None, None, None),
            P("dp", "fsdp"),
            P("dp", "fsdp"),
            P("dp", "fsdp"),
            P("dp", "fsdp"),
            P(),
        ),
        check_vma=False,
    )
```

profile of v0, /device:TPU:27, one launch (start us, length us, event | category | flops | bytes accessed | tf_op | source)
XLA Modules:
  0.0 1504.1 jit_solution(5191103674072602303)
XLA Ops:
  49.9 34.4 %all-gather.12.cloned.1.call-done = bf16[768,2304]{1,0:T(8,128)(2,1)} async-done(((bf16[96,2304]{1,0:T(8,128)(2,1)}), bf16[768,2304]{1,0:T(8,128)(2,1)}) %all-gather.12.cloned.1.call-update) | async-done | bytes 3538960 | tf_op jit(solution)/shard_map/all_gather | solution.py:213
  100.8 70.3 %while.48 = (s32[]{:T(128)}, bf16[2,12,64,512]{3,2,1,0:T(8,128)(2,1)}, f32[2,12,512]{2,1,0:T(8,128)S(1)}, bf16[2,12,64,512]{3,2,1,0:T(8,128)(2,1)S(1)}, bf16[12,...) while((s32[]{:T(128)}, ...), condition=%wide.region_5.6_spmd.clone, body=%wide.region_2.5_spmd.clone.sunk | while | flops 1686498304 | bytes 99332296 | solution.py:84
  181.7 25.5 %all-gather.16.cloned.1.call-done = bf16[768,3072]{1,0:T(8,128)(2,1)} async-done(((bf16[96,3072]{1,0:T(8,128)(2,1)}), bf16[768,3072]{1,0:T(8,128)(2,1)}) %all-gather.16.cloned.1.call-update) | async-done | bytes 4718608 | tf_op jit(solution)/shard_map/all_gather | solution.py:215
  207.2 38.1 %multiply_convert_fusion.1 = (bf16[1024,3072]{1,0:T(8,128)(2,1)}, f32[1024,3072]{1,0:T(8,128)}, f32[1024,3072]{1,0:T(8,128)}) fusion(f32[3072]{0:T(1024)S(1)} %copy-done.65, bf16[768,3072]{1,0:T(8,128)(2,1)} %all-gather.16.cloned.1.call-done, f32[1024,768]{0,1:T(8,128)} %copy-done.6, f32[768]{0:T(1024)S(1)} %copy-done.71, f32[768]{0:T(1024)S(1)} %copy-done.60, ...), kind=kOutput, calls=%fused_computation.63 | convolution fusion | flops 5043388416 | bytes 39348224 | tf_op jit(solution)/shard_map/dot_general | solution.py:39
  245.4 43.0 %all-gather.18.cloned.1.call-done = bf16[3072,768]{0,1:T(8,128)(2,1)} async-done(((bf16[384,768]{0,1:T(8,128)(2,1)}), bf16[3072,768]{0,1:T(8,128)(2,1)}) %all-gather.18.cloned.1.call-update) | async-done | bytes 4718608 | tf_op jit(solution)/shard_map/all_gather | solution.py:216
  288.3 19.0 %fusion.97 = (bf16[3072]{0:T(1024)(128)(2,1)}, bf16[1024,3072]{1,0:T(8,128)(2,1)}) fusion(f32[1024,3072]{1,0:T(8,128)} %get-tuple-element.417, bf16[1024,768]{1,0:T(8,128)(2,1)} %param.31, bf16[3072,768]{0,1:T(8,128)(2,1)} %all-gather.18.cloned.1.call-done, f32[1024,3072]{1,0:T(8,128)} %get-tuple-element.460, f32[3072]{0:T(1024)S(1)} %copy-done.65), kind=kOutput, calls=%fused_computation.179 | convolution fusion | flops 4882166784 | bytes 37767168 | tf_op jit(solution)/shard_map/dot_general | solution.py:49
  341.8 164.2 %while.49 = (s32[]{:T(128)}, f32[12,64,1024]{2,1,0:T(8,128)}, f32[12,64,1024]{2,1,0:T(8,128)}, bf16[2,12,64,512]{3,2,1,0:T(8,128)(2,1)}, bf16[2,12,64,512]{3,2,1...) while((s32[]{:T(128)}, f32[12,64,1024]{2,1,0:T(8,128)}, ...), condition=%wide.region_12.13_spmd.clone, body=%wide.region_10.12_spmd.clone.sunk | while | flops 4125223936 | bytes 217239728 | solution.py:128
  366.3 17.5 %multiply_reduce_fusion.6 = (f32[12,512]{1,0:T(8,128)S(1)}, f32[12,512,1024]{2,1,0:T(8,128)}) fusion(f32[12,512,1024]{2,1,0:T(8,128)} %fusion.158, f32[12,512]{1,0:T(8,128)S(1)} %dynamic-slice_bitcast_fusion.2, pred[1024]{0:T(1024)(128)(4,1)S(1)} %compare_reduce_fusion.6, bf16[12,64,1024]{2,1,0:T(8,128)(2,1)} %get-tuple-element.641, ...), kind=kOutput, calls=%fused_computation.34.clone.1 | convolution fusion | flops 836757504 | bytes 52741124 | tf_op jit(solution)/shard_map/while/body/eval_jaxpr/while/body/eval_jaxpr/hdq,hdk->hqk/dot_general | solution.py:103
  383.9 21.6 %multiply_convert_fusion.3 = bf16[12,512,1024]{2,1,0:T(8,128)(2,1)} fusion(f32[12,512,1024]{2,1,0:T(8,128)} %get-tuple-element.583, f32[12,512,1024]{2,1,0:T(8,128)} %fusion.158, f32[12,512]{1,0:T(8,128)S(1)} %get-tuple-element.584, f32[12,512]{1,0:T(8,128)S(1)} %dynamic-slice_bitcast_fusion.2, pred[1024]{0:T(1024)(128)(4,1)S(1)} %compare_reduce_fusion.6), kind=kLoop, calls=%fused_computation.33.clone.1 | loop fusion | flops 37748736 | bytes 62964736 | tf_op jit(solution)/shard_map/while/body/eval_jaxpr/while/body/eval_jaxpr/convert_element_type | solution.py:107
  448.1 17.4 %multiply_reduce_fusion.6 = (f32[12,512]{1,0:T(8,128)S(1)}, f32[12,512,1024]{2,1,0:T(8,128)}) fusion(f32[12,512,1024]{2,1,0:T(8,128)} %fusion.158, f32[12,512]{1,0:T(8,128)S(1)} %dynamic-slice_bitcast_fusion.2, pred[1024]{0:T(1024)(128)(4,1)S(1)} %compare_reduce_fusion.6, bf16[12,64,1024]{2,1,0:T(8,128)(2,1)} %get-tuple-element.641, ...), kind=kOutput, calls=%fused_computation.34.clone.1 | convolution fusion | flops 836757504 | bytes 52741124 | tf_op jit(solution)/shard_map/while/body/eval_jaxpr/while/body/eval_jaxpr/hdq,hdk->hqk/dot_general | solution.py:103
  465.5 21.5 %multiply_convert_fusion.3 = bf16[12,512,1024]{2,1,0:T(8,128)(2,1)} fusion(f32[12,512,1024]{2,1,0:T(8,128)} %get-tuple-element.583, f32[12,512,1024]{2,1,0:T(8,128)} %fusion.158, f32[12,512]{1,0:T(8,128)S(1)} %get-tuple-element.584, f32[12,512]{1,0:T(8,128)S(1)} %dynamic-slice_bitcast_fusion.2, pred[1024]{0:T(1024)(128)(4,1)S(1)} %compare_reduce_fusion.6), kind=kLoop, calls=%fused_computation.33.clone.1 | loop fusion | flops 37748736 | bytes 62964736 | tf_op jit(solution)/shard_map/while/body/eval_jaxpr/while/body/eval_jaxpr/convert_element_type | solution.py:107
  549.2 53.8 %reduce-scatter.15.cloned.1.call-done = bf16[96,2304]{1,0:T(8,128)(2,1)} async-done(((bf16[768,2304]{1,0:T(8,128)(2,1)}), bf16[96,2304]{1,0:T(8,128)(2,1)}) %reduce-scatter.15.cloned.1.call-update) | async-done | bytes 442384 | tf_op jit(solution)/shard_map/reduce_scatter | solution.py:311
  605.1 97.2 %reduce-scatter.19.cloned.1.call-done = bf16[96,3072]{1,0:T(8,128)(2,1)} async-done(((bf16[768,3072]{1,0:T(8,128)(2,1)}), bf16[96,3072]{1,0:T(8,128)(2,1)}) %reduce-scatter.19.cloned.1.call-update) | async-done | bytes 589840 | tf_op jit(solution)/shard_map/reduce_scatter | solution.py:317
  702.5 98.8 %reduce-scatter.23.cloned.1.call-done = bf16[384,768]{1,0:T(8,128)(2,1)} async-done(((bf16[3072,768]{1,0:T(8,128)(2,1)}), bf16[384,768]{1,0:T(8,128)(2,1)}) %reduce-scatter.23.cloned.1.call-update) | async-done | bytes 589840 | tf_op jit(solution)/shard_map/reduce_scatter | solution.py:320
  803.4 21.1 %reduce-scatter.27.cloned.1.call-done = bf16[192,96]{1,0:T(8,128)(2,1)} async-done(((bf16[768,96]{1,0:T(8,128)(2,1)}), bf16[192,96]{1,0:T(8,128)(2,1)}) %reduce-scatter.27.cloned.1.call-update) | async-done | bytes 36880
  831.9 17.8 %reduce-scatter.25.cloned.1.call-done = bf16[576,96]{1,0:T(8,128)(2,1)} async-done(((bf16[2304,96]{1,0:T(8,128)(2,1)}), bf16[576,96]{1,0:T(8,128)(2,1)}) %reduce-scatter.25.cloned.1.call-update) | async-done | bytes 110608
  919.0 20.9 %all-gather.22.cloned.1.call-done = bf16[768,768]{1,0:T(8,128)(2,1)} async-done(((bf16[96,768]{1,0:T(8,128)(2,1)}), bf16[768,768]{1,0:T(8,128)(2,1)}) %all-gather.22.cloned.1.call-update) | async-done | bytes 1179664 | tf_op jit(solution)/shard_map/all_gather | solution.py:391
  941.3 66.2 %all-gather.20.cloned.1.call-done = bf16[768,2304]{1,0:T(8,128)(2,1)} async-done(((bf16[96,2304]{1,0:T(8,128)(2,1)}), bf16[768,2304]{1,0:T(8,128)(2,1)}) %all-gather.20.cloned.1.call-update) | async-done | bytes 3538960 | tf_op jit(solution)/shard_map/all_gather | solution.py:388
  1012.9 74.7 %all-gather.24.cloned.1.call-done = bf16[768,3072]{1,0:T(8,128)(2,1)} async-done(((bf16[96,3072]{1,0:T(8,128)(2,1)}), bf16[768,3072]{1,0:T(8,128)(2,1)}) %all-gather.24.cloned.1.call-update) | async-done | bytes 4718608 | tf_op jit(solution)/shard_map/all_gather | solution.py:394
  1094.9 73.8 %all-gather.26.cloned.1.call-done = bf16[3072,768]{0,1:T(8,128)(2,1)} async-done(((bf16[384,768]{0,1:T(8,128)(2,1)}), bf16[3072,768]{0,1:T(8,128)(2,1)}) %all-gather.26.cloned.1.call-update) | async-done | bytes 4718608 | tf_op jit(solution)/shard_map/all_gather | solution.py:397
  1246.5 52.6 %all-reduce.1 = bf16[9216]{0:T(1024)(128)(2,1)S(1)} all-reduce(bf16[9216]{0:T(1024)(128)(2,1)S(1)} %constant_dynamic-update-slice_fusion), channel_id=10, replica_groups=mesh['dp'=8,'fsdp'=4] {'dp'}, use_global_device_ids=true, to_apply=%region_32.33.clone | all-reduce | flops 9216 | bytes 36864
  1299.2 16.7 %all-reduce.2 = bf16[1152]{0:T(1024)(128)(2,1)S(1)} all-reduce(bf16[1152]{0:T(1024)(128)(2,1)S(1)} %dynamic-slice.7), channel_id=11, replica_groups=mesh['dp'=8,'fsdp'=4] {'fsdp'}, use_global_device_ids=true, to_apply=%region_33.34.clone | all-reduce | flops 1152 | bytes 4608
  1322.3 24.6 %all-gather.1 = bf16[8,1,1152]{2,1,0:T(2,128)(2,1)S(1)} all-gather(bf16[1,1,1152]{2,1,0:T(2,128)(2,1)S(1)} %reshape.184), channel_id=1, replica_groups=mesh['dp'=8,'fsdp'=4] {'dp'}, dimensions={0}, use_global_device_ids=true | all-gather | bytes 20736 | tf_op jit(solution)/shard_map/all_gather | solution.py:400
  1352.1 134.1 %all-reduce.6.cloned.1.call-done = (bf16[768,768]{0,1:T(8,128)(2,1)}, bf16[768,768]{0,1:T(8,128)(2,1)}, bf16[768,768]{0,1:T(8,128)(2,1)}, bf16[768,768]{0,1:T(8,...) async-done(((bf16[768,768]{0,1:T(8,128)(2,1)}, ...) | async-done | bytes 14155792 | tf_op jit(solution)/shard_map/psum | solution.py:24
  (356 shorter events, 488.0 us)
Async XLA Ops:
  7.2 77.1 %all-gather.12.cloned.1.call-start = ((), (), s32[]{:S(2)}) async-start(), calls=%async_computation.8 | async-start | bytes 3981312 | tf_op jit(solution)/shard_map/all_gather | solution.py:213
  21.3 154.4 %all-gather.14.cloned.1.call-start = ((), (), s32[]{:S(2)}) async-start(), calls=%async_computation.9 | async-start | bytes 1327104 | tf_op jit(solution)/shard_map/all_gather | solution.py:214
  27.9 179.3 %all-gather.16.cloned.1.call-start = ((), (), s32[]{:S(2)}) async-start(), calls=%async_computation.10 | async-start | bytes 5308416 | tf_op jit(solution)/shard_map/all_gather | solution.py:215
  36.1 252.2 %all-gather.18.cloned.1.call-start = ((), (), s32[]{:S(2)}) async-start(), calls=%async_computation.11 | async-start | bytes 5308416 | tf_op jit(solution)/shard_map/all_gather | solution.py:216
  44.3 503.0 %reduce-scatter.17.cloned.1.call-start = ((), (), s32[]{:S(2)}) async-start(), calls=%async_computation.13 | async-start | bytes 1327104 | tf_op jit(solution)/shard_map/reduce_scatter | solution.py:314
  179.7 144.6 %copy-start.52 = (f32[1024]{0:T(1024)}, f32[1024]{0:T(1024)S(1)}, u32[]{:S(2)}) copy-start(f32[1024]{0:T(1024)S(1)} %broadcast_multiply_fusion) | copy-start | bytes 12292
  181.7 142.6 %copy-start.62 = (f32[1024]{0:T(1024)}, f32[1024]{0:T(1024)S(1)}, u32[]{:S(2)}) copy-start(f32[1024]{0:T(1024)S(1)} %fusion.80) | copy-start | bytes 12292
  330.6 272.4 %reduce-scatter.15.cloned.1.call-start = ((), (), s32[]{:S(2)}) async-start(), calls=%async_computation.12 | async-start | bytes 3981312 | tf_op jit(solution)/shard_map/reduce_scatter | solution.py:311
  524.4 178.0 %reduce-scatter.19.cloned.1.call-start = ((), (), s32[]{:S(2)}) async-start(), calls=%async_computation.14 | async-start | bytes 5308416 | tf_op jit(solution)/shard_map/reduce_scatter | solution.py:317
  536.1 265.1 %reduce-scatter.23.cloned.1.call-start = ((), (), s32[]{:S(2)}) async-start(), calls=%async_computation.16 | async-start | bytes 5308416 | tf_op jit(solution)/shard_map/reduce_scatter | solution.py:320
  547.3 277.3 %reduce-scatter.27.cloned.1.call-start = ((), (), s32[]{:S(2)}) async-start(), calls=%async_computation.22 | async-start | bytes 245760
  549.1 300.6 %reduce-scatter.25.cloned.1.call-start = ((), (), s32[]{:S(2)}) async-start(), calls=%async_computation.21 | async-start | bytes 737280
  605.1 269.2 %reduce-scatter.21.cloned.1.call-start = ((), (), s32[]{:S(2)}) async-start(), calls=%async_computation.15 | async-start | bytes 737280 | tf_op jit(solution)/shard_map/reduce_scatter | solution.py:334
  702.4 196.9 %reduce-scatter.29.cloned.1.call-start = ((), (), s32[]{:S(2)}) async-start(), calls=%async_computation.23 | async-start | bytes 737280
  803.4 136.5 %all-gather.22.cloned.1.call-start = ((), (), s32[]{:S(2)}) async-start(), calls=%async_computation.18 | async-start | bytes 1327104 | tf_op jit(solution)/shard_map/all_gather | solution.py:391
  831.8 175.6 %all-gather.20.cloned.1.call-start = ((), (), s32[]{:S(2)}) async-start(), calls=%async_computation.17 | async-start | bytes 3981312 | tf_op jit(solution)/shard_map/all_gather | solution.py:388
  860.2 227.4 %all-gather.24.cloned.1.call-start = ((), (), s32[]{:S(2)}) async-start(), calls=%async_computation.19 | async-start | bytes 5308416 | tf_op jit(solution)/shard_map/all_gather | solution.py:394
  883.0 285.7 %all-gather.26.cloned.1.call-start = ((), (), s32[]{:S(2)}) async-start(), calls=%async_computation.20 | async-start | bytes 5308416 | tf_op jit(solution)/shard_map/all_gather | solution.py:397
  908.0 578.1 %all-reduce.6.cloned.1.call-start = ((), (), s32[]{:S(2)}) async-start(), calls=%async_computation.24 | async-start | bytes 28311552 | tf_op jit(solution)/shard_map/psum | solution.py:24
  1245.1 105.3 %copy-start.41 = (bf16[192,384]{1,0:T(8,128)(2,1)S(1)}, bf16[192,384]{1,0:T(8,128)(2,1)}, u32[]{:S(2)}) copy-start(bf16[192,384]{1,0:T(8,128)(2,1)} %reduce-scatter.29.cloned.1.call-done) | copy-start | bytes 442372
  1245.1 106.3 %copy-start.40 = (bf16[96,768]{1,0:T(8,128)(2,1)S(1)}, bf16[96,768]{1,0:T(8,128)(2,1)}, u32[]{:S(2)}) copy-start(bf16[96,768]{1,0:T(8,128)(2,1)} %reduce-scatter.21.cloned.1.call-done) | copy-start | bytes 442372
  1245.1 241.1 %copy-start.39 = (f32[96,192]{0,1:T(8,128)S(1)}, f32[96,192]{0,1:T(8,128)}, u32[]{:S(2)}) copy-start(f32[96,192]{0,1:T(8,128)} %copy-done.38) | copy-start | bytes 221188
  1245.1 244.9 %copy-start.33 = (f32[96,576]{0,1:T(8,128)S(1)}, f32[96,576]{0,1:T(8,128)}, u32[]{:S(2)}) copy-start(f32[96,576]{0,1:T(8,128)} %copy.168) | copy-start | bytes 663556
  1346.9 144.3 %copy-start.42 = (f32[8,1,1152]{2,1,0:T(1,128)}, f32[8,1,1152]{2,1,0:T(1,128)S(1)}, u32[]{:S(2)}) copy-start(f32[8,1,1152]{2,1,0:T(1,128)S(1)} %convert_element_type.299) | copy-start | bytes 110596
  (74 other events, 1056.3 us)
Sparse Core Ops, SparseCore 0:
  21.4 62.8 all-gather.11
  87.1 38.5 all-gather.13
  127.8 79.3 all-gather.15
  209.1 79.1 all-gather.17
  330.8 61.4 reduce-scatter.16
  524.5 78.4 reduce-scatter.14
  606.6 95.7 reduce-scatter.18
  706.0 95.1 reduce-scatter.22
  804.2 20.2 reduce-scatter.26
  827.5 22.1 reduce-scatter.24
  852.2 22.0 reduce-scatter.20
  877.2 22.0 reduce-scatter.28
  902.1 37.6 all-gather.21
  942.5 64.9 all-gather.19
  1009.5 78.0 all-gather.23
  1089.5 79.1 all-gather.25
  1192.1 294.0 all-reduce.5
where the time goes:
time: 1520 us; the launch traced here: 1500 us
  waiting for transfers between devices  792 us (52%)
  matrix products  289 us (19%)
  blocking collectives  161 us (11%)
  other arithmetic  132 us (9%)
  local copies, waits for them, and re-layouts  92.9 us (6%)
  between operations  26.8 us (2%)
    psum x1, waiting for transfers between devices, broadcast(): return lax.psum(kept, axis)  134 us
    reduce_scatter x1, waiting for transfers between devices, local(): lax.psum_scatter(grad_down.astype(jnp.bfloat16), 'dp', scatter_dimension=...  98.8 us
    reduce_scatter x1, waiting for transfers between devices, local(): lax.psum_scatter(grad_up.astype(jnp.bfloat16), 'dp', scatter_dimension=0,...  97.2 us
    unnamed x3, blocking collectives  75.4 us
    all_gather x1, waiting for transfers between devices, local(): lax.all_gather(band_up.astype(jnp.bfloat16), 'dp', axis=0, tiled=True)  74.7 us
    all_gather x1, waiting for transfers between devices, local(): lax.all_gather(band_down.astype(jnp.bfloat16), 'dp', axis=0, tiled=True)  73.8 us
    all_gather x1, waiting for transfers between devices, local(): lax.all_gather(band_qkv.astype(jnp.bfloat16), 'dp', axis=0, tiled=True)  66.2 us
    dot_general x4, matrix products, row_dot(): return jnp.dot(left, right, preferred_element_type=jnp.float32)  57.8 us
  transfers between devices with their start and end apart: 17, of which 15 were waited for; matrix products, arithmetic and copies ran while one was open for 28% of the time, Pallas kernels for 0%

commit v1 on v0

--- a/solution.py
+++ b/solution.py
@@ -3,7 +3,338 @@
 import jax
 import jax.numpy as jnp
 from jax import lax
+from jax.experimental import pallas as pl
+from jax.experimental.pallas import tpu as pltpu
 from jax.sharding import PartitionSpec as P
+
+MESH = pl.DeviceIdType.MESH
+ANY = pl.BlockSpec(memory_space=pl.ANY)
+VM = pl.BlockSpec(memory_space=pltpu.VMEM)
+
+
+class Grid:
+    def __init__(self, n_dp, n_fsdp):
+        self.Z = 4
+        self.X = n_dp // 4
+        self.Y = n_fsdp // 2
+        self.swap = self.X == self.Y
+        self.A, self.B = self.X, self.Y
+
+    def here(self):
+        dp, fs = lax.axis_index("dp"), lax.axis_index("fsdp")
+        self.z, self.x = dp // self.X, dp % self.X
+        self.y, self.c = fs // 2, fs % 2
+        if self.swap:
+            self.a = self.x + self.c * (self.y - self.x)
+            self.b = self.y + self.c * (self.x - self.y)
+        else:
+            self.a, self.b = self.x, self.y
+        return self
+
+    def xy(self, a, b, c):
+        if self.swap:
+            return a + c * (b - a), b + c * (a - b)
+        return a, b
+
+    def device(self, z, a, b, c, frame=None):
+        x, y = self.xy(a, b, self.c if frame is None else frame)
+        return {"dp": z * self.X + x, "fsdp": y * 2 + c}
+
+    def shape(self, order, r, w):
+        if order == "j":
+            return (self.Y, 2, self.Z, self.X, r, w)
+        return (self.Z, self.X, self.Y, 2, r, w)
+
+    def at(self, ref, order, y, c, z, x):
+        return ref.at[y, c, z, x] if order == "j" else ref.at[z, x, y, c]
+
+    def peers(self):
+        out = [self.device((self.z + k) % self.Z, self.a, self.b, self.c) for k in range(1, self.Z)]
+        out += [self.device(self.z, (self.a + k) % self.A, self.b, self.c) for k in range(1, self.A)]
+        out += [self.device(self.z, self.a, (self.b + k) % self.B, self.c) for k in range(1, self.B)]
+        out += [{"dp": self.z * self.X + self.x, "fsdp": self.y * 2 + 1 - self.c}]
+        return out
+
+    def barrier(self):
+        sem = pltpu.get_barrier_semaphore()
+        peers = self.peers()
+        for peer in peers:
+            pl.semaphore_signal(sem, inc=1, device_id=peer, device_id_type=MESH)
+        pl.semaphore_wait(sem, len(peers))
+
+
+class Gather:
+    def __init__(self, grid, order, src, out, local, send, recv):
+        g = self.g = grid
+        self.order, self.src, self.out = order, src, out
+        self.local, self.send, self.recv = local, send, recv
+        self.copies = {}
+
+    @staticmethod
+    def slots(g):
+        return (g.Z - 1) + 2 * (g.A - 1) + 2 * (g.B - 1) * g.A + 1
+
+    def _copy(self, stage, slot, src, dst, device):
+        cp = pltpu.make_async_remote_copy(
+            src_ref=src, dst_ref=dst, send_sem=self.send.at[slot], recv_sem=self.recv.at[slot],
+            device_id=device, device_id_type=MESH)
+        cp.start()
+        self.copies.setdefault(stage, []).append(cp)
+
+    def _piece(self, a, b, c, z=slice(None)):
+        x, y = self.g.xy(a, b, self.g.c)
+        return self.g.at(self.out, self.order, y, c, z, x)
+
+    def start(self):
+        g = self.g
+        self.own = pltpu.make_async_copy(self.src, self._piece(g.a, g.b, g.c, g.z), self.local)
+        self.own.start()
+        for k in range(1, g.Z):
+            self._copy("z", k - 1, self.src, self._piece(g.a, g.b, g.c, g.z),
+                       g.device((g.z + k) % g.Z, g.a, g.b, g.c))
+
+    def _sibling(self, stage, slot, a, b):
+        g = self.g
+        ref = self._piece(a, b, g.c)
+        self._copy(stage, slot, ref, ref, {"dp": g.z * g.X + g.x, "fsdp": g.y * 2 + 1 - g.c})
+
+    def after_z(self):
+        g = self.g
+        self.own.wait()
+        for cp in self.copies["z"]:
+            cp.wait_recv()
+        base = g.Z - 1
+        ref = self._piece(g.a, g.b, g.c)
+        for k in range(1, g.A):
+            self._copy("a", base + k - 1, ref, ref, g.device(g.z, (g.a + k) % g.A, g.b, g.c))
+        self._sibling("d", base + g.A - 1, g.a, g.b)
+
+    def after_a(self):
+        g = self.g
+        for cp in self.copies["a"]:
+            cp.wait_recv()
+        base = g.Z - 1 + g.A
+        for a in range(g.A):
+            ref = self._piece(a, g.b, g.c)
+            for k in range(1, g.B):
+                self._copy("b", base + a * (g.B - 1) + k - 1, ref, ref,
+                           g.device(g.z, a * 0 + g.a, (g.b + k) % g.B, g.c))
+        base += g.A * (g.B - 1)
+        for k in range(1, g.A):
+            self._sibling("d", base + k - 1, (g.a - k + g.A) % g.A, g.b)
+
+    def after_b(self):
+        g = self.g
+        for cp in self.copies["b"]:
+            cp.wait_recv()
+        base = g.Z - 1 + g.A + g.A * (g.B - 1) + g.A - 1
+        for a in range(g.A):
+            for k in range(1, g.B):
+                self._sibling("d", base + a * (g.B - 1) + k - 1, a, (g.b - k + g.B) % g.B)
+
+    def arrive(self):
+        for cp in self.copies["d"]:
+            cp.wait_recv()
+
+    def finish(self):
+        for group in self.copies.values():
+            for cp in group:
+                cp.wait_send()
+
+
+class Scatter:
+    def __init__(self, grid, order, src, work, recv_b, recv_a, recv_z, mine, local, send, recv):
+        self.g, self.order, self.src = grid, order, src
+        self.work, self.recv_b, self.recv_a, self.recv_z, self.mine = work, recv_b, recv_a, recv_z, mine
+        self.local, self.send, self.recv = local, send, recv
+        self.copies = {}
+
+    @staticmethod
+    def slots(g):
+        return g.A * g.B + (g.B - 1) + (g.A - 1) + (g.Z - 1)
+
+    @staticmethod
+    def scratch(g, r, w, staged=True):
+        return [
+            pltpu.VMEM((g.B, g.Z, g.A, r, w), jnp.bfloat16),
+            pltpu.VMEM((max(g.B - 1, 1), g.Z, g.A, r, w), jnp.bfloat16),
+            pltpu.VMEM((max(g.A - 1, 1), g.Z, r, w), jnp.bfloat16),
+            pltpu.VMEM((g.Z - 1, r, w), jnp.bfloat16),
+            pltpu.VMEM((g.B, g.Z, g.A, r, w), jnp.bfloat16),
+        ]
+
+    def _copy(self, stage, slot, src, dst, device):
+        cp = pltpu.make_async_remote_copy(
+            src_ref=src, dst_ref=dst, send_sem=self.send.at[slot], recv_sem=self.recv.at[slot],
+            device_id=device, device_id_type=MESH)
+        cp.start()
+        self.copies.setdefault(stage, []).append(cp)
+
+    def start(self):
+        g = self.g
+        other = 1 - g.c
+        self.owns = []
+        for b in range(g.B):
+            for a in range(g.A):
+                x, y = g.xy(a, b, other)
+                self._copy("d", b * g.A + a, g.at(self.src, self.order, y, other, slice(None), x),
+                           self.work.at[b, :, a], {"dp": g.z * g.X + g.x, "fsdp": g.y * 2 + other})
+        for b in range(g.B):
+            for a in range(g.A):
+                x, y = g.xy(a, b, g.c)
+                cp = pltpu.make_async_copy(g.at(self.src, self.order, y, g.c, slice(None), x),
+                                           self.mine.at[b, :, a], self.local.at[b * g.A + a])
+                cp.start()
+                self.owns.append(cp)
+
+    def after_d(self):
+        g = self.g
+        for cp in self.owns:
+            cp.wait()
+        for cp in self.copies["d"]:
+            cp.wait_recv()
+
+        def add(n, carry):
+            b, z, a = n // (g.Z * g.A), n // g.A % g.Z, n % g.A
+            self.work[b, z, a] = (self.work[b, z, a].astype(jnp.float32)
+                                  + self.mine[b, z, a].astype(jnp.float32)).astype(jnp.bfloat16)
+            return carry
+
+        lax.fori_loop(0, g.B * g.Z * g.A, add, 0)
+        base = g.A * g.B
+        for k in range(1, g.B):
+            b = (g.b + k) % g.B
+            self._copy("b", base + k - 1, self.work.at[b], self.recv_b.at[k - 1], g.device(g.z, g.a, b, g.c))
+
+    def after_b(self):
+        g = self.g
+        for cp in self.copies.get("b", []):
+            cp.wait_recv()
+
+        def add(n, carry):
+            z, a = n // g.A, n % g.A
+            total = self.work[g.b, z, a].astype(jnp.float32)
+            for k in range(1, g.B):
+                total = total + self.recv_b[k - 1, z, a].astype(jnp.float32)
+            self.work[g.b, z, a] = total.astype(jnp.bfloat16)
+            return carry
+
+        lax.fori_loop(0, g.Z * g.A, add, 0)
+        base = g.A * g.B + g.B - 1
+        for k in range(1, g.A):
+            a = (g.a + k) % g.A
+            self._copy("a", base + k - 1, self.work.at[g.b, :, a], self.recv_a.at[k - 1],
+                       g.device(g.z, a, g.b, g.c))
+
+    def after_a(self):
+        g = self.g
+        for cp in self.copies.get("a", []):
+            cp.wait_recv()
+
+        def add(z, carry):
+            total = self.work[g.b, z, g.a].astype(jnp.float32)
+            for k in range(1, g.A):
+                total = total + self.recv_a[k - 1, z].astype(jnp.float32)
+            self.work[g.b, z, g.a] = total.astype(jnp.bfloat16)
+            return carry
+
+        lax.fori_loop(0, g.Z, add, 0)
+        base = g.A * g.B + g.B - 1 + g.A - 1
+        for k in range(1, g.Z):
+            z = (g.z + k) % g.Z
+            self._copy("z", base + k - 1, self.work.at[g.b, z, g.a], self.recv_z.at[k - 1],
+                       g.device(z, g.a, g.b, g.c))
+
+    def total(self):
+        g = self.g
+        for cp in self.copies["z"]:
+            cp.wait_recv()
+        total = self.work[g.b, g.z, g.a].astype(jnp.float32)
+        for k in range(1, g.Z):
+            total = total + self.recv_z[k - 1].astype(jnp.float32)
+        return total
+
+    def finish(self):
+        for group in self.copies.values():
+            for cp in group:
+                cp.wait_send()
+
+
+def gather_all(n_dp, n_fsdp, shards, orders, collective_id):
+    grid = Grid(n_dp, n_fsdp)
+    count = len(shards)
+    slots = Gather.slots(grid)
+
+    def kernel(*refs):
+        ins, outs, (local, send, recv) = refs[:count], refs[count : 2 * count], refs[2 * count :]
+        g = grid.here()
+        g.barrier()
+        jobs = [Gather(g, orders[n], ins[n], outs[n], local.at[n], send.at[n], recv.at[n]) for n in range(count)]
+        for job in jobs:
+            job.start()
+        stages = ["after_z", "after_a", "after_b", "arrive"]
+        for step in range(count + len(stages) - 1):
+            for s in reversed(range(len(stages))):
+                if 0 <= step - s < count:
+                    getattr(jobs[step - s], stages[s])()
+        for job in jobs:
+            job.finish()
+
+    return pl.pallas_call(
+        kernel,
+        out_shape=[jax.ShapeDtypeStruct(grid.shape(o, *s.shape), s.dtype) for s, o in zip(shards, orders)],
+        in_specs=[ANY] * count,
+        out_specs=[ANY] * count,
+        scratch_shapes=[pltpu.SemaphoreType.DMA((count,)), pltpu.SemaphoreType.DMA((count, slots)),
+                        pltpu.SemaphoreType.DMA((count, slots))],
+        compiler_params=pltpu.CompilerParams(collective_id=collective_id, has_side_effects=True),
+        name="gather_all",
+    )(*shards)
+
+
+def scatter_all(n_dp, n_fsdp, wholes, orders, collective_id):
+    grid = Grid(n_dp, n_fsdp)
+    count = len(wholes)
+    slots = Scatter.slots(grid)
+    sizes = [w.shape[-2:] for w in wholes]
+
+    def kernel(*refs):
+        ins, outs = refs[:count], refs[count : 2 * count]
+        bufs, (local, send, recv) = refs[2 * count : 2 * count + 5 * count], refs[7 * count :]
+        g = grid.here()
+        g.barrier()
+        jobs = [Scatter(g, orders[n], ins[n], *bufs[5 * n : 5 * n + 5], local.at[n], send.at[n], recv.at[n])
+                for n in range(count)]
+        for job in jobs:
+            job.start()
+
+        stages = ["after_d", "after_b", "after_a", "total"]
+        for step in range(count + len(stages) - 1):
+            for s in reversed(range(len(stages))):
+                n = step - s
+                if 0 <= n < count:
+                    if stages[s] == "total":
+                        outs[n][...] = jobs[n].total()
+                    else:
+                        getattr(jobs[n], stages[s])()
+        for job in jobs:
+            job.finish()
+
+    scratch = []
+    for r, w in sizes:
+        scratch += Scatter.scratch(grid, r, w)
+    return pl.pallas_call(
+        kernel,
+        out_shape=[jax.ShapeDtypeStruct(s, jnp.float32) for s in sizes],
+        in_specs=[ANY] * count,
+        out_specs=[VM] * count,
+        scratch_shapes=scratch + [pltpu.SemaphoreType.DMA((count, grid.A * grid.B)),
+                                  pltpu.SemaphoreType.DMA((count, slots)), pltpu.SemaphoreType.DMA((count, slots))],
+        compiler_params=pltpu.CompilerParams(collective_id=collective_id, has_side_effects=True,
+                                             vmem_limit_bytes=60 * 1024 * 1024),
+        name="scatter_all",
+    )(*wholes)
+
 
 D = 768
 HEADS = 12
@@ -155,36 +486,28 @@
     return pickers
 
 
-def fetch_update(update, root):
-    return broadcast(update.astype(jnp.bfloat16), ("dp", "fsdp"), root).astype(update.dtype)
-
-
-def band_tile(band, like, column_index):
-    columns_here = like.shape[1]
-    return lax.dynamic_slice_in_dim(band, column_index * columns_here, columns_here, 1)
-
-
-def row_band(pieces, like, row_index):
-    rows_here = like.shape[0]
-    start = row_index * rows_here
-    return jnp.concatenate(
-        [lax.dynamic_slice_in_dim(piece, start, rows_here, 0) for piece in pieces], axis=1
-    )
-
-
-def stacked_band(pieces, like, row_index):
-    rows_here = like.shape[0]
-    start = row_index * rows_here
-    owner_block = start // D
-    picked = jnp.zeros((rows_here, D), jnp.float32)
-    for number in range(len(pieces)):
-        inside = jnp.clip(start - number * D, 0, D - rows_here)
-        piece = lax.dynamic_slice_in_dim(pieces[number], inside, rows_here, 0)
-        picked = jnp.where(owner_block == number, piece, picked)
-    return picked
+def wholes_of(pieces, orders):
+    out = []
+    for piece, order in zip(pieces, orders):
+        rows, columns = piece.shape[-2:]
+        if order == "j":
+            folded = piece.reshape(piece.shape[0] * piece.shape[1], -1, columns)
+        else:
+            folded = piece.reshape(piece.shape[0] * piece.shape[1], -1, columns)
+        out.append(folded.transpose(1, 0, 2).reshape(folded.shape[1], -1))
+    return out
+
+
+def pieces_of(whole, order, n_dp, n_fsdp):
+    grid = Grid(n_dp, n_fsdp)
+    n_rows, n_columns = (n_dp, n_fsdp) if order == "j" else (n_fsdp, n_dp)
+    rows, columns = whole.shape[0] // n_rows, whole.shape[1] // n_columns
+    folded = whole.reshape(whole.shape[0], n_columns, columns).transpose(1, 0, 2)
+    return folded.reshape(grid.shape(order, rows, columns))
 
 
 def local(
+    sizes,
     tokens,
     counts,
     cotangent,
@@ -203,18 +526,10 @@
     out_low = out_weight.astype(jnp.bfloat16)
     up_low = up_weight.astype(jnp.bfloat16)
     down_low = down_weight.astype(jnp.bfloat16)
-    qkv_cols, out_cols, up_cols, down_cols = (
-        lax.all_gather(qkv_low, "fsdp", axis=1, tiled=True),
-        lax.all_gather(out_low, "fsdp", axis=1, tiled=True),
-        lax.all_gather(up_low, "fsdp", axis=1, tiled=True),
-        lax.all_gather(down_low, "fsdp", axis=1, tiled=True),
-    )
-    qkv_full, out_full, up_full, down_full = (
-        lax.all_gather(qkv_cols, "dp", axis=0, tiled=True),
-        lax.all_gather(out_cols, "dp", axis=0, tiled=True),
-        lax.all_gather(up_cols, "dp", axis=0, tiled=True),
-        lax.all_gather(down_cols, "dp", axis=0, tiled=True),
-    )
+    n_dp, n_fsdp = sizes
+    orders = ("j", "j", "j", "i")
+    gathered = gather_all(n_dp, n_fsdp, (qkv_low, out_low, up_low, down_low.T), orders, 1)
+    qkv_full, out_full, up_full, down_full_t = wholes_of(gathered, orders)
     (
         gain_one,
         shift_one,
@@ -250,34 +565,22 @@
     normed_two = layer_norm(middle, gain_two, shift_two).astype(jnp.bfloat16)
     hidden = row_dot(normed_two, up_full) + bias_up
     active = jax.nn.gelu(hidden, approximate=False).astype(jnp.bfloat16)
-    layer_rows = (middle + row_dot(active, down_full) + bias_down).astype(jnp.bfloat16)
-    qkv_part, out_part, up_part, down_part = (
-        lax.all_gather(qkv_low, "fsdp", axis=1, tiled=True),
-        lax.all_gather(out_low, "fsdp", axis=1, tiled=True),
-        lax.all_gather(up_low, "fsdp", axis=1, tiled=True),
-        lax.all_gather(down_low, "fsdp", axis=1, tiled=True),
-    )
-    qkv_back, out_back, up_back, down_back = (
-        lax.all_gather(qkv_part, "dp", axis=0, tiled=True),
-        lax.all_gather(out_part, "dp", axis=0, tiled=True),
-        lax.all_gather(up_part, "dp", axis=0, tiled=True),
-        lax.all_gather(down_part, "dp", axis=0, tiled=True),
-    )
-    grad_down = column_dot(active, cotangent)
+    layer_rows = (middle + transposed_dot(active, down_full_t) + bias_down).astype(jnp.bfloat16)
+    grad_down_t = column_dot(cotangent, active)
     grad_bias_down = jnp.sum(cotangent.astype(jnp.float32), axis=0)
-    active_grad = transposed_dot(cotangent, down_back)
+    active_grad = row_dot(cotangent, down_full_t)
     unused_value, gelu_pull = jax.vjp(partial(jax.nn.gelu, approximate=False), hidden)
     hidden_grad = gelu_pull(active_grad)[0].astype(jnp.bfloat16)
     grad_up = column_dot(normed_two, hidden_grad)
     grad_bias_up = jnp.sum(hidden_grad.astype(jnp.float32), axis=0)
-    normed_two_grad = transposed_dot(hidden_grad, up_back)
+    normed_two_grad = transposed_dot(hidden_grad, up_full)
     unused_norm, norm_two_pull = jax.vjp(layer_norm, middle, gain_two, shift_two)
     middle_grad, grad_gain_two, grad_shift_two = norm_two_pull(normed_two_grad)
     middle_grad = middle_grad + cotangent.astype(jnp.float32)
     branch_grad = middle_grad.astype(jnp.bfloat16)
     grad_out = column_dot(attended, branch_grad)
     grad_bias_out = jnp.sum(branch_grad.astype(jnp.float32), axis=0)
-    attended_grad = transposed_dot(branch_grad, out_back).astype(jnp.bfloat16)
+    attended_grad = transposed_dot(branch_grad, out_full).astype(jnp.bfloat16)
     query_grad, key_grad, value_grad = lax.map(
         clip_backward,
         (queries, key_rows, value_rows, counts, log_totals, heads_view(attended_grad)),
@@ -290,7 +593,7 @@
     grad_qkv = column_dot(normed, projected_grad)
     grad_bias_query = jnp.sum(projected_grad[:, :D].astype(jnp.float32), axis=0)
     grad_bias_value = jnp.sum(projected_grad[:, 2 * D :].astype(jnp.float32), axis=0)
-    normed_grad = transposed_dot(projected_grad, qkv_back)
+    normed_grad = transposed_dot(projected_grad, qkv_full)
     unused_first, norm_one_pull = jax.vjp(layer_norm, inputs, gain_one, shift_one)
     input_rows_grad, grad_gain_one, grad_shift_one = norm_one_pull(normed_grad)
     input_grad = (middle_grad + input_rows_grad).astype(jnp.bfloat16)
@@ -307,57 +610,16 @@
             grad_bias_up,
         ]
     )
-    row_qkv, row_out, row_up, row_down, row_small = (
-        lax.psum_scatter(
-            grad_qkv.astype(jnp.bfloat16), "dp", scatter_dimension=0, tiled=True
-        ).astype(jnp.float32),
-        lax.psum_scatter(
-            grad_out.astype(jnp.bfloat16), "dp", scatter_dimension=0, tiled=True
-        ).astype(jnp.float32),
-        lax.psum_scatter(
-            grad_up.astype(jnp.bfloat16), "dp", scatter_dimension=0, tiled=True
-        ).astype(jnp.float32),
-        lax.psum_scatter(
-            grad_down.astype(jnp.bfloat16), "dp", scatter_dimension=0, tiled=True
-        ).astype(jnp.float32),
-        lax.psum_scatter(
-            small_grad.astype(jnp.bfloat16), "dp", scatter_dimension=0, tiled=True
-        ).astype(jnp.float32),
-    )
-    shard_qkv, shard_out, shard_up, shard_down, shard_small = (
-        lax.psum_scatter(
-            row_qkv.astype(jnp.bfloat16), "fsdp", scatter_dimension=1, tiled=True
-        ).astype(jnp.float32),
-        lax.psum_scatter(
-            row_out.astype(jnp.bfloat16), "fsdp", scatter_dimension=1, tiled=True
-        ).astype(jnp.float32),
-        lax.psum_scatter(
-            row_up.astype(jnp.bfloat16), "fsdp", scatter_dimension=1, tiled=True
-        ).astype(jnp.float32),
-        lax.psum_scatter(
-            row_down.astype(jnp.bfloat16), "fsdp", scatter_dimension=1, tiled=True
-        ).astype(jnp.float32),
-        lax.psum_scatter(
-            row_small.astype(jnp.bfloat16), "fsdp", scatter_dimension=0, tiled=True
-        ).astype(jnp.float32),
-    )
-    band_qkv, band_out, band_up, band_down, band_small = (
-        lax.all_gather(shard_qkv.astype(jnp.bfloat16), "fsdp", axis=1, tiled=True).astype(
-            shard_qkv.dtype
-        ),
-        lax.all_gather(shard_out.astype(jnp.bfloat16), "fsdp", axis=1, tiled=True).astype(
-            shard_out.dtype
-        ),
-        lax.all_gather(shard_up.astype(jnp.bfloat16), "fsdp", axis=1, tiled=True).astype(
-            shard_up.dtype
-        ),
-        lax.all_gather(shard_down.astype(jnp.bfloat16), "fsdp", axis=1, tiled=True).astype(
-            shard_down.dtype
-        ),
-        lax.all_gather(shard_small.astype(jnp.bfloat16), "fsdp", axis=0, tiled=True).astype(
-            shard_small.dtype
-        ),
-    )
+    whole_small = lax.psum(small_grad, ("dp", "fsdp"))
+    split = [
+        pieces_of(grad.astype(jnp.bfloat16), order, n_dp, n_fsdp)
+        for grad, order in zip((grad_qkv, grad_out, grad_up, grad_down_t), orders)
+    ]
+    shards = scatter_all(n_dp, n_fsdp, split, orders, 2)
+    shard_qkv, shard_out, shard_up, shard_down_t = shards
+    gradients = gather_all(n_dp, n_fsdp, [s.astype(jnp.bfloat16) for s in shards], orders, 3)
+    whole_qkv, whole_out, whole_up, whole_down_t = wholes_of(gradients, orders)
+    shard_down = shard_down_t.T
     rank = lax.axis_index(("dp", "fsdp"))
     row_index = lax.axis_index("dp")
     column_index = lax.axis_index("fsdp")
@@ -367,53 +629,36 @@
     owning = jnp.any(matches)
 
     def update_slot(gradient):
-        left_stat = decay_rate * statistics[0, 0] + (1.0 - decay_rate) * jnp.dot(
-            gradient, gradient.T, precision=highest, preferred_element_type=jnp.float32
-        )
-        right_stat = decay_rate * statistics[0, 1] + (1.0 - decay_rate) * jnp.dot(
-            gradient.T, gradient, precision=highest, preferred_element_type=jnp.float32
-        )
+        left_stat = decay_rate * statistics[0, 0] + (1.0 - decay_rate) * transposed_dot(gradient, gradient)
+        right_stat = decay_rate * statistics[0, 1] + (1.0 - decay_rate) * column_dot(gradient, gradient)
+        wide = gradient.astype(jnp.float32)
         left_step = jnp.dot(
-            inverse_roots[0, 0], gradient, precision=highest, preferred_element_type=jnp.float32
+            inverse_roots[0, 0], wide, precision=highest, preferred_element_type=jnp.float32
         )
         update = jnp.dot(
             left_step, inverse_roots[0, 1], precision=highest, preferred_element_type=jnp.float32
         )
-        return (jnp.stack([left_stat, right_stat])[None], update)
+        return (jnp.stack([left_stat, right_stat])[None], update.astype(jnp.bfloat16))
 
     def keep_slot(gradient):
-        return (statistics, jnp.zeros((D, D), jnp.float32))
-
-    whole_qkv, whole_out, whole_up, whole_down, whole_small = (
-        lax.all_gather(band_qkv.astype(jnp.bfloat16), "dp", axis=0, tiled=True).astype(
-            band_qkv.dtype
-        ),
-        lax.all_gather(band_out.astype(jnp.bfloat16), "dp", axis=0, tiled=True).astype(
-            band_out.dtype
-        ),
-        lax.all_gather(band_up.astype(jnp.bfloat16), "dp", axis=0, tiled=True).astype(
-            band_up.dtype
-        ),
-        lax.all_gather(band_down.astype(jnp.bfloat16), "dp", axis=0, tiled=True).astype(
-            band_down.dtype
-        ),
-        lax.all_gather(band_small.astype(jnp.bfloat16), "dp", axis=0, tiled=True).astype(
-            band_small.dtype
-        ),
-    )
+        return (statistics, jnp.zeros((D, D), jnp.bfloat16))
+
+    whole_down = whole_down_t.T
     gradient = lax.switch(mine, block_pickers(), (whole_qkv, whole_out, whole_up, whole_down))
     new_statistics, update = lax.cond(owning, update_slot, keep_slot, gradient)
-    arrivals = []
-    for number in range(BLOCKS):
-        arrivals.append(fetch_update(update, owners[number]))
-    tile_qkv = band_tile(row_band(arrivals[0:3], qkv_weight, row_index), qkv_weight, column_index)
-    tile_out = band_tile(row_band(arrivals[3:4], out_weight, row_index), out_weight, column_index)
-    tile_up = band_tile(
-        row_band(arrivals[4 : 4 + FF // D], up_weight, row_index), up_weight, column_index
-    )
-    tile_down = band_tile(
-        stacked_band(arrivals[4 + FF // D :], down_weight, row_index), down_weight, column_index
-    )
+    zero = jnp.zeros((D, D), jnp.bfloat16)
+    steps = [jnp.where(owners[number] == rank, update, zero) for number in range(BLOCKS)]
+    update_t = update.T
+    turned = [jnp.where(owners[number] == rank, update_t, zero) for number in range(4 + FF // D, BLOCKS)]
+    masked = (
+        jnp.concatenate(steps[0:3], axis=1),
+        steps[3],
+        jnp.concatenate(steps[4 : 4 + FF // D], axis=1),
+        jnp.concatenate(turned, axis=1),
+    )
+    split = [pieces_of(whole, order, n_dp, n_fsdp) for whole, order in zip(masked, orders)]
+    tile_qkv, tile_out, tile_up, tile_down_t = scatter_all(n_dp, n_fsdp, split, orders, 4)
+    tile_down = tile_down_t.T
     new_qkv = qkv_weight - step_rate * tile_qkv
     new_out = out_weight - step_rate * tile_out
     new_up = up_weight - step_rate * tile_up
@@ -453,7 +698,7 @@
         P(),
     )
     return jax.shard_map(
-        local,
+        partial(local, (mesh.shape["dp"], mesh.shape["fsdp"])),
         mesh=mesh,
         in_specs=placed,
         out_specs=(

time: 1520 us -> 1010 us (0.66)
  waiting for transfers between devices: 792 us -> 0 us
  Pallas kernels: 0 us -> 386 us
  blocking collectives: 161 us -> 48.4 us
  local copies, waits for them, and re-layouts: 92.9 us -> 140 us
  between operations: 26.8 us -> 11.5 us
    pallas_call x0 -> x4, Pallas kernels: none -> 386 us  [the longest x2 193 us: scatter_all(): pl.pallas_call(kernel, out_shape=[jax.ShapeDtypeStruct(s, jnp.float32) fo...]
    all_gather x8 -> x0, waiting for transfers between devices: 338 us -> none  [the longest x1 74.7 us: local(): lax.all_gather(band_up.astype(jnp.bfloat16), 'dp', axis=0, tiled=True)]
    reduce_scatter x5 -> x0, waiting for transfers between devices: 264 us -> none  [the longest x1 98.8 us: local(): lax.psum_scatter(grad_down.astype(jnp.bfloat16), 'dp', scatter_dimension=...]
    psum x1 -> x0, waiting for transfers between devices: 134 us -> none  [broadcast(): return lax.psum(kept, axis)]
    all_gather x9 -> x0, blocking collectives: 85.1 us -> none  [the longest x1 24.6 us: local(): lax.all_gather(band_small.astype(jnp.bfloat16), 'dp', axis=0, tiled=True)]
    unnamed x3 -> x0, blocking collectives: 75.4 us -> none
    reshape x0 -> x13, local copies, waits for them, and re-layouts: none -> 61.3 us  [the longest x7 34.6 us: wholes_of(): folded = piece.reshape(piece.shape[0] * piece.shape[1], -1, columns)]
    unnamed x20 -> x0, waiting for transfers between devices: 55.5 us -> none
  transfers between devices with their start and end apart: 17 -> 0, of which waited for: 15 -> 0; matrix products, arithmetic and copies ran while one was open for 28% -> 0% of each run, Pallas kernels for 0% -> 0%
where the time goes in v1:
time: 1010 us; the launch traced here: 997 us
  Pallas kernels  386 us (38%)
  matrix products  290 us (29%)
  local copies, waits for them, and re-layouts  140 us (14%)
  other arithmetic  120 us (12%)
  blocking collectives  48.4 us (5%)
  between operations  11.5 us (1%)
    pallas_call x2, Pallas kernels, scatter_all(): pl.pallas_call(kernel, out_shape=[jax.ShapeDtypeStruct(s, jnp.float32) fo...  193 us
    pallas_call x2, Pallas kernels, gather_all(): pl.pallas_call(kernel, out_shape=[jax.ShapeDtypeStruct(grid.shape(o, *s.s...  192 us
    dot_general x4, matrix products, row_dot(): return jnp.dot(left, right, preferred_element_type=jnp.float32)  60.7 us
    psum x1, blocking collectives, local(): whole_small = lax.psum(small_grad, ('dp', 'fsdp'))  48.4 us
    convert_element_type x2, other arithmetic, one_block(): (softmax_weights * (weight_grad - inner_sum)).astype(jnp.bfloat16)  42.9 us
    dot_general x4, matrix products, one_block(): jnp.einsum('hdq,hdk->hqk', query_block, key_rows, preferred_element_type=...  40.6 us
    dot_general x2, matrix products, one_block(): jnp.einsum('hdq,hdk->hqk', grad_block, value_rows, preferred_element_type...  34.8 us
    reshape x7, local copies, waits for them, and re-layouts, wholes_of(): folded = piece.reshape(piece.shape[0] * piece.shape[1], -1, columns)  34.6 us

profile of v1, /device:TPU:27, one launch (start us, length us, event | category | flops | bytes accessed | tf_op | source)
XLA Modules:
  0.0 996.7 jit_solution(5538061761102631637)
XLA Ops:
  25.0 93.0 %gather_all.2 = (bf16[2,2,4,2,96,576]{5,4,3,2,1,0:T(8,128)(2,1)}, bf16[2,2,4,2,96,192]{5,4,3,2,1,0:T(8,128)(2,1)}, bf16[2,2,4,2,96,768]{5,4,3,2,1,0:T(8,128)(2,1)}, bf16[4,2,2,2,192,384]{5,4,3,2,1,0:T(8,128)(2,1)}) custom-call(bf16[96,576]{1,0:T(8,128)(2,1)} %convert_element_type.121.refs_0_, bf16[96,192]{1,0:T(8,128)(2,1)} %convert_element_type.122.refs_1_, ...), custom_call_target="tpu_custom_call" | custom-call | tf_op jit(solution)/shard_map/gather_all/pallas_call | solution.py:283
  155.4 69.5 %while.48 = (s32[]{:T(128)}, bf16[2,12,64,512]{3,2,1,0:T(8,128)(2,1)}, f32[2,12,512]{2,1,0:T(8,128)S(1)}, bf16[2,12,64,512]{3,2,1,0:T(8,128)(2,1)S(1)}, bf16[12,...) while((s32[]{:T(128)}, ...), condition=%wide.region_5.6_spmd.clone, body=%wide.region_2.5_spmd.clone.sunk | while | flops 1686498304 | bytes 99332296 | solution.py:415
  156.4 10.2 %fusion.149 = (f32[12,512]{1,0:T(8,128)S(1)}, f32[12,512,1024]{2,1,0:T(8,128)}) fusion(pred[1024]{0:T(1024)(128)(4,1)S(1)} %compare_reduce_fusion.5, bf16[12,64,1024]{2,1,0:T(8,128)(2,1)S(1)} %get-tuple-element.570, bf16[2,12,64,512]{3,2,1,0:T(8,128)(2,1)S(1)} %get-tuple-element.569, s32[]{:T(128)S(6)} %copy.115), kind=kOutput, calls=%fused_computation.19.clone.1 | convolution fusion | flops 824174592 | bytes 27550724 | tf_op jit(solution)/shard_map/while/body/eval_jaxpr/while/body/eval_jaxpr/hdq,hdk->hqk/dot_general | solution.py:402
  166.6 11.4 %fusion.150 = f32[12,512]{1,0:T(8,128)S(1)} fusion(f32[12,512,1024]{2,1,0:T(8,128)} %get-tuple-element.536, f32[12,512]{1,0:T(8,128)S(1)} %get-tuple-element.537, pred[1024]{0:T(1024)(128)(4,1)S(1)} %compare_reduce_fusion.5), kind=kLoop, calls=%fused_computation.20.clone.1 | loop fusion | flops 25159680 | bytes 25216000 | tf_op jit(solution)/shard_map/while/body/eval_jaxpr/while/body/eval_jaxpr/reduce_sum | solution.py:408
  178.0 11.2 %fusion.151 = bf16[2,12,64,512]{3,2,1,0:T(8,128)(2,1)S(1)} fusion(bf16[2,12,64,512]{3,2,1,0:T(8,128)(2,1)S(1)} %copy-done.30, s32[]{:T(128)S(6)} %copy.115, bf16[12,64,1024]{2,1,0:T(8,128)(2,1)S(1)} %copy-done.5, f32[12,512,1024]{2,1,0:T(8,128)} %get-tuple-element.536, f32[12,512]{1,0:T(8,128)S(1)} %fusion.150, ...), kind=kOutput, calls=%fused_computation.24.clone.1 | convolution fusion | flops 837156864 | bytes 27591684 | tf_op jit(solution)/shard_map/while/body/eval_jaxpr/while/body/eval_jaxpr/hqk,hdk->hdq/dot_general | solution.py:410
  191.0 10.2 %fusion.149 = (f32[12,512]{1,0:T(8,128)S(1)}, f32[12,512,1024]{2,1,0:T(8,128)}) fusion(pred[1024]{0:T(1024)(128)(4,1)S(1)} %compare_reduce_fusion.5, bf16[12,64,1024]{2,1,0:T(8,128)(2,1)S(1)} %get-tuple-element.570, bf16[2,12,64,512]{3,2,1,0:T(8,128)(2,1)S(1)} %get-tuple-element.569, s32[]{:T(128)S(6)} %copy.115), kind=kOutput, calls=%fused_computation.19.clone.1 | convolution fusion | flops 824174592 | bytes 27550724 | tf_op jit(solution)/shard_map/while/body/eval_jaxpr/while/body/eval_jaxpr/hdq,hdk->hqk/dot_general | solution.py:402
  201.2 11.4 %fusion.150 = f32[12,512]{1,0:T(8,128)S(1)} fusion(f32[12,512,1024]{2,1,0:T(8,128)} %get-tuple-element.536, f32[12,512]{1,0:T(8,128)S(1)} %get-tuple-element.537, pred[1024]{0:T(1024)(128)(4,1)S(1)} %compare_reduce_fusion.5), kind=kLoop, calls=%fused_computation.20.clone.1 | loop fusion | flops 25159680 | bytes 25216000 | tf_op jit(solution)/shard_map/while/body/eval_jaxpr/while/body/eval_jaxpr/reduce_sum | solution.py:408
  212.6 11.2 %fusion.151 = bf16[2,12,64,512]{3,2,1,0:T(8,128)(2,1)S(1)} fusion(bf16[2,12,64,512]{3,2,1,0:T(8,128)(2,1)S(1)} %copy-done.30, s32[]{:T(128)S(6)} %copy.115, bf16[12,64,1024]{2,1,0:T(8,128)(2,1)S(1)} %copy-done.5, f32[12,512,1024]{2,1,0:T(8,128)} %get-tuple-element.536, f32[12,512]{1,0:T(8,128)S(1)} %fusion.150, ...), kind=kOutput, calls=%fused_computation.24.clone.1 | convolution fusion | flops 837156864 | bytes 27591684 | tf_op jit(solution)/shard_map/while/body/eval_jaxpr/while/body/eval_jaxpr/hqk,hdk->hdq/dot_general | solution.py:410
  232.5 35.6 %multiply_convert_fusion.1 = (bf16[1024,3072]{1,0:T(8,128)(2,1)}, f32[1024,3072]{1,0:T(8,128)}, f32[1024,3072]{1,0:T(8,128)}) fusion(f32[3072]{0:T(1024)S(1)} %copy-done.70, bf16[768,3072]{0,1:T(8,128)(2,1)S(1)} %bitcast.341, f32[1024,768]{0,1:T(8,128)S(1)} %get-tuple-element.430, f32[768]{0:T(1024)S(1)} %copy-done.73, f32[768]{0:T(1024)S(1)} %copy-done.66, ...), kind=kOutput, calls=%fused_computation.72 | convolution fusion | flops 5043388416 | bytes 39348224 | tf_op jit(solution)/shard_map/dot_general | solution.py:370
  268.2 17.4 %convert_reduce_fusion = (f32[3072]{0:T(1024)}, bf16[1024,3072]{1,0:T(8,128)(2,1)}) fusion(f32[1024,3072]{1,0:T(8,128)} %get-tuple-element.388, bf16[768,3072]{0,1:T(8,128)(2,1)} %bitcast.343, bf16[1024,768]{1,0:T(8,128)(2,1)S(1)} %copy-done.27, f32[1024,3072]{1,0:T(8,128)} %get-tuple-element.431, f32[3072]{0:T(1024)S(1)} %copy-done.70), kind=kOutput, calls=%fused_computation.71 | convolution fusion | flops 4885312512 | bytes 37773312 | tf_op jit(solution)/shard_map/dot_general | solution.py:370
  355.3 163.7 %while.49 = (s32[]{:T(128)}, f32[12,64,1024]{2,1,0:T(8,128)}, f32[12,64,1024]{2,1,0:T(8,128)}, bf16[2,12,64,512]{3,2,1,0:T(8,128)(2,1)}, bf16[2,12,64,512]{3,2,1...) while((s32[]{:T(128)}, f32[12,64,1024]{2,1,0:T(8,128)}, ...), condition=%wide.region_12.13_spmd.clone, body=%wide.region_10.12_spmd.clone.sunk | while | flops 4125223936 | bytes 217239728 | solution.py:459
  356.4 10.1 %fusion.161 = f32[12,512,1024]{2,1,0:T(8,128)} fusion(bf16[12,64,1024]{2,1,0:T(8,128)(2,1)S(1)} %get-tuple-element.603, bf16[2,12,64,512]{3,2,1,0:T(8,128)(2,1)S(1)} %get-tuple-element.602, s32[]{:T(128)S(6)} %copy.125), kind=kOutput, calls=%fused_computation.46.clone.1 | convolution fusion | flops 805306368 | bytes 27525124 | tf_op jit(solution)/shard_map/while/body/eval_jaxpr/while/body/eval_jaxpr/hdq,hdk->hqk/dot_general | solution.py:429
  366.6 12.9 %select_add_fusion.5 = f32[12,64,1024]{2,1,0:T(8,128)} fusion(f32[12,64,1024]{2,1,0:T(8,128)} %get-tuple-element.588, f32[12,512,1024]{2,1,0:T(8,128)} %fusion.161, f32[12,512]{1,0:T(8,128)S(1)} %dynamic-slice_bitcast_fusion.2, pred[1024]{0:T(1024)(128)(4,1)S(1)} %compare_reduce_fusion.6, pred[]{:T(512)S(6)} %compare.3, ...), kind=kOutput, calls=%fused_computation.39.clone.1 | convolution fusion | flops 832045056 | bytes 32277508 | tf_op jit(solution)/shard_map/while/body/eval_jaxpr/while/body/eval_jaxpr/hqk,hdq->hdk/dot_general | solution.py:450
  379.5 17.4 %multiply_reduce_fusion.6 = (f32[12,512]{1,0:T(8,128)S(1)}, f32[12,512,1024]{2,1,0:T(8,128)}) fusion(f32[12,512,1024]{2,1,0:T(8,128)} %fusion.161, f32[12,512]{1,0:T(8,128)S(1)} %dynamic-slice_bitcast_fusion.2, pred[1024]{0:T(1024)(128)(4,1)S(1)} %compare_reduce_fusion.6, bf16[12,64,1024]{2,1,0:T(8,128)(2,1)} %get-tuple-element.606, ...), kind=kOutput, calls=%fused_computation.34.clone.1 | convolution fusion | flops 836757504 | bytes 52741124 | tf_op jit(solution)/shard_map/while/body/eval_jaxpr/while/body/eval_jaxpr/hdq,hdk->hqk/dot_general | solution.py:434
  396.9 21.4 %multiply_convert_fusion.3 = bf16[12,512,1024]{2,1,0:T(8,128)(2,1)} fusion(f32[12,512,1024]{2,1,0:T(8,128)} %get-tuple-element.548, f32[12,512,1024]{2,1,0:T(8,128)} %fusion.161, f32[12,512]{1,0:T(8,128)S(1)} %get-tuple-element.549, f32[12,512]{1,0:T(8,128)S(1)} %dynamic-slice_bitcast_fusion.2, pred[1024]{0:T(1024)(128)(4,1)S(1)} %compare_reduce_fusion.6), kind=kLoop, calls=%fused_computation.33.clone.1 | loop fusion | flops 37748736 | bytes 62964736 | tf_op jit(solution)/shard_map/while/body/eval_jaxpr/while/body/eval_jaxpr/convert_element_type | solution.py:438
  437.1 10.1 %fusion.161 = f32[12,512,1024]{2,1,0:T(8,128)} fusion(bf16[12,64,1024]{2,1,0:T(8,128)(2,1)S(1)} %get-tuple-element.603, bf16[2,12,64,512]{3,2,1,0:T(8,128)(2,1)S(1)} %get-tuple-element.602, s32[]{:T(128)S(6)} %copy.125), kind=kOutput, calls=%fused_computation.46.clone.1 | convolution fusion | flops 805306368 | bytes 27525124 | tf_op jit(solution)/shard_map/while/body/eval_jaxpr/while/body/eval_jaxpr/hdq,hdk->hqk/dot_general | solution.py:429
  447.2 13.8 %select_add_fusion.5 = f32[12,64,1024]{2,1,0:T(8,128)} fusion(f32[12,64,1024]{2,1,0:T(8,128)} %get-tuple-element.588, f32[12,512,1024]{2,1,0:T(8,128)} %fusion.161, f32[12,512]{1,0:T(8,128)S(1)} %dynamic-slice_bitcast_fusion.2, pred[1024]{0:T(1024)(128)(4,1)S(1)} %compare_reduce_fusion.6, pred[]{:T(512)S(6)} %compare.3, ...), kind=kOutput, calls=%fused_computation.39.clone.1 | convolution fusion | flops 832045056 | bytes 32277508 | tf_op jit(solution)/shard_map/while/body/eval_jaxpr/while/body/eval_jaxpr/hqk,hdq->hdk/dot_general | solution.py:450
  461.1 17.4 %multiply_reduce_fusion.6 = (f32[12,512]{1,0:T(8,128)S(1)}, f32[12,512,1024]{2,1,0:T(8,128)}) fusion(f32[12,512,1024]{2,1,0:T(8,128)} %fusion.161, f32[12,512]{1,0:T(8,128)S(1)} %dynamic-slice_bitcast_fusion.2, pred[1024]{0:T(1024)(128)(4,1)S(1)} %compare_reduce_fusion.6, bf16[12,64,1024]{2,1,0:T(8,128)(2,1)} %get-tuple-element.606, ...), kind=kOutput, calls=%fused_computation.34.clone.1 | convolution fusion | flops 836757504 | bytes 52741124 | tf_op jit(solution)/shard_map/while/body/eval_jaxpr/while/body/eval_jaxpr/hdq,hdk->hqk/dot_general | solution.py:434
  478.5 21.4 %multiply_convert_fusion.3 = bf16[12,512,1024]{2,1,0:T(8,128)(2,1)} fusion(f32[12,512,1024]{2,1,0:T(8,128)} %get-tuple-element.548, f32[12,512,1024]{2,1,0:T(8,128)} %fusion.161, f32[12,512]{1,0:T(8,128)S(1)} %get-tuple-element.549, f32[12,512]{1,0:T(8,128)S(1)} %dynamic-slice_bitcast_fusion.2, pred[1024]{0:T(1024)(128)(4,1)S(1)} %compare_reduce_fusion.6), kind=kLoop, calls=%fused_computation.33.clone.1 | loop fusion | flops 37748736 | bytes 62964736 | tf_op jit(solution)/shard_map/while/body/eval_jaxpr/while/body/eval_jaxpr/convert_element_type | solution.py:438
  561.7 48.4 %psum.7 = f32[9216]{0:T(1024)S(1)} all-reduce(f32[9216]{0:T(1024)S(1)} %constant_dynamic-update-slice_fusion), channel_id=1, replica_groups=mesh['dp'=8,'fsdp'=4] {'dp','fsdp'}, use_global_device_ids=true, to_apply=%region_24.25 | all-reduce | flops 9216 | bytes 73728 | tf_op jit(solution)/shard_map/psum | solution.py:613
  621.3 95.5 %scatter_all.2 = (f32[96,576]{1,0:T(8,128)}, f32[96,192]{1,0:T(8,128)}, f32[96,768]{1,0:T(8,128)}, f32[192,384]{1,0:T(8,128)}) custom-call(bf16[2,2,4,2,96,576]{5,4,3,2,1,0:T(8,128)(2,1)} %bitcast.316, bf16[2,2,4,2,96,192]{5,4,3,2,1,0:T(8,128)(2,1)} %bitcast.326, bf16[2,2,4,2,96,768]{5,4,3,2,1,0:T(8,128)(2,1)} %bitcast.296, ...), custom_call_target="tpu_custom_call" | custom-call | tf_op jit(solution)/shard_map/scatter_all/pallas_call | solution.py:326
  723.3 99.1 %gather_all.3 = (bf16[2,2,4,2,96,576]{5,4,3,2,1,0:T(8,128)(2,1)}, bf16[2,2,4,2,96,192]{5,4,3,2,1,0:T(8,128)(2,1)}, bf16[2,2,4,2,96,768]{5,4,3,2,1,0:T(8,128)(2,1)}, bf16[4,2,2,2,192,384]{5,4,3,2,1,0:T(8,128)(2,1)}) custom-call(bf16[96,576]{1,0:T(8,128)(2,1)} %convert_element_type.146.refs_0_, bf16[96,192]{1,0:T(8,128)(2,1)} %convert_element_type.147.refs_1_, ...), custom_call_target="tpu_custom_call" | custom-call | tf_op jit(solution)/shard_map/gather_all/pallas_call | solution.py:283
  843.0 19.7 %conditional.3 = (f32[1,2,768,768]{3,2,1,0:T(8,128)}, bf16[768,768]{0,1:T(8,128)(2,1)S(1)}) conditional(s32[]{:T(128)} %convert_element_type.145, f32[1,2,768,768]{3,2,1,0:T(8,128)} %copy.164, (f32[1,2,768,768]{3,2,1,0:T(8,128)}, bf16[768,768]{0,1:T(8,128)(2,1)S(1)}, f32[1,2,768,768]{3,2,1,0:T(8,128)}) %tuple.67), branch_computations={%region_39.40_spmd, %region_40.41_spmd} | conditional | flops 12687704064 | bytes 56623148 | solution.py:648
  889.1 97.9 %scatter_all.3 = (f32[96,576]{1,0:T(8,128)}, f32[96,192]{1,0:T(8,128)}, f32[96,768]{1,0:T(8,128)}, f32[192,384]{1,0:T(8,128)}) custom-call(bf16[2,2,4,2,96,576]{5,4,3,2,1,0:T(8,128)(2,1)} %bitcast.315, bf16[2,2,4,2,96,192]{5,4,3,2,1,0:T(8,128)(2,1)} %bitcast.333, bf16[2,2,4,2,96,768]{5,4,3,2,1,0:T(8,128)(2,1)} %bitcast.298, ...), custom_call_target="tpu_custom_call" | custom-call | tf_op jit(solution)/shard_map/scatter_all/pallas_call | solution.py:326
  (302 shorter events, 308.1 us)
Async XLA Ops:
  0.6 19.9 %copy-start.25 = (bf16[1024,768]{1,0:T(8,128)(2,1)S(1)}, bf16[1024,768]{1,0:T(8,128)(2,1)}, u32[]{:S(2)}) copy-start(bf16[1024,768]{1,0:T(8,128)(2,1)} %param.29) | copy-start | bytes 4718596
  0.7 17.9 %copy-start.42 = (f32[96,576]{1,0:T(8,128)S(1)}, f32[96,576]{1,0:T(8,128)}, u32[]{:S(2)}) copy-start(f32[96,576]{1,0:T(8,128)} %param.32) | copy-start | bytes 663556
  0.7 17.3 %copy-start.48 = (f32[96,192]{1,0:T(8,128)S(1)}, f32[96,192]{1,0:T(8,128)}, u32[]{:S(2)}) copy-start(f32[96,192]{1,0:T(8,128)} %param.33) | copy-start | bytes 221188
  0.7 18.6 %copy-start.34 = (f32[96,768]{1,0:T(8,128)S(1)}, f32[96,768]{1,0:T(8,128)}, u32[]{:S(2)}) copy-start(f32[96,768]{1,0:T(8,128)} %param.34) | copy-start | bytes 884740
  0.7 19.2 %copy-start.36 = (f32[384,192]{0,1:T(8,128)S(1)}, f32[384,192]{0,1:T(8,128)}, u32[]{:S(2)}) copy-start(f32[384,192]{0,1:T(8,128)} %param.35) | copy-start | bytes 884740
  0.7 16.0 %copy-start.51 = (f32[9216]{0:T(1024)S(1)}, f32[9216]{0:T(1024)}, u32[]{:S(2)}) copy-start(f32[9216]{0:T(1024)} %param.36) | copy-start | bytes 110596
  17.9 121.1 %copy-start.55 = (f32[768]{0:T(1024)}, f32[768]{0:T(1024)S(1)}, u32[]{:S(2)}) copy-start(f32[768]{0:T(1024)S(1)} %get-tuple-element.416) | copy-start | bytes 9220
  17.9 121.1 %copy-start.71 = (f32[768]{0:T(1024)}, f32[768]{0:T(1024)S(1)}, u32[]{:S(2)}) copy-start(f32[768]{0:T(1024)S(1)} %get-tuple-element.415) | copy-start | bytes 9220
  21.3 117.6 %copy-start.6 = (bf16[1024,768]{0,1:T(8,128)(2,1)}, bf16[1024,768]{0,1:T(8,128)(2,1)S(1)}, u32[]{:S(2)}) copy-start(bf16[1024,768]{0,1:T(8,128)(2,1)S(1)} %copy.48) | copy-start | bytes 4718596
  21.6 117.4 %copy-start.52 = (f32[1024]{0:T(1024)}, f32[1024]{0:T(1024)S(1)}, u32[]{:S(2)}) copy-start(f32[1024]{0:T(1024)S(1)} %broadcast_multiply_fusion.1) | copy-start | bytes 12292
  23.3 115.7 %copy-start.57 = (f32[1024]{0:T(1024)}, f32[1024]{0:T(1024)S(1)}, u32[]{:S(2)}) copy-start(f32[1024]{0:T(1024)S(1)} %fusion.85) | copy-start | bytes 12292
  166.6 11.4 %copy-start.5 = (bf16[12,64,1024]{2,1,0:T(8,128)(2,1)S(1)}, bf16[12,64,1024]{2,1,0:T(8,128)(2,1)}, u32[]{:S(2)}) copy-start(bf16[12,64,1024]{2,1,0:T(8,128)(2,1)} %get-tuple-element.571) | copy-start | bytes 4718596 | tf_op jit(solution)/shard_map/while/body/eval_jaxpr/while
  166.6 11.4 %copy-start.30 = (bf16[2,12,64,512]{3,2,1,0:T(8,128)(2,1)S(1)}, bf16[2,12,64,512]{3,2,1,0:T(8,128)(2,1)}, u32[]{:S(2)}) copy-start(bf16[2,12,64,512]{3,2,1,0:T(8,128)(2,1)} %get-tuple-element.559) | copy-start | bytes 4718596 | tf_op jit(solution)/shard_map/while/body/eval_jaxpr/while
  201.2 11.4 %copy-start.5 = (bf16[12,64,1024]{2,1,0:T(8,128)(2,1)S(1)}, bf16[12,64,1024]{2,1,0:T(8,128)(2,1)}, u32[]{:S(2)}) copy-start(bf16[12,64,1024]{2,1,0:T(8,128)(2,1)} %get-tuple-element.571) | copy-start | bytes 4718596 | tf_op jit(solution)/shard_map/while/body/eval_jaxpr/while
  201.2 11.4 %copy-start.30 = (bf16[2,12,64,512]{3,2,1,0:T(8,128)(2,1)S(1)}, bf16[2,12,64,512]{3,2,1,0:T(8,128)(2,1)}, u32[]{:S(2)}) copy-start(bf16[2,12,64,512]{3,2,1,0:T(8,128)(2,1)} %get-tuple-element.559) | copy-start | bytes 4718596 | tf_op jit(solution)/shard_map/while/body/eval_jaxpr/while
  232.5 35.7 %copy-start.27 = (bf16[1024,768]{1,0:T(8,128)(2,1)S(1)}, bf16[1024,768]{1,0:T(8,128)(2,1)}, u32[]{:S(2)}) copy-start(bf16[1024,768]{1,0:T(8,128)(2,1)} %param.31) | copy-start | bytes 4718596
  268.2 17.4 %copy-start.74 = (f32[768]{0:T(1024)S(1)}, f32[768]{0:T(1024)}, u32[]{:S(2)}) copy-start(f32[768]{0:T(1024)} %get-tuple-element.409) | copy-start | bytes 9220
  356.4 10.1 %copy-start.13 = (bf16[2,12,64,512]{3,2,1,0:T(8,128)(2,1)S(1)}, bf16[2,12,64,512]{3,2,1,0:T(8,128)(2,1)}, u32[]{:S(2)}) copy-start(bf16[2,12,64,512]{3,2,1,0:T(8,128)(2,1)} %get-tuple-element.605) | copy-start | bytes 4718596 | tf_op jit(solution)/shard_map/while/body/eval_jaxpr/while
  437.1 10.1 %copy-start.13 = (bf16[2,12,64,512]{3,2,1,0:T(8,128)(2,1)S(1)}, bf16[2,12,64,512]{3,2,1,0:T(8,128)(2,1)}, u32[]{:S(2)}) copy-start(bf16[2,12,64,512]{3,2,1,0:T(8,128)(2,1)} %get-tuple-element.605) | copy-start | bytes 4718596 | tf_op jit(solution)/shard_map/while/body/eval_jaxpr/while
  889.1 97.9 %copy-start.43 = (f32[96,576]{1,0:T(8,128)S(1)}, f32[96,576]{1,0:T(8,128)}, u32[]{:S(2)}) copy-start(f32[96,576]{1,0:T(8,128)} %param.32) | copy-start | bytes 663556
  889.1 99.7 %copy-start.49 = (f32[96,192]{1,0:T(8,128)S(1)}, f32[96,192]{1,0:T(8,128)}, u32[]{:S(2)}) copy-start(f32[96,192]{1,0:T(8,128)} %param.33) | copy-start | bytes 221188
  889.1 101.2 %copy-start.35 = (f32[96,768]{1,0:T(8,128)S(1)}, f32[96,768]{1,0:T(8,128)}, u32[]{:S(2)}) copy-start(f32[96,768]{1,0:T(8,128)} %param.34) | copy-start | bytes 884740
  889.1 102.9 %copy-start.37 = (f32[384,192]{0,1:T(8,128)S(1)}, f32[384,192]{0,1:T(8,128)}, u32[]{:S(2)}) copy-start(f32[384,192]{0,1:T(8,128)} %param.35) | copy-start | bytes 884740
  889.1 104.6 %copy-start.44 = (f32[96,576]{1,0:T(8,128)S(1)}, f32[96,576]{1,0:T(8,128)}, u32[]{:S(2)}) copy-start(f32[96,576]{1,0:T(8,128)} %get-tuple-element.629) | copy-start | bytes 663556
  (61 other events, 236.6 us)

commit v2 on v0

--- a/solution.py
+++ b/solution.py
@@ -3,7 +3,857 @@
 import jax
 import jax.numpy as jnp
 from jax import lax
+from jax.experimental import pallas as pl
+from jax.experimental.pallas import tpu as pltpu
 from jax.sharding import PartitionSpec as P
+
+MESH = pl.DeviceIdType.MESH
+ANY = pl.BlockSpec(memory_space=pl.ANY)
+VM = pl.BlockSpec(memory_space=pltpu.VMEM)
+
+
+class Grid:
+    def __init__(self, n_dp, n_fsdp):
+        self.Z = 4
+        self.X = n_dp // 4
+        self.Y = n_fsdp // 2
+        self.swap = self.X == self.Y
+        self.A, self.B = self.X, self.Y
+
+    def here(self):
+        dp, fs = lax.axis_index("dp"), lax.axis_index("fsdp")
+        self.z, self.x = dp // self.X, dp % self.X
+        self.y, self.c = fs // 2, fs % 2
+        if self.swap:
+            self.a = self.x + self.c * (self.y - self.x)
+            self.b = self.y + self.c * (self.x - self.y)
+        else:
+            self.a, self.b = self.x, self.y
+        return self
+
+    def xy(self, a, b, c):
+        if self.swap:
+            return a + c * (b - a), b + c * (a - b)
+        return a, b
+
+    def device(self, z, a, b, c, frame=None):
+        x, y = self.xy(a, b, self.c if frame is None else frame)
+        return {"dp": z * self.X + x, "fsdp": y * 2 + c}
+
+    def shape(self, order, r, w):
+        if order == "j":
+            return (self.Y, 2, self.Z, self.X, r, w)
+        return (self.Z, self.X, self.Y, 2, r, w)
+
+    def at(self, ref, order, y, c, z, x):
+        return ref.at[y, c, z, x] if order == "j" else ref.at[z, x, y, c]
+
+    def peers(self):
+        out = [self.device((self.z + k) % self.Z, self.a, self.b, self.c) for k in range(1, self.Z)]
+        out += [self.device(self.z, (self.a + k) % self.A, self.b, self.c) for k in range(1, self.A)]
+        out += [self.device(self.z, self.a, (self.b + k) % self.B, self.c) for k in range(1, self.B)]
+        out += [{"dp": self.z * self.X + self.x, "fsdp": self.y * 2 + 1 - self.c}]
+        return out
+
+    def barrier(self):
+        sem = pltpu.get_barrier_semaphore()
+        peers = self.peers()
+        for peer in peers:
+            pl.semaphore_signal(sem, inc=1, device_id=peer, device_id_type=MESH)
+        pl.semaphore_wait(sem, len(peers))
+
+
+def remote(src, dst, send, recv, slot, device):
+    return pltpu.make_async_remote_copy(
+        src_ref=src, dst_ref=dst, send_sem=send.at[slot], recv_sem=recv.at[slot], device_id=device, device_id_type=MESH
+    )
+
+
+def start_all(copies):
+    for copy in copies:
+        copy.start()
+
+
+def arrived(copies):
+    for copy in copies:
+        copy.wait_recv()
+
+
+def sent(copies):
+    for copy in copies:
+        copy.wait_send()
+
+
+class Gather:
+    def __init__(self, g, order, path, rows, src, out, local, send, recv):
+        size = {"z": g.Z, "a": g.A, "b": g.B}
+        place = {"z": g.z, "a": g.a, "b": g.b}
+
+        def piece(cell):
+            x, y = g.xy(cell["a"], cell["b"], g.c)
+            return g.at(out, order, y, g.c, cell["z"], x).at[..., rows, :]
+
+        def cells(full):
+            out = [dict(place)]
+            for axis in full:
+                if axis == "z":
+                    out = [dict(cell, z=slice(None)) for cell in out]
+                else:
+                    out = [dict(cell, **{axis: n}) for cell in out for n in range(size[axis])]
+            return out
+
+        near = {"dp": g.z * g.X + g.x, "fsdp": g.y * 2 + 1 - g.c}
+        self.slot = 0
+
+        def copy(start, end, device):
+            self.slot += 1
+            return remote(start, end, send, recv, self.slot - 1, device)
+
+        own = src.at[rows, :]
+        self.own = pltpu.make_async_copy(own, piece(place), local)
+        self.stages, self.near = [], [[copy(own, piece(place), near)]]
+        full = ""
+        for axis in path:
+            out_copies, near_copies = [], []
+            for cell in cells(full):
+                start = piece(cell) if full else own
+                for k in range(1, size[axis]):
+                    to = dict(place, **{axis: (place[axis] + k) % size[axis]})
+                    out_copies.append(copy(start, piece(cell), g.device(to["z"], to["a"], to["b"], g.c)))
+                    came = piece(dict(cell, **{axis: (place[axis] - k + size[axis]) % size[axis]}))
+                    near_copies.append(copy(came, came, near))
+            self.stages.append(out_copies)
+            self.near.append(near_copies)
+            full += axis
+
+    @staticmethod
+    def slots(g):
+        zab = (g.Z - 1) + (g.A - 1) + g.A * (g.B - 1)
+        abz = (g.A - 1) + g.A * (g.B - 1) + g.A * g.B * (g.Z - 1)
+        return 1 + 2 * max(zab, abz)
+
+    def step(self, number):
+        if number == 0:
+            self.own.start()
+        else:
+            if number == 1:
+                self.own.wait()
+            arrived(self.stages[number - 1])
+        start_all(self.near[number])
+        if number < 3:
+            start_all(self.stages[number])
+
+    def finish(self):
+        for group in self.near:
+            arrived(group)
+        for group in self.near + self.stages:
+            sent(group)
+
+
+class Scatter:
+    def __init__(self, g, order, path, rows, src, bufs, local, send, recv):
+        self.g, self.path, self.count = g, path, rows.size
+        self.work, self.mine = bufs[0], bufs[1]
+        self.recv = dict(zip(path, bufs[2:]))
+        work, other = self.work, 1 - g.c
+        size = {"z": g.Z, "a": g.A, "b": g.B}
+        place = {"z": g.z, "a": g.a, "b": g.b}
+        self.size = size
+        self.slot = 0
+
+        def copy(start, end, device):
+            self.slot += 1
+            return remote(start, end, send, recv, self.slot - 1, device)
+
+        self.owns, near = [], []
+        for b in range(g.B):
+            for a in range(g.A):
+                x, y = g.xy(a, b, other)
+                near.append(copy(g.at(src, order, y, other, slice(None), x).at[:, rows, :], work.at[b, :, a],
+                                 {"dp": g.z * g.X + g.x, "fsdp": g.y * 2 + other}))
+                x, y = g.xy(a, b, g.c)
+                self.owns.append(pltpu.make_async_copy(g.at(src, order, y, g.c, slice(None), x).at[:, rows, :],
+                                                       self.mine.at[b, :, a], local.at[b * g.A + a]))
+        self.stages = [near]
+        done = ""
+        for axis in path:
+            copies = []
+            for k in range(1, size[axis]):
+                to = dict(place, **{axis: (place[axis] + k) % size[axis]})
+                where = {name: (place[name] if name in done else slice(None)) for name in "bza"}
+                where[axis] = to[axis]
+                copies.append(copy(work.at[where["b"], where["z"], where["a"]], self.recv[axis].at[k - 1],
+                                   g.device(to["z"], to["a"], to["b"], g.c)))
+            self.stages.append(copies)
+            done += axis
+
+    @staticmethod
+    def slots(g):
+        return g.A * g.B + (g.B - 1) + (g.A - 1) + (g.Z - 1)
+
+    @staticmethod
+    def scratch(g, path, r, w):
+        size = {"z": g.Z, "a": g.A, "b": g.B}
+        out = [pltpu.VMEM((g.B, g.Z, g.A, r, w), jnp.bfloat16)] * 2
+        done = ""
+        for axis in path:
+            done += axis
+            out.append(pltpu.VMEM((size[axis] - 1,) + tuple(size[n] for n in "bza" if n not in done) + (r, w), jnp.bfloat16))
+        return out
+
+    def _cell(self, index, done):
+        place = {"z": self.g.z, "a": self.g.a, "b": self.g.b}
+        return [place[n] if n in done else index[n] for n in "bza"]
+
+    def _add(self, number):
+        g, done = self.g, self.path[:number]
+        left = [n for n in "bza" if n not in done]
+        total = 1
+        for name in left:
+            total *= self.size[name]
+
+        def add(n, carry):
+            index = {}
+            for name in reversed(left):
+                index[name] = n % self.size[name]
+                n = n // self.size[name]
+            b, z, a = self._cell(index, done)
+            if number == 0:
+                summed = self.work[b, z, a].astype(jnp.float32) + self.mine[b, z, a].astype(jnp.float32)
+            else:
+                summed = self._sum(number, b, z, a, [index[name] for name in left])
+            self.work[b, z, a] = summed.astype(jnp.bfloat16)
+            return carry
+
+        lax.fori_loop(0, total, add, 0)
+
+    def _sum(self, number, b, z, a, index):
+        axis = self.path[number - 1]
+        summed = self.work[b, z, a].astype(jnp.float32)
+        for k in range(self.size[axis] - 1):
+            summed = summed + self.recv[axis][tuple([k] + index)].astype(jnp.float32)
+        return summed
+
+    def step(self, number):
+        if number == 0:
+            start_all(self.stages[0] + self.owns)
+            return
+        if number == 1:
+            for copy in self.owns:
+                copy.wait()
+        arrived(self.stages[number - 1])
+        self._add(number - 1)
+        start_all(self.stages[number])
+
+    def total(self):
+        arrived(self.stages[3])
+        return self._sum(3, self.g.b, self.g.z, self.g.a, [])
+
+    def finish(self):
+        for group in self.stages:
+            sent(group)
+
+
+GATHER_PATHS = ("zab", "abz")
+SCATTER_PATHS = ("baz", "zba")
+
+
+def row_parts(rows):
+    first = rows * 2 // 3 // 16 * 16
+    if first == 0 or first == rows:
+        return [(0, pl.ds(0, rows))]
+    return [(0, pl.ds(0, first)), (1, pl.ds(first, rows - first))]
+
+
+def job_list(sizes):
+    return [(n, path, rows) for n, (r, _) in enumerate(sizes) for path, rows in row_parts(r)]
+
+
+def rounds(jobs, last):
+    return [(n, step) for step in range(last + 1) for n in range(len(jobs))]
+
+
+def gather_scratch(g, count):
+    lanes = Gather.slots(g)
+    dma = pltpu.SemaphoreType.DMA
+    return [dma((count,)), dma((count, lanes)), dma((count, lanes))]
+
+
+def gather_all(n_dp, n_fsdp, shards, orders, collective_id):
+    grid = Grid(n_dp, n_fsdp)
+    count = len(shards)
+    jobs = job_list([s.shape for s in shards])
+
+    def kernel(*refs):
+        ins, outs, (local, send, recv) = refs[:count], refs[count : 2 * count], refs[2 * count :]
+        g = grid.here()
+        g.barrier()
+        work = [Gather(g, orders[n], GATHER_PATHS[path], rows, ins[n], outs[n], local.at[j], send.at[j], recv.at[j])
+                for j, (n, path, rows) in enumerate(jobs)]
+        for j, step in rounds(jobs, 3):
+            work[j].step(step)
+        for job in work:
+            job.finish()
+
+    return pl.pallas_call(
+        kernel,
+        out_shape=[jax.ShapeDtypeStruct(grid.shape(o, *s.shape), s.dtype) for s, o in zip(shards, orders)],
+        in_specs=[ANY] * count,
+        out_specs=[ANY] * count,
+        scratch_shapes=gather_scratch(grid, len(jobs)),
+        compiler_params=pltpu.CompilerParams(collective_id=collective_id, has_side_effects=True),
+        name="gather_all",
+    )(*shards)
+
+
+def scatter_scratch(g, sizes, jobs):
+    out = []
+    for n, path, rows in jobs:
+        out += Scatter.scratch(g, SCATTER_PATHS[path], rows.size, sizes[n][1])
+    dma = pltpu.SemaphoreType.DMA
+    lanes = Scatter.slots(g)
+    return out + [dma((len(jobs), g.A * g.B)), dma((len(jobs), lanes)), dma((len(jobs), lanes))]
+
+
+def scatter_jobs(g, orders, jobs, ins, scratch):
+    local, send, recv = scratch[5 * len(jobs) :]
+    return [Scatter(g, orders[n], SCATTER_PATHS[path], rows, ins[n], scratch[5 * j : 5 * j + 5], local.at[j], send.at[j],
+                    recv.at[j]) for j, (n, path, rows) in enumerate(jobs)]
+
+
+def scatter_all(n_dp, n_fsdp, wholes, orders, collective_id, dtype=jnp.float32):
+    grid = Grid(n_dp, n_fsdp)
+    count = len(wholes)
+    sizes = [w.shape[-2:] for w in wholes]
+    jobs = job_list(sizes)
+
+    def kernel(*refs):
+        ins, outs, scratch = refs[:count], refs[count : 2 * count], refs[2 * count :]
+        g = grid.here()
+        g.barrier()
+        work = scatter_jobs(g, orders, jobs, ins, scratch)
+        for j, step in rounds(jobs, 3):
+            work[j].step(step)
+        for job, (n, path, rows) in zip(work, jobs):
+            outs[n][rows, :] = job.total().astype(dtype)
+        for job in work:
+            job.finish()
+
+    return pl.pallas_call(
+        kernel,
+        out_shape=[jax.ShapeDtypeStruct(s, dtype) for s in sizes],
+        in_specs=[ANY] * count,
+        out_specs=[VM] * count,
+        scratch_shapes=scatter_scratch(grid, sizes, jobs),
+        compiler_params=pltpu.CompilerParams(collective_id=collective_id, has_side_effects=True,
+                                             vmem_limit_bytes=60 * 1024 * 1024),
+        name="scatter_all",
+    )(*wholes)
+
+
+HEAD = 64
+PAIR = 128
+
+
+def last_dot(left, right):
+    return lax.dot_general(left, right, (((1,), (1,)), ((), ())), preferred_element_type=jnp.float32)
+
+
+def plain_dot(left, right):
+    return lax.dot_general(left, right, (((1,), (0,)), ((), ())), preferred_element_type=jnp.float32)
+
+
+def attend_block(length, start, size, q_heads, k_ref, v_turned, o_ref, lse_ref):
+    slots = k_ref.shape[0]
+    half = slots // 2
+    keys = k_ref[...]
+    key_index = lax.broadcasted_iota(jnp.int32, (slots - half, size), 0) + half
+    scores, tops = [], []
+    for head in range(2):
+        q = q_heads[head, pl.ds(start, size), :]
+        low = last_dot(keys[:half], q)
+        high = jnp.where(key_index < length, last_dot(keys[half:], q), -1000000000.0)
+        tops.append(jnp.maximum(jnp.max(low, axis=0, keepdims=True), jnp.max(high, axis=0, keepdims=True)))
+        scores.append((low, high))
+    raised = [[jnp.exp(s - tops[head]).astype(jnp.bfloat16) for s in scores[head]] for head in range(2)]
+    parts = []
+    for head in range(2):
+        summed = plain_dot(v_turned[head][:, :half], raised[head][0])
+        summed = summed + plain_dot(v_turned[head][:, half:], raised[head][1])
+        mine = summed[head * HEAD : (head + 1) * HEAD]
+        total = summed[(1 - head) * HEAD : (1 - head) * HEAD + 1]
+        parts.append(mine * (1.0 / total))
+        lse_ref[head, pl.ds(start, size)] = (tops[head] + jnp.log(total))[0]
+    o_ref[pl.ds(start, size), :] = jnp.concatenate(parts, axis=0).T.astype(jnp.bfloat16)
+
+
+def attend_prepare(q_ref, v_ref, q_heads, v_turned):
+    slots = q_ref.shape[0]
+    lane = lax.broadcasted_iota(jnp.int32, (slots, PAIR), 1)
+    row = lax.broadcasted_iota(jnp.int32, (PAIR, slots), 0)
+    q = q_ref[...].astype(jnp.float32) * (HEAD ** (-0.5))
+    v = v_ref[...].astype(jnp.float32).T
+    for head in range(2):
+        q_heads[head] = jnp.where(lane // HEAD == head, q, 0.0).astype(jnp.bfloat16)
+        v_turned[head] = jnp.where(row // HEAD == head, v, 1.0).astype(jnp.bfloat16)
+
+
+def attend_kernel(size, count_ref, q_ref, k_ref, v_ref, o_ref, lse_ref, q_heads, v_turned):
+    attend_prepare(q_ref, v_ref, q_heads, v_turned)
+    length = count_ref[0]
+
+    def step(n, carry):
+        attend_block(length, pl.multiple_of(n * size, size), size, q_heads, k_ref, v_turned, o_ref, lse_ref.at[0])
+        return carry
+
+    lax.fori_loop(0, q_ref.shape[0] // size, step, 0)
+
+
+def attend(counts, projected, size=256):
+    slots, width = projected.shape
+    d = width // 3
+    pairs = d // PAIR
+    spec = lambda part: pl.BlockSpec((slots, PAIR), lambda p, n, part=part: (0, part * pairs + p))
+    return pl.pallas_call(
+        partial(attend_kernel, size),
+        out_shape=[jax.ShapeDtypeStruct((slots, d), jnp.bfloat16),
+                   jax.ShapeDtypeStruct((pairs, 2, slots), jnp.float32)],
+        grid_spec=pltpu.PrefetchScalarGridSpec(
+            num_scalar_prefetch=1, grid=(pairs,),
+            in_specs=[spec(0), spec(1), spec(2)],
+            out_specs=[pl.BlockSpec((slots, PAIR), lambda p, n: (0, p)),
+                       pl.BlockSpec((1, 2, slots), lambda p, n: (p, 0, 0))],
+            scratch_shapes=[pltpu.VMEM((2, slots, PAIR), jnp.bfloat16), pltpu.VMEM((2, PAIR, slots), jnp.bfloat16)]),
+        compiler_params=pltpu.CompilerParams(vmem_limit_bytes=48 * 1024 * 1024),
+        name="attend",
+    )(counts, projected, projected, projected)
+
+
+def attend_back_scratch(slots):
+    return [pltpu.VMEM((2, slots, PAIR), jnp.bfloat16), pltpu.VMEM((2, slots, PAIR), jnp.bfloat16),
+            pltpu.VMEM((2, PAIR, slots), jnp.bfloat16), pltpu.VMEM((2, slots), jnp.float32),
+            pltpu.VMEM((slots, PAIR), jnp.float32), pltpu.VMEM((slots, PAIR), jnp.float32)]
+
+
+def attend_back_body(size, count_ref, q_ref, k_ref, v_ref, o_ref, do_ref, lse_ref, out_ref,
+                     q_heads, do_heads, k_turned, inner, dk_sum, dv_sum, hook):
+    slots = q_ref.shape[0]
+    length = count_ref[0]
+    lane = lax.broadcasted_iota(jnp.int32, (slots, PAIR), 1)
+    row = lax.broadcasted_iota(jnp.int32, (PAIR, slots), 0)
+    q = q_ref[...].astype(jnp.float32) * (HEAD ** (-0.5))
+    do = do_ref[...].astype(jnp.float32)
+    k = k_ref[...].astype(jnp.float32).T * (HEAD ** (-0.5))
+    product = (do * o_ref[...].astype(jnp.float32)).T
+    for head in range(2):
+        q_heads[head] = jnp.where(lane // HEAD == head, q, 0.0).astype(jnp.bfloat16)
+        do_heads[head] = jnp.where(lane // HEAD == head, do, 0.0).astype(jnp.bfloat16)
+        k_turned[head] = jnp.where(row // HEAD == head, k, 0.0).astype(jnp.bfloat16)
+        inner[head] = jnp.sum(product[head * HEAD : (head + 1) * HEAD], axis=0)
+    dk_sum[...] = jnp.zeros_like(dk_sum)
+    dv_sum[...] = jnp.zeros_like(dv_sum)
+    key_index = lax.broadcasted_iota(jnp.int32, (slots, size), 0)
+
+    def step(n, carry):
+        rows = pl.ds(pl.multiple_of(n * size, size), size)
+        keys, values = k_ref[...], v_ref[...]
+        dq = jnp.zeros((PAIR, size), jnp.float32)
+        for head in range(2):
+            q_block, do_block = q_heads[head, rows, :], do_heads[head, rows, :]
+            scores = last_dot(keys, q_block)
+            weights = jnp.exp(scores - lse_ref[0, head, rows][None, :])
+            weights = jnp.where(key_index < length, weights, 0.0)
+            weight_grad = last_dot(values, do_block)
+            score_grad = (weights * (weight_grad - inner[head, rows][None, :])).astype(jnp.bfloat16)
+            dv_sum[...] += plain_dot(weights.astype(jnp.bfloat16), do_block)
+            dk_sum[...] += plain_dot(score_grad, q_block)
+            dq = dq + plain_dot(k_turned[head], score_grad)
+        out_ref[0, rows, :] = dq.T.astype(jnp.bfloat16)
+        return carry
+
+    steps = slots // size
+    for half in range(2):
+        hook(half)
+        lax.fori_loop(half * steps // 2, (half + 1) * steps // 2, step, 0)
+    out_ref[1] = dk_sum[...].astype(jnp.bfloat16)
+    out_ref[2] = dv_sum[...].astype(jnp.bfloat16)
+
+
+def attend_gather(n_dp, n_fsdp, counts, projected, shards, orders, plan, collective_id, size=512):
+    slots, width = projected.shape
+    d = width // 3
+    pairs = d // PAIR
+    grid = Grid(n_dp, n_fsdp)
+    count = len(shards)
+    jobs = job_list([s.shape for s in shards])
+    steps = slots // size
+
+    def kernel(count_ref, q_ref, k_ref, v_ref, *refs):
+        ins, (o_ref, lse_ref), outs = refs[:count], refs[count : count + 2], refs[count + 2 : 2 * count + 2]
+        q_heads, v_turned, local, send, recv = refs[2 * count + 2 :]
+        g = grid.here()
+        work = [Gather(g, orders[n], GATHER_PATHS[path], rows, ins[n], outs[n], local.at[j], send.at[j], recv.at[j])
+                for j, (n, path, rows) in enumerate(jobs)]
+        pair = pl.program_id(0)
+
+        def run(when):
+            for j, step in plan.get(when, []):
+                work[j].step(step)
+
+        for p in range(pairs):
+            if any(p * steps == when for when in plan):
+
+                @pl.when(pair == p)
+                def _():
+                    if p == 0:
+                        g.barrier()
+                    run(p * steps)
+
+        attend_prepare(q_ref, v_ref, q_heads, v_turned)
+        length = count_ref[0]
+        for n in range(steps):
+            for p in range(pairs):
+                if n > 0 and p * steps + n in plan:
+                    pl.when(pair == p)(partial(run, p * steps + n))
+
+            attend_block(length, n * size, size, q_heads, k_ref, v_turned, o_ref, lse_ref.at[0])
+
+        @pl.when(pair == pairs - 1)
+        def _():
+            run("end")
+            for job in work:
+                job.finish()
+
+    spec = lambda part: pl.BlockSpec((slots, PAIR), lambda p, n, part=part: (0, part * pairs + p))
+    return pl.pallas_call(
+        kernel,
+        out_shape=[jax.ShapeDtypeStruct((slots, d), jnp.bfloat16),
+                   jax.ShapeDtypeStruct((pairs, 2, slots), jnp.float32)]
+        + [jax.ShapeDtypeStruct(grid.shape(o, *s.shape), s.dtype) for s, o in zip(shards, orders)],
+        grid_spec=pltpu.PrefetchScalarGridSpec(
+            num_scalar_prefetch=1, grid=(pairs,),
+            in_specs=[spec(0), spec(1), spec(2)] + [ANY] * count,
+            out_specs=[pl.BlockSpec((slots, PAIR), lambda p, n: (0, p)),
+                       pl.BlockSpec((1, 2, slots), lambda p, n: (p, 0, 0))] + [ANY] * count,
+            scratch_shapes=[pltpu.VMEM((2, slots, PAIR), jnp.bfloat16), pltpu.VMEM((2, PAIR, slots), jnp.bfloat16)]
+            + gather_scratch(grid, len(jobs))),
+        compiler_params=pltpu.CompilerParams(vmem_limit_bytes=56 * 1024 * 1024, collective_id=collective_id,
+                                             has_side_effects=True),
+        name="attend_gather",
+    )(counts, projected, projected, projected, *shards)
+
+
+FORWARD_PLAN = {
+    0: [(0, 0), (1, 0), (2, 0), (3, 0)],
+    2: [(0, 1), (1, 1)],
+    3: [(0, 2), (1, 2), (4, 0), (5, 0)],
+    4: [(2, 1), (3, 1)],
+    5: [(0, 3), (1, 3)],
+    7: [(2, 2), (3, 2)],
+    8: [(4, 1), (5, 1)],
+    10: [(4, 2), (5, 2)],
+    11: [(2, 3), (3, 3)],
+    "end": [(4, 3), (5, 3)],
+}
+
+
+def attend_back_scatter(n_dp, n_fsdp, counts, projected, attended, attended_grad, lse, wholes, plan, collective_id, size=256):
+    slots, width = projected.shape
+    d = width // 3
+    pairs = d // PAIR
+    grid = Grid(n_dp, n_fsdp)
+    count = len(wholes)
+    sizes = [w.shape[-2:] for w in wholes]
+    jobs = job_list(sizes)
+
+    def kernel(count_ref, q_ref, k_ref, v_ref, o_ref, do_ref, lse_ref, *refs):
+        ins, out_ref, outs = refs[:count], refs[count], refs[count + 1 : 2 * count + 1]
+        own, scratch = refs[2 * count + 1 : 2 * count + 7], refs[2 * count + 7 :]
+        g = grid.here()
+        work = scatter_jobs(g, ["j"] * count, jobs, ins, scratch)
+        pair = pl.program_id(0)
+
+        def run(when):
+            for j, step in plan.get(when, []):
+                work[j].step(step)
+
+        for p in range(pairs):
+            for half in range(2):
+                if half == 0 and p * 2 in plan:
+
+                    @pl.when(pair == p)
+                    def _():
+                        if p == 0:
+                            g.barrier()
+                        run(p * 2)
+
+        def hook(half):
+            for p in range(pairs):
+                if half and p * 2 + half in plan:
+                    pl.when(pair == p)(partial(run, p * 2 + half))
+
+        attend_back_body(size, count_ref, q_ref, k_ref, v_ref, o_ref, do_ref, lse_ref, out_ref, *own, hook)
+
+        @pl.when(pair == pairs - 1)
+        def _():
+            run("end")
+            for job, (n, path, rows) in zip(work, jobs):
+                outs[n][rows, :] = job.total().astype(jnp.bfloat16)
+            for job in work:
+                job.finish()
+
+    spec = lambda part: pl.BlockSpec((slots, PAIR), lambda p, n, part=part: (0, part * pairs + p))
+    return pl.pallas_call(
+        kernel,
+        out_shape=[jax.ShapeDtypeStruct((3, slots, d), jnp.bfloat16)]
+        + [jax.ShapeDtypeStruct(s, jnp.bfloat16) for s in sizes],
+        grid_spec=pltpu.PrefetchScalarGridSpec(
+            num_scalar_prefetch=1, grid=(pairs,),
+            in_specs=[spec(0), spec(1), spec(2), spec(0), spec(0), pl.BlockSpec((1, 2, slots), lambda p, n: (p, 0, 0))]
+            + [ANY] * count,
+            out_specs=[pl.BlockSpec((3, slots, PAIR), lambda p, n: (0, 0, p))] + [VM] * count,
+            scratch_shapes=attend_back_scratch(slots) + scatter_scratch(grid, sizes, jobs)),
+        compiler_params=pltpu.CompilerParams(vmem_limit_bytes=60 * 1024 * 1024, collective_id=collective_id,
+                                             has_side_effects=True),
+        name="attend_back_scatter",
+    )(counts, projected, projected, projected, attended, attended_grad, lse, *wholes)
+
+
+BACKWARD_PLAN = {
+    0: [(n, 0) for n in range(6)],
+    3: [(0, 1), (1, 1)],
+    4: [(2, 1), (3, 1), (4, 1), (5, 1)],
+    6: [(0, 2), (1, 2)],
+    7: [(2, 2), (3, 2), (4, 2), (5, 2)],
+    9: [(0, 3), (1, 3)],
+    10: [(2, 3), (3, 3), (4, 3), (5, 3)],
+}
+
+
+PIECE = (48, 384)
+
+
+class Spread:
+    def __init__(self, g, u, tiles, send, recv, base):
+        qkv, out, up, down = tiles
+        me = g.y * 2 + g.c
+        rows = pl.ds(pl.multiple_of(g.y * 48, 16), 48)
+        self.g, self.u, self.tiles, self.rows, self.me = g, u, tiles, rows, me
+        self.copies = []
+
+        def copy(src, dst, device):
+            self.copies.append(remote(src, dst, send, recv, base + len(self.copies), device))
+
+        for k in range(1, 4):
+            to = (me + k) % 4
+            device = {"dp": g.z * 2 + g.x, "fsdp": to}
+            block, half = self.qkv_place(to)
+            copy(u.at[block], qkv.at[half, rows, :], device)
+            copy(u.at[3], out.at[g.c, rows, :], device)
+            copy(u.at[4 + to], up.at[g.c, rows, :], device)
+        for k in range(1, 4):
+            to = (g.z + k) % 4
+            copy(u.at[8 + to], down.at[pl.ds(pl.multiple_of(g.z * 48, 16), 48), :], {"dp": to * 2 + g.x, "fsdp": me})
+
+    def qkv_place(self, to):
+        c = self.g.c
+        middle = (to + 1) // 2 % 2
+        return to - to // 3 - middle * c, middle + c - 2 * middle * c
+
+    def start(self):
+        start_all(self.copies)
+        g, u = self.g, self.u
+        qkv, out, up, down = self.tiles
+        block, half = self.qkv_place(self.me)
+        qkv[half, self.rows, :] = u[block]
+        out[g.c, self.rows, :] = u[3]
+        up[g.c, self.rows, :] = u[4 + self.me]
+        down[pl.ds(pl.multiple_of(g.z * 48, 16), 48), :] = u[8 + g.z]
+
+    def finish(self):
+        arrived(self.copies)
+        sent(self.copies)
+
+
+TILES = [jax.ShapeDtypeStruct((2, 96, 384), jnp.bfloat16)] * 3 + [jax.ShapeDtypeStruct((192, 384), jnp.bfloat16)]
+
+
+def meet_all(g, n_dp, n_fsdp):
+    count = n_dp * n_fsdp
+    me = (g.z * g.X + g.x) * n_fsdp + g.y * 2 + g.c
+    sem = pltpu.get_barrier_semaphore()
+    ranks = [(me + k) % count for k in range(1, count)]
+    peers = [{"dp": rank // n_fsdp, "fsdp": rank % n_fsdp} for rank in ranks]
+    for peer in peers:
+        pl.semaphore_signal(sem, inc=1, device_id=peer, device_id_type=MESH)
+    pl.semaphore_wait(sem, count - 1)
+    return me, ranks, peers
+
+
+def to_owners(n_dp, n_fsdp, blocks_of, u, small, collective_id):
+    grid = Grid(n_dp, n_fsdp)
+    count = n_dp * n_fsdp
+
+    def kernel(of_ref, u_ref, small_ref, got, all_small, qkv, out, up, down, slots, send, recv):
+        g = grid.here()
+        me, ranks, peers = meet_all(g, n_dp, n_fsdp)
+
+        def fill(n, carry):
+            slots[n] = u_ref[of_ref[n]]
+            return carry
+
+        lax.fori_loop(0, count, fill, 0)
+        copies = []
+        for k, (rank, peer) in enumerate(zip(ranks, peers)):
+            copies.append(remote(slots.at[rank], got.at[me], send, recv, k, peer))
+        for k, peer in enumerate(peers):
+            copies.append(remote(small_ref, all_small.at[me], send, recv, count - 1 + k, peer))
+        start_all(copies)
+        spread = Spread(g, u_ref, (qkv, out, up, down), send, recv, 2 * count - 2)
+        spread.start()
+        got[me] = slots[me]
+        all_small[me] = small_ref[...]
+        arrived(copies)
+        sent(copies)
+        spread.finish()
+
+    lanes = 2 * count - 2 + 12
+    return pl.pallas_call(
+        kernel,
+        out_shape=[jax.ShapeDtypeStruct((count,) + PIECE, jnp.bfloat16),
+                   jax.ShapeDtypeStruct((count,) + small.shape, jnp.float32)] + TILES,
+        in_specs=[pl.BlockSpec(memory_space=pltpu.SMEM), VM, VM],
+        out_specs=[VM] * 6,
+        scratch_shapes=[pltpu.VMEM((count,) + PIECE, jnp.bfloat16), pltpu.SemaphoreType.DMA((lanes,)),
+                        pltpu.SemaphoreType.DMA((lanes,))],
+        compiler_params=pltpu.CompilerParams(collective_id=collective_id, has_side_effects=True),
+        name="to_owners",
+    )(blocks_of, u, small)
+
+
+def to_tiles(n_dp, n_fsdp, owners, pieces, collective_id):
+    grid = Grid(n_dp, n_fsdp)
+    count = n_dp * n_fsdp
+
+    def kernel(owners_ref, pieces_ref, qkv, out, up, down, got, u, send, recv):
+        g = grid.here()
+        me, ranks, peers = meet_all(g, n_dp, n_fsdp)
+        copies = [remote(pieces_ref.at[rank], got.at[me], send, recv, k, peer)
+                  for k, (rank, peer) in enumerate(zip(ranks, peers))]
+        start_all(copies)
+        got[me] = pieces_ref[me]
+        arrived(copies)
+
+        def fill(n, carry):
+            u[n] = got[owners_ref[n]]
+            return carry
+
+        lax.fori_loop(0, 12, fill, 0)
+        spread = Spread(g, u, (qkv, out, up, down), send, recv, count - 1)
+        spread.start()
+        sent(copies)
+        spread.finish()
+
+    lanes = count - 1 + 12
+    return pl.pallas_call(
+        kernel,
+        out_shape=TILES,
+        in_specs=[pl.BlockSpec(memory_space=pltpu.SMEM), VM],
+        out_specs=[VM] * 4,
+        scratch_shapes=[pltpu.VMEM((count,) + PIECE, jnp.bfloat16), pltpu.VMEM((12,) + PIECE, jnp.bfloat16),
+                        pltpu.SemaphoreType.DMA((lanes,)), pltpu.SemaphoreType.DMA((lanes,))],
+        compiler_params=pltpu.CompilerParams(collective_id=collective_id, has_side_effects=True),
+        name="to_tiles",
+    )(owners, pieces)
+
+
+def piece_rows(turned, z, x, y, c):
+    if turned:
+        return 192 * (2 * y + c) + 48 * z, 384 * x
+    return 96 * (2 * z + x) + 48 * y, 384 * c
+
+
+def places():
+    return [(z, x, y, c) for z in range(4) for x in range(2) for y in range(2) for c in range(2)]
+
+
+def precondition_kernel(flags, pieces, stats, roots, new_stats, steps, block, turned):
+    own, down = flags[0], flags[1]
+
+    @pl.when(own == 0)
+    def _():
+        new_stats[...] = stats[...]
+
+    @pl.when(own == 1)
+    def _():
+        for kind in range(2):
+
+            @pl.when(down == kind)
+            def _():
+                for n, place in enumerate(places()):
+                    row, column = piece_rows(kind, *place)
+                    block[row : row + 48, column : column + 384] = pieces[n]
+
+        turned[...] = block[...].astype(jnp.float32).T.astype(jnp.bfloat16)
+        new_stats[down] = 0.5 * stats[down] + 0.5 * last_dot(block[...], block[...])
+        new_stats[1 - down] = 0.5 * stats[1 - down] + 0.5 * last_dot(turned[...], turned[...])
+        left = plain_dot(roots[down].astype(jnp.bfloat16), block[...]).astype(jnp.bfloat16)
+        block[...] = plain_dot(left, roots[1 - down].astype(jnp.bfloat16)).astype(jnp.bfloat16)
+        for kind in range(2):
+
+            @pl.when(down == kind)
+            def _():
+                for n, place in enumerate(places()):
+                    row, column = piece_rows(kind, *place)
+                    steps[n] = block[row : row + 48, column : column + 384]
+
+
+def precondition(flags, pieces, stats, roots):
+    return pl.pallas_call(
+        precondition_kernel,
+        out_shape=[jax.ShapeDtypeStruct(stats.shape, jnp.float32), jax.ShapeDtypeStruct(pieces.shape, jnp.bfloat16)],
+        in_specs=[pl.BlockSpec(memory_space=pltpu.SMEM), VM, VM, VM],
+        out_specs=[VM, VM],
+        scratch_shapes=[pltpu.VMEM(stats.shape[1:], jnp.bfloat16)] * 2,
+        compiler_params=pltpu.CompilerParams(vmem_limit_bytes=56 * 1024 * 1024),
+        name="precondition",
+    )(flags, pieces, stats, roots)
+
+
+def block_grads_kernel(turned_blocks, left, right, out, sums, left_turned):
+    @pl.when(pl.program_id(0) == 0)
+    def _():
+        left_turned[...] = left[...].astype(jnp.float32).T.astype(jnp.bfloat16)
+
+    values = right[...].reshape(right.shape[-2:])
+    grad = plain_dot(left_turned[...], values).astype(jnp.bfloat16)
+    for z, x, y, c in places():
+        row, column = piece_rows(turned_blocks, z, x, y, c)
+        out[y, c, z, x] = grad[row : row + 48, column : column + 384]
+    sums[...] = jnp.sum(values.astype(jnp.float32), axis=0).reshape(sums.shape)
+
+
+def block_grads(left, right, turned_blocks):
+    rows, d = left.shape
+    if right.ndim == 3:
+        count = right.shape[0]
+        spec = pl.BlockSpec((1, rows, d), lambda b: (b, 0, 0))
+    else:
+        count = right.shape[1] // d
+        spec = pl.BlockSpec((rows, d), lambda b: (0, b))
+    return pl.pallas_call(
+        partial(block_grads_kernel, turned_blocks),
+        out_shape=[jax.ShapeDtypeStruct((2, 2, 4, 2, count * 48, 384), jnp.bfloat16),
+                   jax.ShapeDtypeStruct((count, 1, d), jnp.float32)],
+        grid=(count,),
+        in_specs=[pl.BlockSpec((rows, d), lambda b: (0, 0)), spec],
+        out_specs=[pl.BlockSpec((2, 2, 4, 2, 48, 384), lambda b: (0, 0, 0, 0, b, 0)),
+                   pl.BlockSpec((1, 1, d), lambda b: (b, 0, 0))],
+        scratch_shapes=[pltpu.VMEM((d, rows), jnp.bfloat16)],
+        compiler_params=pltpu.CompilerParams(vmem_limit_bytes=56 * 1024 * 1024),
+        name="block_grads",
+    )(left, right)
+
 
 D = 768
 HEADS = 12
@@ -184,7 +1034,7 @@
     return picked
 
 
-def local(
+def local_any(
     tokens,
     counts,
     cotangent,
@@ -438,6 +1288,149 @@
     )
 
 
+def local_staged(
+    sizes,
+    tokens,
+    counts,
+    cotangent,
+    qkv_weight,
+    out_weight,
+    up_weight,
+    down_weight,
+    small_params,
+    statistics,
+    inverse_roots,
+    owners,
+):
+    n_dp, n_fsdp = sizes
+    qkv_low = qkv_weight.astype(jnp.bfloat16)
+    later = (
+        out_weight.astype(jnp.bfloat16),
+        up_weight.astype(jnp.bfloat16),
+        down_weight.astype(jnp.bfloat16).T,
+    )
+    (
+        gain_one,
+        shift_one,
+        gain_two,
+        shift_two,
+        bias_query,
+        bias_value,
+        bias_out,
+        bias_down,
+        bias_up,
+    ) = unpack(small_params)
+    (qkv_pieces,) = gather_all(n_dp, n_fsdp, (qkv_low,), ("j",), 1)
+    qkv_full = whole_of(qkv_pieces)
+    inputs = tokens.astype(jnp.float32)
+    normed = layer_norm(inputs, gain_one, shift_one).astype(jnp.bfloat16)
+    bias_qkv = jnp.concatenate([bias_query, jnp.zeros((D,), jnp.float32), bias_value])
+    projected = (row_dot(normed, qkv_full) + bias_qkv).astype(jnp.bfloat16)
+    attended, log_totals, out_pieces, up_pieces, down_pieces = attend_gather(
+        n_dp, n_fsdp, counts, projected, later, ("j", "j", "i"), FORWARD_PLAN, 2
+    )
+    out_full, up_full, down_full_t = whole_of(out_pieces), whole_of(up_pieces), whole_of(down_pieces)
+    middle = inputs + (row_dot(attended, out_full) + bias_out)
+    normed_two = layer_norm(middle, gain_two, shift_two).astype(jnp.bfloat16)
+    hidden = row_dot(normed_two, up_full) + bias_up
+    active = jax.nn.gelu(hidden, approximate=False).astype(jnp.bfloat16)
+    layer_rows = (middle + transposed_dot(active, down_full_t) + bias_down).astype(jnp.bfloat16)
+    grad_bias_down = jnp.sum(cotangent.astype(jnp.float32), axis=0)
+    active_grad = row_dot(cotangent, down_full_t)
+    unused_value, gelu_pull = jax.vjp(partial(jax.nn.gelu, approximate=False), hidden)
+    hidden_grad = gelu_pull(active_grad)[0].astype(jnp.bfloat16)
+    normed_two_grad = transposed_dot(hidden_grad, up_full)
+    unused_norm, norm_two_pull = jax.vjp(layer_norm, middle, gain_two, shift_two)
+    middle_grad, grad_gain_two, grad_shift_two = norm_two_pull(normed_two_grad)
+    middle_grad = middle_grad + cotangent.astype(jnp.float32)
+    branch_grad = middle_grad.astype(jnp.bfloat16)
+    attended_grad = transposed_dot(branch_grad, out_full).astype(jnp.bfloat16)
+    split_down, unused_sums = block_grads(cotangent, active, True)
+    split_up, grad_bias_up = block_grads(normed_two, hidden_grad, False)
+    split_out, grad_bias_out = block_grads(attended, branch_grad, False)
+    projected_grad, mine_down, mine_up, mine_out = attend_back_scatter(
+        n_dp, n_fsdp, counts, projected, attended, attended_grad, log_totals,
+        (split_down, split_up, split_out), BACKWARD_PLAN, 3,
+    )
+    split_qkv, grad_bias_qkv = block_grads(normed, projected_grad, False)
+    normed_grad = sum(
+        transposed_dot(projected_grad[part], qkv_full[:, part * D : (part + 1) * D]) for part in range(3)
+    )
+    unused_first, norm_one_pull = jax.vjp(layer_norm, inputs, gain_one, shift_one)
+    input_rows_grad, grad_gain_one, grad_shift_one = norm_one_pull(normed_grad)
+    input_grad = (middle_grad + input_rows_grad).astype(jnp.bfloat16)
+    small_grad = jnp.concatenate(
+        [
+            grad_gain_one,
+            grad_shift_one,
+            grad_gain_two,
+            grad_shift_two,
+            grad_bias_qkv[0, 0],
+            grad_bias_qkv[2, 0],
+            grad_bias_out.reshape(-1),
+            grad_bias_down,
+            grad_bias_up.reshape(-1),
+        ]
+    )
+    devices = n_dp * n_fsdp
+    small_split = jnp.pad(small_grad.astype(jnp.bfloat16).reshape(devices, -1), ((0, 0), (0, 2048 - 9216 // devices)))
+    small_split = small_split.reshape(4, 2, 2, 2, 16, 128).transpose(2, 3, 0, 1, 4, 5)
+    mine_qkv, mine_small = scatter_all(n_dp, n_fsdp, (split_qkv, small_split), ("j", "j"), 4)
+    mine = jnp.concatenate([mine_qkv.astype(jnp.bfloat16), mine_out, mine_up, mine_down], axis=0)
+    numbers = jnp.arange(BLOCKS, dtype=jnp.int32)
+    ranks = jnp.arange(devices, dtype=jnp.int32)
+    blocks_of = jnp.sum(jnp.where(owners[None, :] == ranks[:, None], numbers[None, :], 0), axis=1).astype(jnp.int32)
+    gathered, small_pieces, *grad_tiles = to_owners(
+        n_dp, n_fsdp, blocks_of, mine.reshape(BLOCKS, 48, 384), mine_small, 5
+    )
+    rank = lax.axis_index(("dp", "fsdp"))
+    owning = jnp.any(owners == rank)
+    flags = jnp.stack([owning, blocks_of[rank] >= 4 + FF // D]).astype(jnp.int32)
+    new_statistics, steps = precondition(flags, gathered, statistics[0], inverse_roots[0])
+    step_tiles = to_tiles(n_dp, n_fsdp, owners, steps, 6)
+    column_index = lax.axis_index("fsdp")
+    shard_qkv, shard_out, shard_up, shard_down = tiles_of(grad_tiles, column_index)
+    tile_qkv, tile_out, tile_up, tile_down = tiles_of(step_tiles, column_index)
+    new_qkv = qkv_weight - step_rate * tile_qkv
+    new_out = out_weight - step_rate * tile_out
+    new_up = up_weight - step_rate * tile_up
+    new_down = down_weight - step_rate * tile_down
+    whole_small = small_pieces.reshape(devices, 2048)[:, : 9216 // devices].reshape(-1)
+    new_small = small_params - small_rate * whole_small * lax.rsqrt(
+        jnp.mean(whole_small * whole_small) + 1e-06
+    )
+    return (
+        layer_rows,
+        input_grad,
+        shard_qkv,
+        shard_out,
+        shard_up,
+        shard_down,
+        whole_small,
+        new_statistics[None],
+        new_qkv,
+        new_out,
+        new_up,
+        new_down,
+        new_small,
+    )
+
+
+def whole_of(pieces):
+    rows, columns = pieces.shape[-2:]
+    folded = pieces.reshape(pieces.shape[0] * pieces.shape[1], -1, columns)
+    return folded.transpose(1, 0, 2).reshape(folded.shape[1], -1)
+
+
+def tiles_of(tiles, column_index):
+    qkv, out, up, down = tiles
+    band = lambda halves: halves.astype(jnp.float32).transpose(1, 0, 2).reshape(96, D)
+    qkv, out = band(qkv), band(out)
+    qkv = jnp.where(column_index % 2 == 1, qkv[:, 192:], qkv[:, : D - 192])
+    out = lax.dynamic_slice_in_dim(out, column_index * 192, 192, 1)
+    return qkv, out, band(up), down.astype(jnp.float32).T
+
+
 def solution(mesh):
     placed = (
         P(("dp", "fsdp"), None),
@@ -452,6 +1445,8 @@
         P(("dp", "fsdp"), None, None, None),
         P(),
     )
+    sizes = (mesh.shape["dp"], mesh.shape["fsdp"])
+    local = partial(local_staged, sizes) if sizes == (8, 4) else local_any
     return jax.shard_map(
         local,
         mesh=mesh,

time: 1520 us -> 521 us (0.34)
  waiting for transfers between devices: 792 us -> 0 us
  Pallas kernels: 0 us -> 350 us
  matrix products: 289 us -> 89.2 us
  blocking collectives: 161 us -> 0 us
  other arithmetic: 132 us -> 35.8 us
  local copies, waits for them, and re-layouts: 92.9 us -> 37.3 us
  between operations: 26.8 us -> 3.58 us
    pallas_call x0 -> x11, Pallas kernels: none -> 350 us  [the longest x1 83.1 us: attend_back_scatter(): pl.pallas_call(kernel, out_shape=[jax.ShapeDtypeStruct((3, slots, d), jnp...]
    all_gather x8 -> x0, waiting for transfers between devices: 338 us -> none  [the longest x1 74.7 us: local(): lax.all_gather(band_up.astype(jnp.bfloat16), 'dp', axis=0, tiled=True)]
    reduce_scatter x5 -> x0, waiting for transfers between devices: 264 us -> none  [the longest x1 98.8 us: local(): lax.psum_scatter(grad_down.astype(jnp.bfloat16), 'dp', scatter_dimension=...]
    dot_general x18 -> x0, matrix products: 191 us -> none  [the longest x4 41 us: one_block(): jnp.einsum('hdq,hdk->hqk', query_block, key_rows, preferred_element_type=...]
    psum x1 -> x0, waiting for transfers between devices: 134 us -> none  [broadcast(): return lax.psum(kept, axis)]
    all_gather x9 -> x0, blocking collectives: 85.1 us -> none  [the longest x1 24.6 us: local(): lax.all_gather(band_small.astype(jnp.bfloat16), 'dp', axis=0, tiled=True)]
    unnamed x3 -> x0, blocking collectives: 75.4 us -> none
    convert_element_type x20 -> x9, other arithmetic: 77.7 us -> 11.6 us  [the longest x1 4.6 us: local_staged(): input_grad = (middle_grad + input_rows_grad).astype(jnp.bfloat16)]
  transfers between devices with their start and end apart: 17 -> 0, of which waited for: 15 -> 0; matrix products, arithmetic and copies ran while one was open for 28% -> 0% of each run, Pallas kernels for 0% -> 0%
where the time goes in v2:
time: 521 us; the launch traced here: 516 us
  Pallas kernels  350 us (67%)
  matrix products  89.2 us (17%)
  local copies, waits for them, and re-layouts  37.3 us (7%)
  other arithmetic  35.8 us (7%)
    pallas_call x1, Pallas kernels, attend_back_scatter(): pl.pallas_call(kernel, out_shape=[jax.ShapeDtypeStruct((3, slots, d), jnp...  83.1 us
    pallas_call x1, Pallas kernels, attend_gather(): pl.pallas_call(kernel, out_shape=[jax.ShapeDtypeStruct((slots, d), jnp.bf...  71.6 us
    dot_general x4, matrix products, row_dot(): return jnp.dot(left, right, preferred_element_type=jnp.float32)  63 us
    pallas_call x1, Pallas kernels, to_tiles(): pl.pallas_call(kernel, out_shape=TILES, in_specs=[pl.BlockSpec(memory_spa...  42.9 us
    pallas_call x1, Pallas kernels, to_owners(): pl.pallas_call(kernel, out_shape=[jax.ShapeDtypeStruct((count,) + PIECE,...  42.9 us
    pallas_call x1, Pallas kernels, gather_all(): pl.pallas_call(kernel, out_shape=[jax.ShapeDtypeStruct(grid.shape(o, *s.s...  36.4 us
    pallas_call x4, Pallas kernels, block_grads(): pl.pallas_call(partial(block_grads_kernel, turned_blocks), out_shape=[jax...  32 us
    pallas_call x1, Pallas kernels, scatter_all(): pl.pallas_call(kernel, out_shape=[jax.ShapeDtypeStruct(s, dtype) for s in...  30.3 us

profile of v2, /device:TPU:27, one launch (start us, length us, event | category | flops | bytes accessed | tf_op | source)
XLA Modules:
  0.0 516.3 jit_solution(10481848412898389461)
XLA Ops:
  8.0 36.4 %gather_all.1 = bf16[2,2,4,2,96,576]{5,4,3,2,1,0:T(8,128)(2,1)} custom-call(bf16[96,576]{1,0:T(8,128)(2,1)} %convert_element_type.69.refs_0_), custom_call_target="tpu_custom_call" | custom-call | tf_op jit(solution)/shard_map/gather_all/pallas_call | solution.py:298
  44.5 6.7 %copy.39 = bf16[4,768,576]{1,2,0:T(8,128)(2,1)} copy(bf16[4,768,576]{2,1,0:T(8,128)(2,1)} %bitcast.106) | data formatting | bytes 7077888 | tf_op jit(solution)/shard_map/reshape | solution.py:1421
  51.2 7.6 %add_convert_fusion.q_ref.k_ref.v_ref = bf16[1024,2304]{1,0:T(8,128)(2,1)} fusion(bf16[1024,768]{1,0:T(8,128)(2,1)S(1)} %fusion.20.left, bf16[768,2304]{0,1:T(8,128)(2,1)} %bitcast.107, f32[2304]{0:T(1024)S(1)} %pad_maximum_fusion.1), kind=kOutput, calls=%fused_computation.25 | convolution fusion | flops 3628597248 | bytes 9839616 | tf_op jit(solution)/shard_map/dot_general | solution.py:889
  61.4 71.6 %attend_gather.1 = (bf16[1024,768]{1,0:T(8,128)(2,1)}, f32[6,2,1024]{2,1,0:T(2,128)}, bf16[2,2,4,2,96,192]{5,4,3,2,1,0:T(8,128)(2,1)}, bf16[2,2,4,2,96,768]{5,4,...) custom-call(s32[1]{0:T(128)S(6)} %copy.75.count_ref, bf16[1024,2304]{1,0:T(8,128)(2,1)} %add_convert_fusion.q_ref.k_ref.v_ref, ...), custom_call_target="tpu_custom_call" | custom-call | tf_op jit(solution)/shard_map/attend_gather/pallas_call | solution.py:528
  134.7 3.4 fusion.44
  139.8 7.2 %copy.42 = bf16[4,768,768]{1,2,0:T(8,128)(2,1)} copy(bf16[4,768,768]{2,1,0:T(8,128)(2,1)} %bitcast.116) | data formatting | bytes 9437184 | tf_op jit(solution)/shard_map/reshape | solution.py:1421
  147.7 36.0 %multiply_convert_fusion = (bf16[1024,3072]{1,0:T(8,128)(2,1)}, f32[1024,3072]{1,0:T(8,128)}, f32[1024,3072]{1,0:T(8,128)}) fusion(f32[3072]{0:T(1024)S(1)} %slice.75, bf16[1024,768]{1,0:T(8,128)(2,1)S(1)} %add_convert_fusion.3.left, bf16[768,3072]{0,1:T(8,128)(2,1)} %bitcast.117), kind=kOutput, calls=%fused_computation.11 | convolution fusion | flops 5039456256 | bytes 37761024 | tf_op jit(solution)/shard_map/dot_general | solution.py:889
  183.7 6.8 %copy.43 = bf16[8,768,384]{1,2,0:T(8,128)(2,1)} copy(bf16[8,768,384]{2,1,0:T(8,128)(2,1)} %bitcast.115) | data formatting | bytes 9437184 | tf_op jit(solution)/shard_map/reshape | solution.py:1421
  190.5 16.1 %fusion.6.right = bf16[1024,3072]{1,0:T(8,128)(2,1)} fusion(f32[1024,3072]{1,0:T(8,128)} %get-tuple-element.85, f32[1024,3072]{1,0:T(8,128)} %get-tuple-element.98, f32[3072]{0:T(1024)S(1)} %slice.75, bf16[768,3072]{0,1:T(8,128)(2,1)} %bitcast.113, bf16[1024,768]{1,0:T(8,128)(2,1)S(1)} %copy-done.7), kind=kOutput, calls=%fused_computation.9 | convolution fusion | flops 4879024128 | bytes 37761024 | tf_op jit(solution)/shard_map/dot_general | solution.py:889
  206.7 7.7 %multiply_reduce_fusion = (bf16[768]{0:T(1024)(128)(2,1)S(1)}, f32[1024]{0:T(1024)S(1)}, bf16[768]{0:T(1024)(128)(2,1)S(1)}, f32[1024,768]{1,0:T(8,128)S(1)}) fusion(f32[1024,768]{1,0:T(8,128)S(1)} %copy-done.3, f32[1024]{0:T(1024)S(1)} %copy-done.39, f32[1024]{0:T(1024)S(1)} %copy-done.35, f32[768]{0:T(1024)S(1)} %copy-done.37, ...), kind=kOutput, calls=%fused_computation.42 | convolution fusion | flops 4838126592 | bytes 17319936 | tf_op jit(solution)/shard_map/dot_general | solution.py:899
  219.5 4.4 block_grads.6
  223.9 9.8 %block_grads.5 = (bf16[2,2,4,2,192,384]{5,4,3,2,1,0:T(8,128)(2,1)}, f32[4,1,768]{2,1,0:T(1,128)}) custom-call(bf16[1024,768]{1,0:T(8,128)(2,1)} %copy-done.13, bf16[1024,3072]{1,0:T(8,128)(2,1)} %fusion.6.right), custom_call_target="tpu_custom_call" | custom-call | tf_op jit(solution)/shard_map/block_grads/pallas_call | solution.py:844
  233.7 2.5 convolution_convert_fusion.do_ref
  236.2 9.6 %block_grads.4 = (bf16[2,2,4,2,192,384]{5,4,3,2,1,0:T(8,128)(2,1)}, f32[4,1,768]{2,1,0:T(1,128)}) custom-call(bf16[1024,768]{1,0:T(8,128)(2,1)} %left.1, bf16[1024,3072]{1,0:T(8,128)(2,1)} %get-tuple-element.84.right), custom_call_target="tpu_custom_call" | custom-call | tf_op jit(solution)/shard_map/block_grads/pallas_call | solution.py:844
  245.8 83.1 %attend_back_scatter.1 = (bf16[3,1024,768]{2,1,0:T(8,128)(2,1)}, bf16[192,384]{1,0:T(8,128)(2,1)}, bf16[192,384]{1,0:T(8,128)(2,1)}, bf16[48,384]{1,0:T(8,128)(2,1)}) custom-call(s32[1]{0:T(128)S(6)} %copy.75.count_ref, bf16[1024,2304]{1,0:T(8,128)(2,1)} %add_convert_fusion.q_ref.k_ref.v_ref, bf16[1024,2304]{1,0:T(8,128)(2,1)} %add_convert_fusion.q_ref.k_ref.v_ref, ...), custom_call_target="tpu_custom_call" | custom-call | tf_op jit(solution)/shard_map/attend_back_scatter/pallas_call | solution.py:606
  329.0 3.3 fusion.26
  338.2 2.2 fusion.21
  341.1 8.2 %block_grads.7 = (bf16[2,2,4,2,144,384]{5,4,3,2,1,0:T(8,128)(2,1)}, f32[3,1,768]{2,1,0:T(1,128)}) custom-call(bf16[1024,768]{1,0:T(8,128)(2,1)} %copy-done.11, bf16[3,1024,768]{2,1,0:T(8,128)(2,1)} %get-tuple-element.51.right), custom_call_target="tpu_custom_call" | custom-call | tf_op jit(solution)/shard_map/block_grads/pallas_call | solution.py:844
  352.2 30.3 %scatter_all.1 = (f32[144,384]{1,0:T(8,128)}, f32[16,128]{1,0:T(8,128)}) custom-call(bf16[2,2,4,2,144,384]{5,4,3,2,1,0:T(8,128)(2,1)} %get-tuple-element.52.refs_0_, bf16[2,2,4,2,16,128]{5,4,3,2,1,0:T(8,128)(2,1)} %bitcast.126), custom_call_target="tpu_custom_call" | custom-call | tf_op jit(solution)/shard_map/scatter_all/pallas_call | solution.py:342
  385.6 42.9 %to_owners.1 = (bf16[32,48,384]{2,1,0:T(8,128)(2,1)}, f32[32,16,128]{2,1,0:T(8,128)}, bf16[2,96,384]{2,1,0:T(8,128)(2,1)}, bf16[2,96,384]{2,1,0:T(8,128)(2,1)}, ...) custom-call(s32[32]{0:T(128)} %select_reduce_fusion.of_ref, bf16[12,48,384]{2,1,0:T(8,128)(2,1)} %bitcast.121, ...), custom_call_target="tpu_custom_call" | custom-call | tf_op jit(solution)/shard_map/to_owners/pallas_call | solution.py:721
  435.4 11.3 %precondition.1 = (f32[2,768,768]{2,1,0:T(8,128)}, bf16[32,48,384]{2,1,0:T(8,128)(2,1)}) custom-call(s32[2]{0:T(128)} %add_convert_fusion.4.flags, bf16[32,48,384]{2,1,0:T(8,128)(2,1)} %get-tuple-element.66.pieces, f32[2,768,768]{2,1,0:T(8,128)} %bitcast.111, f32[2,768,768]{2,1,0:T(8,128)} %bitcast.112), custom_call_target="tpu_custom_call" | custom-call | tf_op jit(solution)/shard_map/precondition/pallas_call | solution.py:812
  446.7 42.9 %to_tiles.1 = (bf16[2,96,384]{2,1,0:T(8,128)(2,1)}, bf16[2,96,384]{2,1,0:T(8,128)(2,1)}, bf16[2,96,384]{2,1,0:T(8,128)(2,1)}, bf16[192,384]{1,0:T(8,128)(2,1)}) custom-call(s32[12]{0:T(128)} %owners_ref.1, bf16[32,48,384]{2,1,0:T(8,128)(2,1)} %get-tuple-element.68.pieces_ref), custom_call_target="tpu_custom_call" | custom-call | tf_op jit(solution)/shard_map/to_tiles/pallas_call | solution.py:758
  502.0 4.6 add_convert_fusion.1
  506.7 9.4 %add_convert_fusion.2 = bf16[1024,768]{1,0:T(8,128)(2,1)} fusion(f32[1024,768]{1,0:T(8,128)S(1)} %copy-done.4, bf16[1024,3072]{1,0:T(8,128)(2,1)} %get-tuple-element.84.right, bf16[768,3072]{0,1:T(8,128)(2,1)} %bitcast.114, f32[768]{0:T(1024)S(1)} %copy-done.48), kind=kOutput, calls=%fused_computation.47 | convolution fusion | flops 4834197504 | bytes 15731712 | tf_op jit(solution)/shard_map/dot_general | solution.py:899
  (176 shorter events, 48.8 us)
Async XLA Ops:
  2.2 136.5 %copy-start.36 = (f32[768]{0:T(1024)}, f32[768]{0:T(1024)S(1)}, u32[]{:S(2)}) copy-start(f32[768]{0:T(1024)S(1)} %get-tuple-element.90) | copy-start | bytes 9220
  7.2 44.0 %copy-start.11 = (bf16[1024,768]{1,0:T(8,128)(2,1)}, bf16[1024,768]{1,0:T(8,128)(2,1)S(1)}, u32[]{:S(2)}) copy-start(bf16[1024,768]{1,0:T(8,128)(2,1)S(1)} %fusion.20.left) | copy-start | bytes 4718596
  51.2 8.9 %copy-start.15 = (f32[96,768]{1,0:T(8,128)S(1)}, f32[96,768]{1,0:T(8,128)}, u32[]{:S(2)}) copy-start(f32[96,768]{1,0:T(8,128)} %param.16) | copy-start | bytes 884740
  51.2 9.6 %copy-start.21 = (f32[96,192]{1,0:T(8,128)S(1)}, f32[96,192]{1,0:T(8,128)}, u32[]{:S(2)}) copy-start(f32[96,192]{1,0:T(8,128)} %param.15) | copy-start | bytes 221188
  138.7 8.3 %copy-start.42 = (f32[1024]{0:T(1024)}, f32[1024]{0:T(1024)S(1)}, u32[]{:S(2)}) copy-start(f32[1024]{0:T(1024)S(1)} %multiply_reduce_fusion.2) | copy-start | bytes 12292
  190.5 16.2 %copy-start.3 = (f32[1024,768]{1,0:T(8,128)S(1)}, f32[1024,768]{1,0:T(8,128)}, u32[]{:S(2)}) copy-start(f32[1024,768]{1,0:T(8,128)} %copy-done.2) | copy-start | bytes 9437188
  190.5 16.2 %copy-start.14 = (bf16[4,768,768]{1,2,0:T(8,128)(2,1)S(1)}, bf16[4,768,768]{1,2,0:T(8,128)(2,1)}, u32[]{:S(2)}) copy-start(bf16[4,768,768]{1,2,0:T(8,128)(2,1)} %copy.42) | copy-start | bytes 14155780
  190.5 16.2 %copy-start.35 = (f32[1024]{0:T(1024)S(1)}, f32[1024]{0:T(1024)}, u32[]{:S(2)}) copy-start(f32[1024]{0:T(1024)} %copy-done.34) | copy-start | bytes 12292
  190.5 16.2 %copy-start.37 = (f32[768]{0:T(1024)S(1)}, f32[768]{0:T(1024)}, u32[]{:S(2)}) copy-start(f32[768]{0:T(1024)} %copy-done.36) | copy-start | bytes 9220
  190.5 16.2 %copy-start.39 = (f32[1024]{0:T(1024)S(1)}, f32[1024]{0:T(1024)}, u32[]{:S(2)}) copy-start(f32[1024]{0:T(1024)} %copy-done.38) | copy-start | bytes 12292
  223.9 9.8 %copy-start.12 = (bf16[1024,768]{1,0:T(8,128)(2,1)S(1)}, bf16[1024,768]{1,0:T(8,128)(2,1)}, u32[]{:S(2)}) copy-start(bf16[1024,768]{1,0:T(8,128)(2,1)} %fusion.24.right) | copy-start | bytes 4718596
  223.9 9.8 %copy-start.19 = (bf16[4,768,192]{1,2,0:T(8,128)(2,1)S(1)}, bf16[4,768,192]{1,2,0:T(8,128)(2,1)}, u32[]{:S(2)}) copy-start(bf16[4,768,192]{1,2,0:T(8,128)(2,1)} %copy-done.18) | copy-start | bytes 3538948
  341.1 9.4 %copy-start.49 = (f32[1,1,768]{2,1,0:T(1,128)S(1)}, f32[1,1,768]{2,1,0:T(1,128)}, u32[]{:S(2)}) copy-start(f32[1,1,768]{2,1,0:T(1,128)} %get-tuple-element.54) | copy-start | bytes 9220
  341.1 9.6 %copy-start.8 = (bf16[1024,768]{1,0:T(8,128)(2,1)S(1)}, bf16[1024,768]{1,0:T(8,128)(2,1)}, u32[]{:S(2)}) copy-start(bf16[1024,768]{1,0:T(8,128)(2,1)} %left.1) | copy-start | bytes 4718596
  341.1 10.1 %copy-start.47 = (f32[4,1,768]{2,1,0:T(1,128)S(1)}, f32[4,1,768]{2,1,0:T(1,128)}, u32[]{:S(2)}) copy-start(f32[4,1,768]{2,1,0:T(1,128)} %get-tuple-element.55) | copy-start | bytes 36868
  350.7 32.7 %copy-start.27 = (bf16[192,384]{1,0:T(8,128)(2,1)S(1)}, bf16[192,384]{1,0:T(8,128)(2,1)}, u32[]{:S(2)}) copy-start(bf16[192,384]{1,0:T(8,128)(2,1)} %get-tuple-element.59) | copy-start | bytes 442372
  350.7 32.7 %copy-start.28 = (bf16[192,384]{1,0:T(8,128)(2,1)S(1)}, bf16[192,384]{1,0:T(8,128)(2,1)}, u32[]{:S(2)}) copy-start(bf16[192,384]{1,0:T(8,128)(2,1)} %get-tuple-element.58) | copy-start | bytes 442372
  351.0 34.0 %copy-start.50 = (s32[12]{0:T(128)S(1)}, s32[12]{0:T(128)}, u32[]{:S(2)}) copy-start(s32[12]{0:T(128)} %owners_ref.1) | copy-start | bytes 148
  351.5 79.5 %copy-start.23 = (f32[9216]{0:T(1024)S(1)}, f32[9216]{0:T(1024)}, u32[]{:S(2)}) copy-start(f32[9216]{0:T(1024)} %param.18) | copy-start | bytes 110596
  352.2 81.3 %copy-start.51 = (s32[12]{0:T(128)S(1)}, s32[12]{0:T(128)}, u32[]{:S(2)}) copy-start(s32[12]{0:T(128)} %owners_ref.1) | copy-start | bytes 148
  435.4 55.3 %copy-start.16 = (f32[96,768]{1,0:T(8,128)S(1)}, f32[96,768]{1,0:T(8,128)}, u32[]{:S(2)}) copy-start(f32[96,768]{1,0:T(8,128)} %param.16) | copy-start | bytes 884740
  446.7 44.8 %copy-start.22 = (f32[96,192]{1,0:T(8,128)S(1)}, f32[96,192]{1,0:T(8,128)}, u32[]{:S(2)}) copy-start(f32[96,192]{1,0:T(8,128)} %param.15) | copy-start | bytes 221188
  493.2 8.8 %copy-start.46 = (f32[1024]{0:T(1024)S(1)}, f32[1024]{0:T(1024)}, u32[]{:S(2)}) copy-start(f32[1024]{0:T(1024)} %get-tuple-element.76) | copy-start | bytes 12292
  493.2 8.8 %copy-start.45 = (f32[1024]{0:T(1024)S(1)}, f32[1024]{0:T(1024)}, u32[]{:S(2)}) copy-start(f32[1024]{0:T(1024)} %copy-done.44) | copy-start | bytes 12292
  (28 other events, 107.9 us)

commit v3 on v2

--- a/solution.py
+++ b/solution.py
@@ -84,17 +84,49 @@
         copy.wait_send()
 
 
+class Copies:
+    def __init__(self, send, recv):
+        self.send, self.recv, self.slot = send, recv, 0
+
+    def add(self, group, describe):
+        group.append((self.slot, describe))
+        self.slot += 1
+
+    def made(self, group):
+        out = []
+        for slot, describe in group:
+            start, end, device = describe()
+            out.append(remote(start, end, self.send, self.recv, slot, device))
+        return out
+
+    def start(self, group):
+        start_all(self.made(group))
+
+    def arrived(self, group):
+        arrived(self.made(group))
+
+    def sent(self, group):
+        sent(self.made(group))
+
+
 class Gather:
     def __init__(self, g, order, path, rows, src, out, local, send, recv):
         size = {"z": g.Z, "a": g.A, "b": g.B}
-        place = {"z": g.z, "a": g.a, "b": g.b}
+        self.copies = Copies(send, recv)
+
+        def at(name, shift):
+            place = {"z": g.z, "a": g.a, "b": g.b}[name]
+            return (place + shift + size[name]) % size[name] if shift else place
 
         def piece(cell):
-            x, y = g.xy(cell["a"], cell["b"], g.c)
-            return g.at(out, order, y, g.c, cell["z"], x).at[..., rows, :]
+            where = {name: (at(name, value[1]) if isinstance(value, tuple) else value) for name, value in cell.items()}
+            x, y = g.xy(where["a"], where["b"], g.c)
+            return g.at(out, order, y, g.c, where["z"], x).at[..., rows, :]
+
+        own_cell = {"z": ("own", 0), "a": ("own", 0), "b": ("own", 0)}
 
         def cells(full):
-            out = [dict(place)]
+            out = [dict(own_cell)]
             for axis in full:
                 if axis == "z":
                     out = [dict(cell, z=slice(None)) for cell in out]
@@ -102,28 +134,29 @@
                     out = [dict(cell, **{axis: n}) for cell in out for n in range(size[axis])]
             return out
 
-        near = {"dp": g.z * g.X + g.x, "fsdp": g.y * 2 + 1 - g.c}
-        self.slot = 0
-
-        def copy(start, end, device):
-            self.slot += 1
-            return remote(start, end, send, recv, self.slot - 1, device)
-
-        own = src.at[rows, :]
-        self.own = pltpu.make_async_copy(own, piece(place), local)
-        self.stages, self.near = [], [[copy(own, piece(place), near)]]
+        def near():
+            return {"dp": g.z * g.X + g.x, "fsdp": g.y * 2 + 1 - g.c}
+
+        def far(axis, k):
+            return g.device(*[at(name, k if name == axis else 0) for name in "zab"], g.c)
+
+        def own():
+            return src.at[rows, :]
+
+        self.own = lambda: pltpu.make_async_copy(own(), piece(own_cell), local)
+        self.stages, self.near = [], [[]]
+        self.copies.add(self.near[0], lambda: (own(), piece(own_cell), near()))
         full = ""
         for axis in path:
-            out_copies, near_copies = [], []
+            self.stages.append([])
+            self.near.append([])
             for cell in cells(full):
-                start = piece(cell) if full else own
                 for k in range(1, size[axis]):
-                    to = dict(place, **{axis: (place[axis] + k) % size[axis]})
-                    out_copies.append(copy(start, piece(cell), g.device(to["z"], to["a"], to["b"], g.c)))
-                    came = piece(dict(cell, **{axis: (place[axis] - k + size[axis]) % size[axis]}))
-                    near_copies.append(copy(came, came, near))
-            self.stages.append(out_copies)
-            self.near.append(near_copies)
+                    from_src = not full
+                    self.copies.add(self.stages[-1], lambda cell=cell, k=k, axis=axis, from_src=from_src: (
+                        own() if from_src else piece(cell), piece(cell), far(axis, k)))
+                    came = dict(cell, **{axis: ("own", -k)})
+                    self.copies.add(self.near[-1], lambda came=came: (piece(came), piece(came), near()))
             full += axis
 
     @staticmethod
@@ -134,57 +167,65 @@
 
     def step(self, number):
         if number == 0:
-            self.own.start()
+            self.own().start()
         else:
             if number == 1:
-                self.own.wait()
-            arrived(self.stages[number - 1])
-        start_all(self.near[number])
+                self.own().wait()
+            self.copies.arrived(self.stages[number - 1])
         if number < 3:
-            start_all(self.stages[number])
-
-    def finish(self):
-        for group in self.near:
-            arrived(group)
-        for group in self.near + self.stages:
-            sent(group)
+            self.copies.start(self.stages[number])
+        self.copies.start(self.near[number])
+
+    def pause(self):
+        self.own().wait()
+        for group in (self.stages[0], self.near[0]):
+            self.copies.arrived(group)
+            self.copies.sent(group)
+
+    def resume(self):
+        self.copies.start(self.stages[1])
+        self.copies.start(self.near[1])
+
+    def finish(self, first=0):
+        for group in self.near[first:]:
+            self.copies.arrived(group)
+        for group in self.near[first:] + self.stages[first:]:
+            self.copies.sent(group)
 
 
 class Scatter:
-    def __init__(self, g, order, path, rows, src, bufs, local, send, recv):
-        self.g, self.path, self.count = g, path, rows.size
-        self.work, self.mine = bufs[0], bufs[1]
-        self.recv = dict(zip(path, bufs[2:]))
-        work, other = self.work, 1 - g.c
+    def __init__(self, g, order, path, rows, src, bufs, send, recv):
+        self.g, self.path, self.order, self.rows, self.src = g, path, order, rows, src
+        self.work = bufs[0]
+        self.recv = dict(zip(path, bufs[1:]))
+        work = self.work
         size = {"z": g.Z, "a": g.A, "b": g.B}
-        place = {"z": g.z, "a": g.a, "b": g.b}
         self.size = size
-        self.slot = 0
-
-        def copy(start, end, device):
-            self.slot += 1
-            return remote(start, end, send, recv, self.slot - 1, device)
-
-        self.owns, near = [], []
+        self.copies = Copies(send, recv)
+        places = lambda: {"z": g.z, "a": g.a, "b": g.b}
+
+        def other(b, a):
+            x, y = g.xy(a, b, 1 - g.c)
+            return (g.at(src, order, y, 1 - g.c, slice(None), x).at[:, rows, :], work.at[b, :, a],
+                    {"dp": g.z * g.X + g.x, "fsdp": g.y * 2 + 1 - g.c})
+
+        def onward(axis, k, done):
+            place = places()
+            to = dict(place, **{axis: (place[axis] + k) % size[axis]})
+            where = {name: (place[name] if name in done else slice(None)) for name in "bza"}
+            where[axis] = to[axis]
+            return (work.at[where["b"], where["z"], where["a"]], self.recv[axis].at[k - 1],
+                    g.device(to["z"], to["a"], to["b"], g.c))
+
+        self.stages = [[]]
         for b in range(g.B):
             for a in range(g.A):
-                x, y = g.xy(a, b, other)
-                near.append(copy(g.at(src, order, y, other, slice(None), x).at[:, rows, :], work.at[b, :, a],
-                                 {"dp": g.z * g.X + g.x, "fsdp": g.y * 2 + other}))
-                x, y = g.xy(a, b, g.c)
-                self.owns.append(pltpu.make_async_copy(g.at(src, order, y, g.c, slice(None), x).at[:, rows, :],
-                                                       self.mine.at[b, :, a], local.at[b * g.A + a]))
-        self.stages = [near]
+                self.copies.add(self.stages[0], partial(other, b, a))
         done = ""
         for axis in path:
-            copies = []
+            self.stages.append([])
             for k in range(1, size[axis]):
-                to = dict(place, **{axis: (place[axis] + k) % size[axis]})
-                where = {name: (place[name] if name in done else slice(None)) for name in "bza"}
-                where[axis] = to[axis]
-                copies.append(copy(work.at[where["b"], where["z"], where["a"]], self.recv[axis].at[k - 1],
-                                   g.device(to["z"], to["a"], to["b"], g.c)))
-            self.stages.append(copies)
+                self.copies.add(self.stages[-1], partial(onward, axis, k, done))
             done += axis
 
     @staticmethod
@@ -194,7 +235,7 @@
     @staticmethod
     def scratch(g, path, r, w):
         size = {"z": g.Z, "a": g.A, "b": g.B}
-        out = [pltpu.VMEM((g.B, g.Z, g.A, r, w), jnp.bfloat16)] * 2
+        out = [pltpu.VMEM((g.B, g.Z, g.A, r, w), jnp.bfloat16)]
         done = ""
         for axis in path:
             done += axis
@@ -219,7 +260,9 @@
                 n = n // self.size[name]
             b, z, a = self._cell(index, done)
             if number == 0:
-                summed = self.work[b, z, a].astype(jnp.float32) + self.mine[b, z, a].astype(jnp.float32)
+                x, y = g.xy(a, b, g.c)
+                mine = g.at(self.src, self.order, y, g.c, z, x)[self.rows, :]
+                summed = self.work[b, z, a].astype(jnp.float32) + mine.astype(jnp.float32)
             else:
                 summed = self._sum(number, b, z, a, [index[name] for name in left])
             self.work[b, z, a] = summed.astype(jnp.bfloat16)
@@ -235,38 +278,32 @@
         return summed
 
     def step(self, number):
-        if number == 0:
-            start_all(self.stages[0] + self.owns)
-            return
-        if number == 1:
-            for copy in self.owns:
-                copy.wait()
-        arrived(self.stages[number - 1])
-        self._add(number - 1)
-        start_all(self.stages[number])
+        if number > 0:
+            self.copies.arrived(self.stages[number - 1])
+            self._add(number - 1)
+        self.copies.start(self.stages[number])
 
     def total(self):
-        arrived(self.stages[3])
+        self.copies.arrived(self.stages[3])
         return self._sum(3, self.g.b, self.g.z, self.g.a, [])
 
     def finish(self):
         for group in self.stages:
-            sent(group)
+            self.copies.sent(group)
 
 
 GATHER_PATHS = ("zab", "abz")
 SCATTER_PATHS = ("baz", "zba")
 
 
-def row_parts(rows):
-    first = rows * 2 // 3 // 16 * 16
-    if first == 0 or first == rows:
-        return [(0, pl.ds(0, rows))]
-    return [(0, pl.ds(0, first)), (1, pl.ds(first, rows - first))]
-
-
-def job_list(sizes):
-    return [(n, path, rows) for n, (r, _) in enumerate(sizes) for path, rows in row_parts(r)]
+def row_parts(rows, share=0):
+    second = rows * share // 6 // 16 * 16
+    parts = [(0, pl.ds(0, rows - second))]
+    return parts + ([(1, pl.ds(rows - second, second))] if second else [])
+
+
+def job_list(sizes, share=0):
+    return [(n, path, rows) for n, (r, _) in enumerate(sizes) for path, rows in row_parts(r, share)]
 
 
 def rounds(jobs, last):
@@ -279,21 +316,30 @@
     return [dma((count,)), dma((count, lanes)), dma((count, lanes))]
 
 
-def gather_all(n_dp, n_fsdp, shards, orders, collective_id):
+def gather_jobs(g, orders, jobs, ins, outs, scratch):
+    local, send, recv = scratch
+    return [Gather(g, orders[n], GATHER_PATHS[path], rows, ins[n], outs[n], local.at[j], send.at[j], recv.at[j])
+            for j, (n, path, rows) in enumerate(jobs)]
+
+
+def gather_first(n_dp, n_fsdp, shards, orders, share, collective_id):
     grid = Grid(n_dp, n_fsdp)
     count = len(shards)
-    jobs = job_list([s.shape for s in shards])
+    jobs = job_list([shards[0].shape]) + [(n + 1, p, r) for n, p, r in job_list([s.shape for s in shards[1:]], share)]
 
     def kernel(*refs):
-        ins, outs, (local, send, recv) = refs[:count], refs[count : 2 * count], refs[2 * count :]
         g = grid.here()
         g.barrier()
-        work = [Gather(g, orders[n], GATHER_PATHS[path], rows, ins[n], outs[n], local.at[j], send.at[j], recv.at[j])
-                for j, (n, path, rows) in enumerate(jobs)]
-        for j, step in rounds(jobs, 3):
-            work[j].step(step)
-        for job in work:
-            job.finish()
+        whole, *others = gather_jobs(g, orders, jobs, refs[:count], refs[count : 2 * count], refs[2 * count :])
+        whole.step(0)
+        whole.step(1)
+        for job in others:
+            job.step(0)
+        whole.step(2)
+        whole.step(3)
+        for job in others:
+            job.pause()
+        whole.finish()
 
     return pl.pallas_call(
         kernel,
@@ -302,7 +348,7 @@
         out_specs=[ANY] * count,
         scratch_shapes=gather_scratch(grid, len(jobs)),
         compiler_params=pltpu.CompilerParams(collective_id=collective_id, has_side_effects=True),
-        name="gather_all",
+        name="gather_first",
     )(*shards)
 
 
@@ -312,20 +358,20 @@
         out += Scatter.scratch(g, SCATTER_PATHS[path], rows.size, sizes[n][1])
     dma = pltpu.SemaphoreType.DMA
     lanes = Scatter.slots(g)
-    return out + [dma((len(jobs), g.A * g.B)), dma((len(jobs), lanes)), dma((len(jobs), lanes))]
+    return out + [dma((len(jobs), lanes)), dma((len(jobs), lanes))]
 
 
 def scatter_jobs(g, orders, jobs, ins, scratch):
-    local, send, recv = scratch[5 * len(jobs) :]
-    return [Scatter(g, orders[n], SCATTER_PATHS[path], rows, ins[n], scratch[5 * j : 5 * j + 5], local.at[j], send.at[j],
-                    recv.at[j]) for j, (n, path, rows) in enumerate(jobs)]
+    send, recv = scratch[4 * len(jobs) :]
+    return [Scatter(g, orders[n], SCATTER_PATHS[path], rows, ins[n], scratch[4 * j : 4 * j + 4], send.at[j], recv.at[j])
+            for j, (n, path, rows) in enumerate(jobs)]
 
 
 def scatter_all(n_dp, n_fsdp, wholes, orders, collective_id, dtype=jnp.float32):
     grid = Grid(n_dp, n_fsdp)
     count = len(wholes)
     sizes = [w.shape[-2:] for w in wholes]
-    jobs = job_list(sizes)
+    jobs = job_list(sizes, 2)
 
     def kernel(*refs):
         ins, outs, scratch = refs[:count], refs[count : 2 * count], refs[2 * count :]
@@ -342,7 +388,7 @@
     return pl.pallas_call(
         kernel,
         out_shape=[jax.ShapeDtypeStruct(s, dtype) for s in sizes],
-        in_specs=[ANY] * count,
+        in_specs=[VM] * count,
         out_specs=[VM] * count,
         scratch_shapes=scatter_scratch(grid, sizes, jobs),
         compiler_params=pltpu.CompilerParams(collective_id=collective_id, has_side_effects=True,
@@ -455,7 +501,7 @@
     key_index = lax.broadcasted_iota(jnp.int32, (slots, size), 0)
 
     def step(n, carry):
-        rows = pl.ds(pl.multiple_of(n * size, size), size)
+        rows = pl.ds(n * size, size)
         keys, values = k_ref[...], v_ref[...]
         dq = jnp.zeros((PAIR, size), jnp.float32)
         for head in range(2):
@@ -471,65 +517,67 @@
         out_ref[0, rows, :] = dq.T.astype(jnp.bfloat16)
         return carry
 
-    steps = slots // size
-    for half in range(2):
-        hook(half)
-        lax.fori_loop(half * steps // 2, (half + 1) * steps // 2, step, 0)
+    for n in range(slots // size):
+        hook(n)
+        step(n, 0)
     out_ref[1] = dk_sum[...].astype(jnp.bfloat16)
     out_ref[2] = dv_sum[...].astype(jnp.bfloat16)
 
 
-def attend_gather(n_dp, n_fsdp, counts, projected, shards, orders, plan, collective_id, size=512):
+def attend_gather(n_dp, n_fsdp, counts, projected, pieces, fresh, orders, plan, collective_id, size=512):
     slots, width = projected.shape
     d = width // 3
     pairs = d // PAIR
     grid = Grid(n_dp, n_fsdp)
-    count = len(shards)
-    jobs = job_list([s.shape for s in shards])
+    begun, count = len(pieces), len(pieces) + len(fresh)
+    jobs = job_list([a.shape[-2:] for a in (*pieces, *fresh)])
+    shapes = [jax.ShapeDtypeStruct(p.shape, p.dtype) for p in pieces]
+    shapes += [jax.ShapeDtypeStruct(grid.shape(o, *a.shape), a.dtype) for a, o in zip(fresh, orders[begun:])]
     steps = slots // size
 
     def kernel(count_ref, q_ref, k_ref, v_ref, *refs):
-        ins, (o_ref, lse_ref), outs = refs[:count], refs[count : count + 2], refs[count + 2 : 2 * count + 2]
-        q_heads, v_turned, local, send, recv = refs[2 * count + 2 :]
+        (o_ref, lse_ref), outs = refs[count : count + 2], refs[count + 2 : 2 * count + 2]
+        q_heads, v_turned = refs[2 * count + 2 : 2 * count + 4]
         g = grid.here()
-        work = [Gather(g, orders[n], GATHER_PATHS[path], rows, ins[n], outs[n], local.at[j], send.at[j], recv.at[j])
-                for j, (n, path, rows) in enumerate(jobs)]
+        work = gather_jobs(g, orders, jobs, outs[:begun] + refs[begun:count], outs, refs[2 * count + 4 :])
         pair = pl.program_id(0)
 
         def run(when):
             for j, step in plan.get(when, []):
-                work[j].step(step)
-
-        for p in range(pairs):
-            if any(p * steps == when for when in plan):
-
-                @pl.when(pair == p)
-                def _():
-                    if p == 0:
-                        g.barrier()
-                    run(p * steps)
-
+                if step == 1 and j < begun:
+                    work[j].resume()
+                else:
+                    work[j].step(step)
+
+        @pl.when(pair == 0)
+        def _():
+            g.barrier()
+
+        def hook(n):
+            for p in range(pairs):
+                if (p, n) in plan:
+                    pl.when(pair == p)(partial(run, (p, n)))
+
+        hook(0)
         attend_prepare(q_ref, v_ref, q_heads, v_turned)
         length = count_ref[0]
         for n in range(steps):
-            for p in range(pairs):
-                if n > 0 and p * steps + n in plan:
-                    pl.when(pair == p)(partial(run, p * steps + n))
-
+            if n > 0:
+                hook(n)
             attend_block(length, n * size, size, q_heads, k_ref, v_turned, o_ref, lse_ref.at[0])
 
         @pl.when(pair == pairs - 1)
         def _():
             run("end")
-            for job in work:
-                job.finish()
+            for j, job in enumerate(work):
+                job.finish(1 if j < begun else 0)
 
     spec = lambda part: pl.BlockSpec((slots, PAIR), lambda p, n, part=part: (0, part * pairs + p))
     return pl.pallas_call(
         kernel,
         out_shape=[jax.ShapeDtypeStruct((slots, d), jnp.bfloat16),
                    jax.ShapeDtypeStruct((pairs, 2, slots), jnp.float32)]
-        + [jax.ShapeDtypeStruct(grid.shape(o, *s.shape), s.dtype) for s, o in zip(shards, orders)],
+        + shapes,
         grid_spec=pltpu.PrefetchScalarGridSpec(
             num_scalar_prefetch=1, grid=(pairs,),
             in_specs=[spec(0), spec(1), spec(2)] + [ANY] * count,
@@ -537,64 +585,89 @@
                        pl.BlockSpec((1, 2, slots), lambda p, n: (p, 0, 0))] + [ANY] * count,
             scratch_shapes=[pltpu.VMEM((2, slots, PAIR), jnp.bfloat16), pltpu.VMEM((2, PAIR, slots), jnp.bfloat16)]
             + gather_scratch(grid, len(jobs))),
+        input_output_aliases={4 + n: 2 + n for n in range(begun)},
         compiler_params=pltpu.CompilerParams(vmem_limit_bytes=56 * 1024 * 1024, collective_id=collective_id,
                                              has_side_effects=True),
         name="attend_gather",
-    )(counts, projected, projected, projected, *shards)
+    )(counts, projected, projected, projected, *pieces, *fresh)
 
 
 FORWARD_PLAN = {
-    0: [(0, 0), (1, 0), (2, 0), (3, 0)],
-    2: [(0, 1), (1, 1)],
-    3: [(0, 2), (1, 2), (4, 0), (5, 0)],
-    4: [(2, 1), (3, 1)],
-    5: [(0, 3), (1, 3)],
-    7: [(2, 2), (3, 2)],
-    8: [(4, 1), (5, 1)],
-    10: [(4, 2), (5, 2)],
-    11: [(2, 3), (3, 3)],
-    "end": [(4, 3), (5, 3)],
+    (0, 0): [(0, 1), (1, 1), (2, 0)],
+    (1, 0): [(0, 2)],
+    (2, 0): [(1, 2), (0, 3)],
+    (3, 0): [(2, 1)],
+    (4, 0): [(2, 2)],
+    "end": [(1, 3), (2, 3)],
 }
 
 
-def attend_back_scatter(n_dp, n_fsdp, counts, projected, attended, attended_grad, lse, wholes, plan, collective_id, size=256):
+def cut_block(grad, turned_blocks, out, rows):
+    for z, x, y, c in places():
+        row, column = piece_rows(turned_blocks, z, x, y, c)
+        out[y, c, z, x, rows, :] = grad[row : row + 48, column : column + 384]
+
+
+def grads_attend_back(n_dp, n_fsdp, counts, projected, attended, attended_grad, lse, cotangent, active, normed, hidden_grad,
+                      branch_grad, plan, collective_id, size=256):
     slots, width = projected.shape
     d = width // 3
     pairs = d // PAIR
+    panels = active.shape[1] // d
+    head = 2 * panels + 1
     grid = Grid(n_dp, n_fsdp)
-    count = len(wholes)
-    sizes = [w.shape[-2:] for w in wholes]
+    sizes = [(panels * 48, 384), (panels * 48, 384), (48, 384)]
     jobs = job_list(sizes)
-
-    def kernel(count_ref, q_ref, k_ref, v_ref, o_ref, do_ref, lse_ref, *refs):
-        ins, out_ref, outs = refs[:count], refs[count], refs[count + 1 : 2 * count + 1]
-        own, scratch = refs[2 * count + 1 : 2 * count + 7], refs[2 * count + 7 :]
+    steps = slots // size
+
+    def kernel(count_ref, q_ref, k_ref, v_ref, o_ref, do_ref, lse_ref, dy, z, h2, du, o_all, db, out_ref, *refs):
+        outs, sums, parts, left = refs[:3], refs[3:5], refs[5:8], refs[8]
+        own, scratch = refs[9:15], refs[15:]
         g = grid.here()
-        work = scatter_jobs(g, ["j"] * count, jobs, ins, scratch)
-        pair = pl.program_id(0)
+        work = scatter_jobs(g, ["j"] * 3, jobs, parts, scratch)
+        step = pl.program_id(0)
 
         def run(when):
-            for j, step in plan.get(when, []):
-                work[j].step(step)
-
-        for p in range(pairs):
-            for half in range(2):
-                if half == 0 and p * 2 in plan:
-
-                    @pl.when(pair == p)
-                    def _():
-                        if p == 0:
-                            g.barrier()
-                        run(p * 2)
-
-        def hook(half):
-            for p in range(pairs):
-                if half and p * 2 + half in plan:
-                    pl.when(pair == p)(partial(run, p * 2 + half))
-
-        attend_back_body(size, count_ref, q_ref, k_ref, v_ref, o_ref, do_ref, lse_ref, out_ref, *own, hook)
-
-        @pl.when(pair == pairs - 1)
+            for j, number in plan.get(when, []):
+                work[j].step(number)
+
+        @pl.when(step == 0)
+        def _():
+            g.barrier()
+
+        def turn(ref):
+            left[...] = ref[...].astype(jnp.float32).T.astype(jnp.bfloat16)
+
+        for first, ref in ((0, dy), (panels, h2), (2 * panels, o_all)):
+            pl.when(step == first)(partial(turn, ref))
+
+        def blocks(part, first, right, kind):
+            @pl.when((step >= first) & (step < first + (1 if part == 2 else panels)))
+            def _():
+                values = right[...]
+                grad = plain_dot(left[...], values).astype(jnp.bfloat16)
+                at = 0 if part == 2 else pl.multiple_of((step - first) * 48, 16)
+                cut_block(grad, kind, parts[part], pl.ds(at, 48))
+                if part > 0:
+                    sums[part - 1][...] = jnp.sum(values.astype(jnp.float32), axis=0).reshape(1, 1, d)
+
+        for when in range(head):
+            if (when, 0) in plan:
+                pl.when(step == when)(partial(run, (when, 0)))
+        blocks(0, 0, z, True)
+        blocks(1, panels, du, False)
+        blocks(2, 2 * panels, db, False)
+
+        def hook(n):
+            for p in range(head, head + pairs):
+                if (p, n) in plan:
+                    pl.when(step == p)(partial(run, (p, n)))
+
+        @pl.when(step >= head)
+        def _():
+            attend_back_body(size, count_ref, q_ref, k_ref, v_ref, o_ref, do_ref, lse_ref, out_ref, *own, hook)
+
+        @pl.when(step == head + pairs - 1)
         def _():
             run("end")
             for job, (n, path, rows) in zip(work, jobs):
@@ -602,31 +675,42 @@
             for job in work:
                 job.finish()
 
-    spec = lambda part: pl.BlockSpec((slots, PAIR), lambda p, n, part=part: (0, part * pairs + p))
+    pair_at = lambda s: jnp.maximum(s - head, 0)
+    spec = lambda part: pl.BlockSpec((slots, PAIR), lambda s, n, part=part: (0, part * pairs + pair_at(s)))
+    once = pl.BlockSpec((slots, d), lambda s, n: (0, 0), pipeline_mode=pl.Buffered(1))
+    panel = lambda first: pl.BlockSpec((slots, d), lambda s, n: (0, jnp.clip(s - first, 0, panels - 1)))
+    low, wide = jnp.bfloat16, jnp.float32
     return pl.pallas_call(
         kernel,
-        out_shape=[jax.ShapeDtypeStruct((3, slots, d), jnp.bfloat16)]
-        + [jax.ShapeDtypeStruct(s, jnp.bfloat16) for s in sizes],
+        out_shape=[jax.ShapeDtypeStruct((3, slots, d), low)]
+        + [jax.ShapeDtypeStruct(s, low) for s in sizes]
+        + [jax.ShapeDtypeStruct((panels, 1, d), wide), jax.ShapeDtypeStruct((1, 1, d), wide)],
         grid_spec=pltpu.PrefetchScalarGridSpec(
-            num_scalar_prefetch=1, grid=(pairs,),
-            in_specs=[spec(0), spec(1), spec(2), spec(0), spec(0), pl.BlockSpec((1, 2, slots), lambda p, n: (p, 0, 0))]
-            + [ANY] * count,
-            out_specs=[pl.BlockSpec((3, slots, PAIR), lambda p, n: (0, 0, p))] + [VM] * count,
-            scratch_shapes=attend_back_scratch(slots) + scatter_scratch(grid, sizes, jobs)),
-        compiler_params=pltpu.CompilerParams(vmem_limit_bytes=60 * 1024 * 1024, collective_id=collective_id,
+            num_scalar_prefetch=1, grid=(head + pairs,),
+            in_specs=[spec(0), spec(1), spec(2), spec(0), spec(0),
+                      pl.BlockSpec((1, 2, slots), lambda s, n: (pair_at(s), 0, 0)),
+                      once, panel(0), once, panel(panels), once, once],
+            out_specs=[pl.BlockSpec((3, slots, PAIR), lambda s, n: (0, 0, pair_at(s)))] + [VM] * 3
+            + [pl.BlockSpec((1, 1, d), lambda s, n: (jnp.clip(s - panels, 0, panels - 1), 0, 0)),
+               pl.BlockSpec((1, 1, d), lambda s, n: (0, 0, 0))],
+            scratch_shapes=[pltpu.VMEM(grid.shape("j", *s), low) for s in sizes] + [pltpu.VMEM((d, slots), low)]
+            + attend_back_scratch(slots) + scatter_scratch(grid, sizes, jobs)),
+        compiler_params=pltpu.CompilerParams(vmem_limit_bytes=62 * 1024 * 1024, collective_id=collective_id,
                                              has_side_effects=True),
-        name="attend_back_scatter",
-    )(counts, projected, projected, projected, attended, attended_grad, lse, *wholes)
+        name="grads_attend_back",
+    )(counts, projected, projected, projected, attended, attended_grad, lse, cotangent, active, normed, hidden_grad,
+      attended, branch_grad)
 
 
 BACKWARD_PLAN = {
-    0: [(n, 0) for n in range(6)],
-    3: [(0, 1), (1, 1)],
-    4: [(2, 1), (3, 1), (4, 1), (5, 1)],
-    6: [(0, 2), (1, 2)],
-    7: [(2, 2), (3, 2), (4, 2), (5, 2)],
-    9: [(0, 3), (1, 3)],
-    10: [(2, 3), (3, 3), (4, 3), (5, 3)],
+    (4, 0): [(0, 0)],
+    (6, 0): [(0, 1)],
+    (8, 0): [(1, 0), (0, 2)],
+    (9, 0): [(2, 0), (1, 1)],
+    (10, 0): [(0, 3)],
+    (10, 2): [(2, 1)],
+    (11, 2): [(1, 2), (2, 2)],
+    (12, 2): [(1, 3), (2, 3)],
 }
 
 
@@ -690,83 +774,6 @@
     return me, ranks, peers
 
 
-def to_owners(n_dp, n_fsdp, blocks_of, u, small, collective_id):
-    grid = Grid(n_dp, n_fsdp)
-    count = n_dp * n_fsdp
-
-    def kernel(of_ref, u_ref, small_ref, got, all_small, qkv, out, up, down, slots, send, recv):
-        g = grid.here()
-        me, ranks, peers = meet_all(g, n_dp, n_fsdp)
-
-        def fill(n, carry):
-            slots[n] = u_ref[of_ref[n]]
-            return carry
-
-        lax.fori_loop(0, count, fill, 0)
-        copies = []
-        for k, (rank, peer) in enumerate(zip(ranks, peers)):
-            copies.append(remote(slots.at[rank], got.at[me], send, recv, k, peer))
-        for k, peer in enumerate(peers):
-            copies.append(remote(small_ref, all_small.at[me], send, recv, count - 1 + k, peer))
-        start_all(copies)
-        spread = Spread(g, u_ref, (qkv, out, up, down), send, recv, 2 * count - 2)
-        spread.start()
-        got[me] = slots[me]
-        all_small[me] = small_ref[...]
-        arrived(copies)
-        sent(copies)
-        spread.finish()
-
-    lanes = 2 * count - 2 + 12
-    return pl.pallas_call(
-        kernel,
-        out_shape=[jax.ShapeDtypeStruct((count,) + PIECE, jnp.bfloat16),
-                   jax.ShapeDtypeStruct((count,) + small.shape, jnp.float32)] + TILES,
-        in_specs=[pl.BlockSpec(memory_space=pltpu.SMEM), VM, VM],
-        out_specs=[VM] * 6,
-        scratch_shapes=[pltpu.VMEM((count,) + PIECE, jnp.bfloat16), pltpu.SemaphoreType.DMA((lanes,)),
-                        pltpu.SemaphoreType.DMA((lanes,))],
-        compiler_params=pltpu.CompilerParams(collective_id=collective_id, has_side_effects=True),
-        name="to_owners",
-    )(blocks_of, u, small)
-
-
-def to_tiles(n_dp, n_fsdp, owners, pieces, collective_id):
-    grid = Grid(n_dp, n_fsdp)
-    count = n_dp * n_fsdp
-
-    def kernel(owners_ref, pieces_ref, qkv, out, up, down, got, u, send, recv):
-        g = grid.here()
-        me, ranks, peers = meet_all(g, n_dp, n_fsdp)
-        copies = [remote(pieces_ref.at[rank], got.at[me], send, recv, k, peer)
-                  for k, (rank, peer) in enumerate(zip(ranks, peers))]
-        start_all(copies)
-        got[me] = pieces_ref[me]
-        arrived(copies)
-
-        def fill(n, carry):
-            u[n] = got[owners_ref[n]]
-            return carry
-
-        lax.fori_loop(0, 12, fill, 0)
-        spread = Spread(g, u, (qkv, out, up, down), send, recv, count - 1)
-        spread.start()
-        sent(copies)
-        spread.finish()
-
-    lanes = count - 1 + 12
-    return pl.pallas_call(
-        kernel,
-        out_shape=TILES,
-        in_specs=[pl.BlockSpec(memory_space=pltpu.SMEM), VM],
-        out_specs=[VM] * 4,
-        scratch_shapes=[pltpu.VMEM((count,) + PIECE, jnp.bfloat16), pltpu.VMEM((12,) + PIECE, jnp.bfloat16),
-                        pltpu.SemaphoreType.DMA((lanes,)), pltpu.SemaphoreType.DMA((lanes,))],
-        compiler_params=pltpu.CompilerParams(collective_id=collective_id, has_side_effects=True),
-        name="to_tiles",
-    )(owners, pieces)
-
-
 def piece_rows(turned, z, x, y, c):
     if turned:
         return 192 * (2 * y + c) + 48 * z, 384 * x
@@ -777,47 +784,100 @@
     return [(z, x, y, c) for z in range(4) for x in range(2) for y in range(2) for c in range(2)]
 
 
-def precondition_kernel(flags, pieces, stats, roots, new_stats, steps, block, turned):
-    own, down = flags[0], flags[1]
-
-    @pl.when(own == 0)
-    def _():
-        new_stats[...] = stats[...]
-
-    @pl.when(own == 1)
-    def _():
-        for kind in range(2):
-
-            @pl.when(down == kind)
-            def _():
-                for n, place in enumerate(places()):
-                    row, column = piece_rows(kind, *place)
-                    block[row : row + 48, column : column + 384] = pieces[n]
-
+def owner_exchange(n_dp, n_fsdp, blocks_of, owners, flags, u, small, stats, roots, collective_id):
+    grid = Grid(n_dp, n_fsdp)
+    count = n_dp * n_fsdp
+    spread_lanes = 12
+
+    def kernel(of_ref, owners_ref, flags_ref, u_ref, small_ref, stats_hbm, roots_hbm,
+               all_small, qkv, out, up, down, s_qkv, s_out, s_up, s_down, new_stats_hbm,
+               slots, got, got_steps, u_steps, stats, roots, block, turned, local, send, recv):
+        g = grid.here()
+        me, ranks, peers = meet_all(g, n_dp, n_fsdp)
+        loads = [pltpu.make_async_copy(stats_hbm, stats, local.at[0]), pltpu.make_async_copy(roots_hbm, roots, local.at[1])]
+
+        def fill(n, carry):
+            slots[n] = u_ref[of_ref[n]]
+            return carry
+
+        lax.fori_loop(0, count, fill, 0)
+        lane = 0
+        copies, small_copies, step_copies = [], [], []
+        for rank, peer in zip(ranks, peers):
+            copies.append(remote(slots.at[rank], got.at[me], send, recv, lane, peer))
+            small_copies.append(remote(small_ref, all_small.at[me], send, recv, lane + 1, peer))
+            step_copies.append(remote(slots.at[rank], got_steps.at[me], send, recv, lane + 2, peer))
+            lane += 3
+        start_all(copies)
+        for load in loads:
+            load.start()
+        got[me] = slots[me]
+        all_small[me] = small_ref[...]
+        for load in loads:
+            load.wait()
+        arrived(copies)
+        sent(copies)
+        spread = Spread(g, u_ref, (qkv, out, up, down), send, recv, lane)
+        spread.start()
+        start_all(small_copies)
+
+        own, kind = flags_ref[0] == 1, flags_ref[1]
+        for turn in range(2):
+            for n, place in enumerate(places()):
+                row, column = piece_rows(turn, *place)
+                (turned if turn else block)[row : row + 48, column : column + 384] = got[n]
+        block[...] = jnp.where(kind == 1, turned[...], block[...])
         turned[...] = block[...].astype(jnp.float32).T.astype(jnp.bfloat16)
-        new_stats[down] = 0.5 * stats[down] + 0.5 * last_dot(block[...], block[...])
-        new_stats[1 - down] = 0.5 * stats[1 - down] + 0.5 * last_dot(turned[...], turned[...])
-        left = plain_dot(roots[down].astype(jnp.bfloat16), block[...]).astype(jnp.bfloat16)
-        block[...] = plain_dot(left, roots[1 - down].astype(jnp.bfloat16)).astype(jnp.bfloat16)
-        for kind in range(2):
-
-            @pl.when(down == kind)
-            def _():
-                for n, place in enumerate(places()):
-                    row, column = piece_rows(kind, *place)
-                    steps[n] = block[row : row + 48, column : column + 384]
-
-
-def precondition(flags, pieces, stats, roots):
+        left = plain_dot(roots[kind].astype(jnp.bfloat16), block[...]).astype(jnp.bfloat16)
+        step = plain_dot(left, roots[1 - kind].astype(jnp.bfloat16)).astype(jnp.bfloat16)
+        for n, place in enumerate(places()):
+            row, column = piece_rows(0, *place)
+            other_row, other_column = piece_rows(1, *place)
+            slots[n] = jnp.where(kind == 1, step[other_row : other_row + 48, other_column : other_column + 384],
+                                 step[row : row + 48, column : column + 384])
+        start_all(step_copies)
+        got_steps[me] = slots[me]
+        rows_by = last_dot(block[...], block[...])
+        columns_by = last_dot(turned[...], turned[...])
+        for side in range(2):
+            mine, other = (rows_by, columns_by) if side == 0 else (columns_by, rows_by)
+            moved = 0.5 * stats[side] + 0.5 * jnp.where(kind == 1, other, mine)
+            stats[side] = jnp.where(own, moved, stats[side])
+        store = pltpu.make_async_copy(stats, new_stats_hbm, local.at[0])
+        store.start()
+        arrived(step_copies)
+
+        def pick(n, carry):
+            u_steps[n] = got_steps[owners_ref[n]]
+            return carry
+
+        lax.fori_loop(0, 12, pick, 0)
+        back = Spread(g, u_steps, (s_qkv, s_out, s_up, s_down), send, recv, lane + spread_lanes)
+        back.start()
+        spread.finish()
+        arrived(small_copies)
+        sent(small_copies + step_copies)
+        back.finish()
+        store.wait()
+
+    lanes = 3 * (count - 1) + 2 * spread_lanes
+    low = jnp.bfloat16
+    smem = pl.BlockSpec(memory_space=pltpu.SMEM)
     return pl.pallas_call(
-        precondition_kernel,
-        out_shape=[jax.ShapeDtypeStruct(stats.shape, jnp.float32), jax.ShapeDtypeStruct(pieces.shape, jnp.bfloat16)],
-        in_specs=[pl.BlockSpec(memory_space=pltpu.SMEM), VM, VM, VM],
-        out_specs=[VM, VM],
-        scratch_shapes=[pltpu.VMEM(stats.shape[1:], jnp.bfloat16)] * 2,
-        compiler_params=pltpu.CompilerParams(vmem_limit_bytes=56 * 1024 * 1024),
-        name="precondition",
-    )(flags, pieces, stats, roots)
+        kernel,
+        out_shape=[jax.ShapeDtypeStruct((count,) + small.shape, jnp.float32)] + TILES + TILES
+        + [jax.ShapeDtypeStruct(stats.shape, jnp.float32)],
+        in_specs=[smem, smem, smem, VM, VM, ANY, ANY],
+        out_specs=[VM] * 9 + [ANY],
+        scratch_shapes=[pltpu.VMEM((count,) + PIECE, low), pltpu.VMEM((count,) + PIECE, low),
+                        pltpu.VMEM((count,) + PIECE, low), pltpu.VMEM((12,) + PIECE, low),
+                        pltpu.VMEM(stats.shape, jnp.float32), pltpu.VMEM(roots.shape, jnp.float32),
+                        pltpu.VMEM(stats.shape[1:], low), pltpu.VMEM(stats.shape[1:], low),
+                        pltpu.SemaphoreType.DMA((2,)), pltpu.SemaphoreType.DMA((lanes,)), pltpu.SemaphoreType.DMA((lanes,))],
+        compiler_params=pltpu.CompilerParams(collective_id=collective_id, has_side_effects=True,
+                                             vmem_limit_bytes=56 * 1024 * 1024),
+        name="owner_exchange",
+    )(blocks_of, owners, flags, u, small, stats, roots)
 
 
 def block_grads_kernel(turned_blocks, left, right, out, sums, left_turned):
@@ -853,6 +913,79 @@
         compiler_params=pltpu.CompilerParams(vmem_limit_bytes=56 * 1024 * 1024),
         name="block_grads",
     )(left, right)
+
+
+def centered(values):
+    center = values - jnp.mean(values, axis=-1, keepdims=True)
+    spread = lax.rsqrt(jnp.mean(center * center, axis=-1, keepdims=True) + 1e-06)
+    return center * spread, spread
+
+
+def norm_back(grads, unit, spread, gain):
+    scaled = grads * gain
+    mean = jnp.mean(scaled, axis=-1, keepdims=True)
+    along = jnp.mean(scaled * unit, axis=-1, keepdims=True)
+    return (scaled - mean - unit * along) * spread
+
+
+def middle_kernel(x, attended, dy, out_w, up_w, down_w, rows, bias_up,
+                  layer, h2, active, hidden_grad, middle_grad, branch_grad, attended_grad, sums):
+    gain, shift, bias_out, bias_down = rows[0:1], rows[1:2], rows[2:3], rows[3:4]
+    middle = x[...].astype(jnp.float32) + (plain_dot(attended[...], out_w[...]) + bias_out)
+    unit, spread = centered(middle)
+    normed = (unit * gain + shift).astype(jnp.bfloat16)
+    h2[...] = normed
+    grad_rows = dy[...]
+    panels = up_w.shape[0]
+    width = up_w.shape[2]
+    half = width // 2
+    y = jnp.zeros_like(middle)
+    dh = jnp.zeros_like(middle)
+    for panel in range(panels):
+        hidden = plain_dot(normed, up_w[panel]) + bias_up[panel : panel + 1]
+        passed = 0.5 + 0.5 * lax.erf(hidden * (0.5**0.5))
+        z = (hidden * passed).astype(jnp.bfloat16)
+        slope = passed + hidden * (jnp.exp(-0.5 * hidden * hidden) * 0.3989422804014327)
+        back = jnp.concatenate([plain_dot(grad_rows, down_w[2 * panel]), plain_dot(grad_rows, down_w[2 * panel + 1])], axis=1)
+        du = (slope * back).astype(jnp.bfloat16)
+        active[:, panel * width : (panel + 1) * width] = z
+        hidden_grad[:, panel * width : (panel + 1) * width] = du
+        y = y + last_dot(z[:, :half], down_w[2 * panel]) + last_dot(z[:, half:], down_w[2 * panel + 1])
+        dh = dh + last_dot(du, up_w[panel])
+    layer[...] = (middle + y + bias_down).astype(jnp.bfloat16)
+    wide = grad_rows.astype(jnp.float32)
+    total = wide + norm_back(dh, unit, spread, gain)
+    low = total.astype(jnp.bfloat16)
+    middle_grad[...] = total
+    branch_grad[...] = low
+    attended_grad[...] = last_dot(low, out_w[...]).astype(jnp.bfloat16)
+
+    @pl.when(pl.program_id(0) == 0)
+    def _():
+        sums[...] = jnp.zeros_like(sums)
+
+    sums[0:1] += jnp.sum(dh * unit, axis=0, keepdims=True)
+    sums[1:2] += jnp.sum(dh, axis=0, keepdims=True)
+    sums[2:3] += jnp.sum(wide, axis=0, keepdims=True)
+
+
+def middle_layer(tokens, attended, cotangent, out_w, up_w, down_w, rows, bias_up, block=256):
+    count, d = tokens.shape
+    ff = up_w.shape[0] * up_w.shape[2]
+    row = lambda width: pl.BlockSpec((block, width), lambda r: (r, 0))
+    whole = lambda array: pl.BlockSpec(array.shape, lambda r: (0,) * array.ndim)
+    low, wide = jnp.bfloat16, jnp.float32
+    shape = jax.ShapeDtypeStruct
+    return pl.pallas_call(
+        middle_kernel,
+        out_shape=[shape((count, d), low), shape((count, d), low), shape((count, ff), low), shape((count, ff), low),
+                   shape((count, d), wide), shape((count, d), low), shape((count, d), low), shape((8, d), wide)],
+        grid=(count // block,),
+        in_specs=[row(d), row(d), row(d)] + [whole(a) for a in (out_w, up_w, down_w, rows, bias_up)],
+        out_specs=[row(d), row(d), row(ff), row(ff), row(d), row(d), row(d), pl.BlockSpec((8, d), lambda r: (0, 0))],
+        compiler_params=pltpu.CompilerParams(vmem_limit_bytes=60 * 1024 * 1024),
+        name="middle_layer",
+    )(tokens, attended, cotangent, out_w, up_w, down_w, rows, bias_up)
 
 
 D = 768
@@ -1320,37 +1453,30 @@
         bias_down,
         bias_up,
     ) = unpack(small_params)
-    (qkv_pieces,) = gather_all(n_dp, n_fsdp, (qkv_low,), ("j",), 1)
+    orders = ("j", "j", "j", "i")
+    qkv_pieces, *begun = gather_first(n_dp, n_fsdp, (qkv_low,) + later[:2], orders[:3], 0, 1)
     qkv_full = whole_of(qkv_pieces)
     inputs = tokens.astype(jnp.float32)
     normed = layer_norm(inputs, gain_one, shift_one).astype(jnp.bfloat16)
     bias_qkv = jnp.concatenate([bias_query, jnp.zeros((D,), jnp.float32), bias_value])
     projected = (row_dot(normed, qkv_full) + bias_qkv).astype(jnp.bfloat16)
     attended, log_totals, out_pieces, up_pieces, down_pieces = attend_gather(
-        n_dp, n_fsdp, counts, projected, later, ("j", "j", "i"), FORWARD_PLAN, 2
-    )
-    out_full, up_full, down_full_t = whole_of(out_pieces), whole_of(up_pieces), whole_of(down_pieces)
-    middle = inputs + (row_dot(attended, out_full) + bias_out)
-    normed_two = layer_norm(middle, gain_two, shift_two).astype(jnp.bfloat16)
-    hidden = row_dot(normed_two, up_full) + bias_up
-    active = jax.nn.gelu(hidden, approximate=False).astype(jnp.bfloat16)
-    layer_rows = (middle + transposed_dot(active, down_full_t) + bias_down).astype(jnp.bfloat16)
-    grad_bias_down = jnp.sum(cotangent.astype(jnp.float32), axis=0)
-    active_grad = row_dot(cotangent, down_full_t)
-    unused_value, gelu_pull = jax.vjp(partial(jax.nn.gelu, approximate=False), hidden)
-    hidden_grad = gelu_pull(active_grad)[0].astype(jnp.bfloat16)
-    normed_two_grad = transposed_dot(hidden_grad, up_full)
-    unused_norm, norm_two_pull = jax.vjp(layer_norm, middle, gain_two, shift_two)
-    middle_grad, grad_gain_two, grad_shift_two = norm_two_pull(normed_two_grad)
-    middle_grad = middle_grad + cotangent.astype(jnp.float32)
-    branch_grad = middle_grad.astype(jnp.bfloat16)
-    attended_grad = transposed_dot(branch_grad, out_full).astype(jnp.bfloat16)
-    split_down, unused_sums = block_grads(cotangent, active, True)
-    split_up, grad_bias_up = block_grads(normed_two, hidden_grad, False)
-    split_out, grad_bias_out = block_grads(attended, branch_grad, False)
-    projected_grad, mine_down, mine_up, mine_out = attend_back_scatter(
+        n_dp, n_fsdp, counts, projected, begun, later[2:], orders[1:], FORWARD_PLAN, 2
+    )
+    layer_rows, normed_two, active, hidden_grad, middle_grad, branch_grad, attended_grad, sums = middle_layer(
+        tokens,
+        attended,
+        cotangent,
+        whole_of(out_pieces),
+        up_pieces.reshape(n_fsdp, D, FF // n_fsdp),
+        down_pieces.reshape(n_dp, D, FF // n_dp),
+        jnp.stack([gain_two, shift_two, bias_out, bias_down]),
+        bias_up.reshape(n_fsdp, FF // n_fsdp),
+    )
+    grad_gain_two, grad_shift_two, grad_bias_down = sums[0], sums[1], sums[2]
+    projected_grad, mine_down, mine_up, mine_out, grad_bias_up, grad_bias_out = grads_attend_back(
         n_dp, n_fsdp, counts, projected, attended, attended_grad, log_totals,
-        (split_down, split_up, split_out), BACKWARD_PLAN, 3,
+        cotangent, active, normed_two, hidden_grad, branch_grad, BACKWARD_PLAN, 3,
     )
     split_qkv, grad_bias_qkv = block_grads(normed, projected_grad, False)
     normed_grad = sum(
@@ -1380,14 +1506,14 @@
     numbers = jnp.arange(BLOCKS, dtype=jnp.int32)
     ranks = jnp.arange(devices, dtype=jnp.int32)
     blocks_of = jnp.sum(jnp.where(owners[None, :] == ranks[:, None], numbers[None, :], 0), axis=1).astype(jnp.int32)
-    gathered, small_pieces, *grad_tiles = to_owners(
-        n_dp, n_fsdp, blocks_of, mine.reshape(BLOCKS, 48, 384), mine_small, 5
-    )
     rank = lax.axis_index(("dp", "fsdp"))
     owning = jnp.any(owners == rank)
     flags = jnp.stack([owning, blocks_of[rank] >= 4 + FF // D]).astype(jnp.int32)
-    new_statistics, steps = precondition(flags, gathered, statistics[0], inverse_roots[0])
-    step_tiles = to_tiles(n_dp, n_fsdp, owners, steps, 6)
+    small_pieces, *tiles, new_statistics = owner_exchange(
+        n_dp, n_fsdp, blocks_of, owners, flags, mine.reshape(BLOCKS, 48, 384), mine_small[:8],
+        statistics[0], inverse_roots[0], 5,
+    )
+    grad_tiles, step_tiles = tiles[:4], tiles[4:]
     column_index = lax.axis_index("fsdp")
     shard_qkv, shard_out, shard_up, shard_down = tiles_of(grad_tiles, column_index)
     tile_qkv, tile_out, tile_up, tile_down = tiles_of(step_tiles, column_index)
@@ -1395,7 +1521,7 @@
     new_out = out_weight - step_rate * tile_out
     new_up = up_weight - step_rate * tile_up
     new_down = down_weight - step_rate * tile_down
-    whole_small = small_pieces.reshape(devices, 2048)[:, : 9216 // devices].reshape(-1)
+    whole_small = small_pieces.reshape(devices, 1024)[:, : 9216 // devices].reshape(-1)
     new_small = small_params - small_rate * whole_small * lax.rsqrt(
         jnp.mean(whole_small * whole_small) + 1e-06
     )

time: 521 us -> 419 us (0.80)
  matrix products: 89.2 us -> 14 us
  local copies, waits for them, and re-layouts: 37.3 us -> 24.1 us
  other arithmetic: 35.8 us -> 26.2 us
  Pallas kernels: 350 us -> 344 us
    dot_general x4 -> x1, matrix products: 63 us -> 7.54 us  [row_dot(): return jnp.dot(left, right, preferred_element_type=jnp.float32)]
    pallas_call x5 -> x4, Pallas kernels: 217 us -> 245 us  [the longest x1 85.9 us: grads_attend_back(): pl.pallas_call(kernel, out_shape=[jax.ShapeDtypeStruct((3, slots, d), low...]
    pallas_call x4 -> x1, Pallas kernels: 32 us -> 8.05 us  [block_grads(): pl.pallas_call(partial(block_grads_kernel, turned_blocks), out_shape=[jax...]
    dot_general x6 -> x3, matrix products: 26.1 us -> 6.45 us  [transposed_dot(): lax.dot_general(left, right, (((1,), (1,)), ((), ())), preferred_element_...]
    reshape x4 -> x2, local copies, waits for them, and re-layouts: 22.4 us -> 7.84 us  [whole_of(): folded = pieces.reshape(pieces.shape[0] * pieces.shape[1], -1, columns)]
    pallas_call x1, Pallas kernels: 71.6 us -> 58.3 us  [attend_gather(): pl.pallas_call(kernel, out_shape=[jax.ShapeDtypeStruct((slots, d), jnp.bf...]
where the time goes in v3:
time: 419 us; the launch traced here: 412 us
  Pallas kernels  344 us (82%)
  other arithmetic  26.2 us (6%)
  local copies, waits for them, and re-layouts  24.1 us (6%)
  matrix products  14 us (3%)
    pallas_call x1, Pallas kernels, grads_attend_back(): pl.pallas_call(kernel, out_shape=[jax.ShapeDtypeStruct((3, slots, d), low...  85.9 us
    pallas_call x1, Pallas kernels, owner_exchange(): pl.pallas_call(kernel, out_shape=[jax.ShapeDtypeStruct((count,) + small.s...  78.2 us
    pallas_call x1, Pallas kernels, attend_gather(): pl.pallas_call(kernel, out_shape=[jax.ShapeDtypeStruct((slots, d), jnp.bf...  58.3 us
    pallas_call x1, Pallas kernels, gather_first(): pl.pallas_call(kernel, out_shape=[jax.ShapeDtypeStruct(grid.shape(o, *s.s...  42.7 us
    pallas_call x1, Pallas kernels, middle_layer(): pl.pallas_call(middle_kernel, out_shape=[shape((count, d), low), shape((c...  38.3 us
    pallas_call x1, Pallas kernels, scatter_all(): pl.pallas_call(kernel, out_shape=[jax.ShapeDtypeStruct(s, dtype) for s in...  32.6 us

profile of v3, /device:TPU:27, one launch (start us, length us, event | category | flops | bytes accessed | tf_op | source)
XLA Modules:
  0.0 411.8 jit_solution(15149096908321875377)
XLA Ops:
  0.7 1.5 fusion.26
  2.2 1.7 convert_reduce_fusion
  3.9 2.0 fusion.9
  9.4 42.7 %gather_first.1 = (bf16[2,2,4,2,96,576]{5,4,3,2,1,0:T(8,128)(2,1)}, bf16[2,2,4,2,96,192]{5,4,3,2,1,0:T(8,128)(2,1)}, bf16[2,2,4,2,96,768]{5,4,3,2,1,0:T(8,128)(2,1)}) custom-call(bf16[96,576]{1,0:T(8,128)(2,1)} %convert_element_type.47.refs_0_, bf16[96,192]{1,0:T(8,128)(2,1)} %convert_element_type.48.refs_1_, bf16[96,768]{1,0:T(8,128)(2,1)} %convert_element_type.49.refs_2_), custom_call_target="tpu_custom_call" | custom-call | tf_op jit(solution)/shard_map/gather_first/pallas_call | solution.py:344
  52.1 6.2 %copy.37 = bf16[4,768,576]{1,2,0:T(8,128)(2,1)} copy(bf16[4,768,576]{2,1,0:T(8,128)(2,1)} %bitcast.82) | data formatting | bytes 7077888 | tf_op jit(solution)/shard_map/reshape | solution.py:1547
  58.2 7.5 %add_convert_fusion.q_ref.k_ref.v_ref = bf16[1024,2304]{1,0:T(8,128)(2,1)} fusion(bf16[1024,768]{1,0:T(8,128)(2,1)S(1)} %fusion.7.left, bf16[768,2304]{0,1:T(8,128)(2,1)} %bitcast.70, f32[2304]{0:T(1024)S(1)} %pad_maximum_fusion.1), kind=kOutput, calls=%fused_computation | convolution fusion | flops 3628597248 | bytes 9839616 | tf_op jit(solution)/shard_map/dot_general | solution.py:1022
  67.1 58.3 %attend_gather.1 = (bf16[1024,768]{1,0:T(8,128)(2,1)}, f32[6,2,1024]{2,1,0:T(2,128)}, bf16[2,2,4,2,96,192]{5,4,3,2,1,0:T(8,128)(2,1)}, bf16[2,2,4,2,96,768]{5,4,...) custom-call(s32[1]{0:T(128)S(6)} %copy.71.count_ref, ...), custom_call_target="tpu_custom_call", output_to_operand_aliasing={{2}: (4, {}), {3}: (5, {})} | custom-call | tf_op jit(solution)/shard_map/attend_gather/pallas_call | solution.py:576
  125.5 1.7 copy.38
  127.2 1.5 copy.39.out_w
  130.0 38.3 %middle_layer.1 = (bf16[1024,768]{1,0:T(8,128)(2,1)}, bf16[1024,768]{1,0:T(8,128)(2,1)}, bf16[1024,3072]{1,0:T(8,128)(2,1)}, bf16[1024,3072]{1,0:T(8,128)(2,1)},...) custom-call(bf16[1024,768]{1,0:T(8,128)(2,1)} %x.3, ...), custom_call_target="tpu_custom_call" | custom-call | tf_op jit(solution)/shard_map/middle_layer/pallas_call | solution.py:979
  168.3 85.9 %grads_attend_back.1 = (bf16[3,1024,768]{2,1,0:T(8,128)(2,1)}, bf16[192,384]{1,0:T(8,128)(2,1)}, bf16[192,384]{1,0:T(8,128)(2,1)}, bf16[48,384]{1,0:T(8,128)(2,1...) custom-call(s32[1]{0:T(128)S(6)} %copy.71.count_ref, bf16[1024,2304]{1,0:T(8,128)(2,1)} %add_convert_fusion.q_ref.k_ref.v_ref, ...), custom_call_target="tpu_custom_call" | custom-call | tf_op jit(solution)/shard_map/grads_attend_back/pallas_call | solution.py:683
  254.2 3.3 fusion.12
  258.5 1.4 fusion.14
  259.9 1.8 fusion.25
  261.7 1.6 copy-done.2
  263.3 2.2 fusion.8
  266.4 8.0 %block_grads.1 = (bf16[2,2,4,2,144,384]{5,4,3,2,1,0:T(8,128)(2,1)}, f32[3,1,768]{2,1,0:T(1,128)}) custom-call(bf16[1024,768]{1,0:T(8,128)(2,1)} %copy-done.6, bf16[3,1024,768]{2,1,0:T(8,128)(2,1)} %get-tuple-element.64.right), custom_call_target="tpu_custom_call" | custom-call | tf_op jit(solution)/shard_map/block_grads/pallas_call | solution.py:904
  277.0 32.6 %scatter_all.1 = (f32[144,384]{1,0:T(8,128)}, f32[16,128]{1,0:T(8,128)}) custom-call(bf16[2,2,4,2,144,384]{5,4,3,2,1,0:T(8,128)(2,1)} %get-tuple-element.65.refs_0_, bf16[2,2,4,2,16,128]{5,4,3,2,1,0:T(8,128)(2,1)} %bitcast.87), custom_call_target="tpu_custom_call" | custom-call | tf_op jit(solution)/shard_map/scatter_all/pallas_call | solution.py:388
  311.4 1.3 slice.114.small_ref
  314.7 1.2 add_convert_fusion.2.flags_ref
  315.9 78.2 %owner_exchange.1 = (f32[32,8,128]{2,1,0:T(8,128)}, bf16[2,96,384]{2,1,0:T(8,128)(2,1)}, bf16[2,96,384]{2,1,0:T(8,128)(2,1)}, bf16[2,96,384]{2,1,0:T(8,128)(2,1)...) custom-call(s32[32]{0:T(128)} %copy-done.33, ...), custom_call_target="tpu_custom_call" | custom-call | tf_op jit(solution)/shard_map/owner_exchange/pallas_call | solution.py:866
  397.2 1.1 convert_bitcast_fusion
  405.6 3.7 add_convert_fusion.1
  409.3 2.2 copy.72
  (136 shorter events, 22.3 us)
Async XLA Ops:
  0.6 6.0 %copy-start = (bf16[1024,768]{1,0:T(8,128)(2,1)S(1)}, bf16[1024,768]{1,0:T(8,128)(2,1)}, u32[]{:S(2)}) copy-start(bf16[1024,768]{1,0:T(8,128)(2,1)} %x.3) | copy-start | bytes 4718596
  2.2 5.1 %copy-start.7 = (f32[96,768]{1,0:T(8,128)S(1)}, f32[96,768]{1,0:T(8,128)}, u32[]{:S(2)}) copy-start(f32[96,768]{1,0:T(8,128)} %param.16) | copy-start | bytes 884740
  2.2 5.9 %copy-start.10 = (f32[96,576]{1,0:T(8,128)S(1)}, f32[96,576]{1,0:T(8,128)}, u32[]{:S(2)}) copy-start(f32[96,576]{1,0:T(8,128)} %param.14) | copy-start | bytes 663556
  3.9 4.8 %copy-start.12 = (f32[96,192]{1,0:T(8,128)S(1)}, f32[96,192]{1,0:T(8,128)}, u32[]{:S(2)}) copy-start(f32[96,192]{1,0:T(8,128)} %param.15) | copy-start | bytes 221188
  7.2 51.0 %copy-start.6 = (bf16[1024,768]{1,0:T(8,128)(2,1)}, bf16[1024,768]{1,0:T(8,128)(2,1)S(1)}, u32[]{:S(2)}) copy-start(bf16[1024,768]{1,0:T(8,128)(2,1)S(1)} %fusion.7.left) | copy-start | bytes 4718596
  58.2 8.2 %copy-start.8 = (f32[384,192]{0,1:T(8,128)S(1)}, f32[384,192]{0,1:T(8,128)}, u32[]{:S(2)}) copy-start(f32[384,192]{0,1:T(8,128)} %param.17) | copy-start | bytes 884740
  254.2 4.3 %copy-start.5 = (bf16[4,768,576]{1,2,0:T(8,128)(2,1)S(1)}, bf16[4,768,576]{1,2,0:T(8,128)(2,1)}, u32[]{:S(2)}) copy-start(bf16[4,768,576]{1,2,0:T(8,128)(2,1)} %copy.37) | copy-start | bytes 10616836
  261.7 4.2 %copy-start.25 = (f32[8,768]{1,0:T(8,128)S(1)}, f32[8,768]{1,0:T(8,128)}, u32[]{:S(2)}) copy-start(f32[8,768]{1,0:T(8,128)} %get-tuple-element.66) | copy-start | bytes 73732
  266.4 9.3 %copy-start.31 = (f32[1,1,768]{2,1,0:T(1,128)S(1)}, f32[1,1,768]{2,1,0:T(1,128)}, u32[]{:S(2)}) copy-start(f32[1,1,768]{2,1,0:T(1,128)} %get-tuple-element.68) | copy-start | bytes 9220
  266.4 9.8 %copy-start.30 = (f32[4,1,768]{2,1,0:T(1,128)S(1)}, f32[4,1,768]{2,1,0:T(1,128)}, u32[]{:S(2)}) copy-start(f32[4,1,768]{2,1,0:T(1,128)} %get-tuple-element.69) | copy-start | bytes 36868
  274.4 36.2 %copy-start.15 = (bf16[192,384]{1,0:T(8,128)(2,1)S(1)}, bf16[192,384]{1,0:T(8,128)(2,1)}, u32[]{:S(2)}) copy-start(bf16[192,384]{1,0:T(8,128)(2,1)} %get-tuple-element.73) | copy-start | bytes 442372
  274.4 36.2 %copy-start.16 = (bf16[192,384]{1,0:T(8,128)(2,1)S(1)}, bf16[192,384]{1,0:T(8,128)(2,1)}, u32[]{:S(2)}) copy-start(bf16[192,384]{1,0:T(8,128)(2,1)} %get-tuple-element.72) | copy-start | bytes 442372
  274.4 36.2 %copy-start.24 = (bf16[48,384]{1,0:T(8,128)(2,1)S(1)}, bf16[48,384]{1,0:T(8,128)(2,1)}, u32[]{:S(2)}) copy-start(bf16[48,384]{1,0:T(8,128)(2,1)} %get-tuple-element.71) | copy-start | bytes 110596
  274.5 38.3 %copy-start.32 = (s32[12]{0:T(128)S(1)}, s32[12]{0:T(128)}, u32[]{:S(2)}) copy-start(s32[12]{0:T(128)} %owners_ref.1) | copy-start | bytes 148
  315.9 80.7 %copy-start.13 = (f32[9216]{0:T(1024)S(1)}, f32[9216]{0:T(1024)}, u32[]{:S(2)}) copy-start(f32[9216]{0:T(1024)} %param.18) | copy-start | bytes 110596
  394.1 6.7 %copy-start.11 = (f32[96,576]{1,0:T(8,128)S(1)}, f32[96,576]{1,0:T(8,128)}, u32[]{:S(2)}) copy-start(f32[96,576]{1,0:T(8,128)} %param.14) | copy-start | bytes 663556
  395.8 4.0 copy-start.19
  397.2 5.2 %copy-start.17 = (bf16[2,96,384]{2,1,0:T(8,128)(2,1)S(1)}, bf16[2,96,384]{2,1,0:T(8,128)(2,1)}, u32[]{:S(2)}) copy-start(bf16[2,96,384]{2,1,0:T(8,128)(2,1)} %get-tuple-element.75) | copy-start | bytes 442372
  397.2 5.2 %copy-start.18 = (bf16[2,96,384]{2,1,0:T(8,128)(2,1)S(1)}, bf16[2,96,384]{2,1,0:T(8,128)(2,1)}, u32[]{:S(2)}) copy-start(bf16[2,96,384]{2,1,0:T(8,128)(2,1)} %get-tuple-element.76) | copy-start | bytes 442372
  399.1 5.0 %copy-start.9 = (f32[384,192]{0,1:T(8,128)S(1)}, f32[384,192]{0,1:T(8,128)}, u32[]{:S(2)}) copy-start(f32[384,192]{0,1:T(8,128)} %param.17) | copy-start | bytes 884740
  399.1 5.0 %copy-start.21 = (bf16[192,384]{1,0:T(8,128)(2,1)S(1)}, bf16[192,384]{1,0:T(8,128)(2,1)}, u32[]{:S(2)}) copy-start(bf16[192,384]{1,0:T(8,128)(2,1)} %get-tuple-element.84) | copy-start | bytes 442372
  400.8 4.1 copy-start.14
  400.8 4.8 %copy-start.26 = (f32[1024]{0:T(1024)S(1)}, f32[1024]{0:T(1024)}, u32[]{:S(2)}) copy-start(f32[1024]{0:T(1024)} %get-tuple-element.86) | copy-start | bytes 12292
  400.9 4.7 %copy-start.3 = (f32[1024,768]{1,0:T(8,128)S(1)}, f32[1024,768]{1,0:T(8,128)}, u32[]{:S(2)}) copy-start(f32[1024,768]{1,0:T(8,128)} %copy-done.2) | copy-start | bytes 9437188
  (13 other events, 34.3 us)

commit v4 on v3

--- a/solution.py
+++ b/solution.py
@@ -524,80 +524,103 @@
     out_ref[2] = dv_sum[...].astype(jnp.bfloat16)
 
 
-def attend_gather(n_dp, n_fsdp, counts, projected, pieces, fresh, orders, plan, collective_id, size=512):
-    slots, width = projected.shape
-    d = width // 3
+def project_attend(n_dp, n_fsdp, counts, tokens, weight_pieces, norm_rows, bias, pieces, fresh, orders, plan, collective_id,
+                   size=512, block=256):
+    slots, d = tokens.shape
+    width = weight_pieces.shape[0] * weight_pieces.shape[2]
     pairs = d // PAIR
+    head = slots // block
     grid = Grid(n_dp, n_fsdp)
     begun, count = len(pieces), len(pieces) + len(fresh)
-    jobs = job_list([a.shape[-2:] for a in (*pieces, *fresh)])
+    jobs = plan["jobs"]
+    waits = [job[0] < begun for job in jobs]
     shapes = [jax.ShapeDtypeStruct(p.shape, p.dtype) for p in pieces]
     shapes += [jax.ShapeDtypeStruct(grid.shape(o, *a.shape), a.dtype) for a, o in zip(fresh, orders[begun:])]
-    steps = slots // size
-
-    def kernel(count_ref, q_ref, k_ref, v_ref, *refs):
-        (o_ref, lse_ref), outs = refs[count : count + 2], refs[count + 2 : 2 * count + 2]
-        q_heads, v_turned = refs[2 * count + 2 : 2 * count + 4]
+
+    def kernel(count_ref, x, w_pieces, rows, bias_ref, *refs):
+        (h_ref, p_ref, w_ref, o_ref, lse_ref), outs = refs[count : count + 5], refs[count + 5 : 2 * count + 5]
+        projected, q_heads, v_turned = refs[2 * count + 5 : 2 * count + 8]
         g = grid.here()
-        work = gather_jobs(g, orders, jobs, outs[:begun] + refs[begun:count], outs, refs[2 * count + 4 :])
-        pair = pl.program_id(0)
+        work = gather_jobs(g, orders, jobs, outs[:begun] + refs[begun:count], outs, refs[2 * count + 8 :])
+        step = pl.program_id(0)
 
         def run(when):
-            for j, step in plan.get(when, []):
-                if step == 1 and j < begun:
+            for j, number in plan.get(when, []):
+                if number == 1 and waits[j]:
                     work[j].resume()
                 else:
-                    work[j].step(step)
-
-        @pl.when(pair == 0)
+                    work[j].step(number)
+
+        @pl.when(step == 0)
         def _():
             g.barrier()
 
-        def hook(n):
-            for p in range(pairs):
-                if (p, n) in plan:
-                    pl.when(pair == p)(partial(run, (p, n)))
-
-        hook(0)
-        attend_prepare(q_ref, v_ref, q_heads, v_turned)
-        length = count_ref[0]
-        for n in range(steps):
-            if n > 0:
-                hook(n)
-            attend_block(length, n * size, size, q_heads, k_ref, v_turned, o_ref, lse_ref.at[0])
-
-        @pl.when(pair == pairs - 1)
+        for when in range(head + pairs):
+            if when in plan:
+                pl.when(step == when)(partial(run, when))
+
+        @pl.when(step == 0)
+        def _():
+            part = w_pieces.shape[2]
+            for n in range(w_pieces.shape[0]):
+                w_ref[:, n * part : (n + 1) * part] = w_pieces[n]
+
+        @pl.when(step < head)
+        def _():
+            unit, spread = centered(x[...].astype(jnp.float32))
+            low = (unit * rows[0:1] + rows[1:2]).astype(jnp.bfloat16)
+            h_ref[...] = low
+            result = (plain_dot(low, w_ref[...]) + bias_ref[...]).astype(jnp.bfloat16)
+            p_ref[...] = result
+            projected[pl.ds(pl.multiple_of(step * block, block), block), :] = result
+
+        @pl.when(step >= head)
+        def _():
+            lane = pl.multiple_of((step - head) * PAIR, PAIR)
+            q_ref, k_ref, v_ref = (projected.at[:, pl.ds(lane + part * d, PAIR)] for part in range(3))
+            attend_prepare(q_ref, v_ref, q_heads, v_turned)
+            length = count_ref[0]
+            for n in range(slots // size):
+                attend_block(length, n * size, size, q_heads, k_ref, v_turned, o_ref, lse_ref.at[0])
+
+        @pl.when(step == head + pairs - 1)
         def _():
             run("end")
             for j, job in enumerate(work):
-                job.finish(1 if j < begun else 0)
-
-    spec = lambda part: pl.BlockSpec((slots, PAIR), lambda p, n, part=part: (0, part * pairs + p))
+                job.finish(1 if waits[j] else 0)
+
+    low = jnp.bfloat16
+    row_at = lambda s: jnp.minimum(s, head - 1)
+    pair_at = lambda s: jnp.maximum(s - head, 0)
+    row = lambda w: pl.BlockSpec((block, w), lambda s, n: (row_at(s), 0))
+    whole = lambda array: pl.BlockSpec(array.shape, lambda s, n: (0,) * array.ndim, pipeline_mode=pl.Buffered(1))
     return pl.pallas_call(
         kernel,
-        out_shape=[jax.ShapeDtypeStruct((slots, d), jnp.bfloat16),
-                   jax.ShapeDtypeStruct((pairs, 2, slots), jnp.float32)]
-        + shapes,
+        out_shape=[jax.ShapeDtypeStruct((slots, d), low), jax.ShapeDtypeStruct((slots, width), low),
+                   jax.ShapeDtypeStruct((d, width), low), jax.ShapeDtypeStruct((slots, d), low),
+                   jax.ShapeDtypeStruct((pairs, 2, slots), jnp.float32)] + shapes,
         grid_spec=pltpu.PrefetchScalarGridSpec(
-            num_scalar_prefetch=1, grid=(pairs,),
-            in_specs=[spec(0), spec(1), spec(2)] + [ANY] * count,
-            out_specs=[pl.BlockSpec((slots, PAIR), lambda p, n: (0, p)),
-                       pl.BlockSpec((1, 2, slots), lambda p, n: (p, 0, 0))] + [ANY] * count,
-            scratch_shapes=[pltpu.VMEM((2, slots, PAIR), jnp.bfloat16), pltpu.VMEM((2, PAIR, slots), jnp.bfloat16)]
-            + gather_scratch(grid, len(jobs))),
-        input_output_aliases={4 + n: 2 + n for n in range(begun)},
+            num_scalar_prefetch=1, grid=(head + pairs,),
+            in_specs=[row(d), whole(weight_pieces), whole(norm_rows), whole(bias)] + [ANY] * count,
+            out_specs=[row(d), row(width), pl.BlockSpec((d, width), lambda s, n: (0, 0)),
+                       pl.BlockSpec((slots, PAIR), lambda s, n: (0, pair_at(s))),
+                       pl.BlockSpec((1, 2, slots), lambda s, n: (pair_at(s), 0, 0))] + [ANY] * count,
+            scratch_shapes=[pltpu.VMEM((slots, width), low), pltpu.VMEM((2, slots, PAIR), low),
+                            pltpu.VMEM((2, PAIR, slots), low)] + gather_scratch(grid, len(jobs))),
+        input_output_aliases={5 + n: 5 + n for n in range(begun)},
         compiler_params=pltpu.CompilerParams(vmem_limit_bytes=56 * 1024 * 1024, collective_id=collective_id,
                                              has_side_effects=True),
-        name="attend_gather",
-    )(counts, projected, projected, projected, *pieces, *fresh)
+        name="project_attend",
+    )(counts, tokens, weight_pieces, norm_rows, bias, *pieces, *fresh)
 
 
 FORWARD_PLAN = {
-    (0, 0): [(0, 1), (1, 1), (2, 0)],
-    (1, 0): [(0, 2)],
-    (2, 0): [(1, 2), (0, 3)],
-    (3, 0): [(2, 1)],
-    (4, 0): [(2, 2)],
+    "jobs": [(0, 0, pl.ds(0, 96)), (1, 0, pl.ds(0, 96)), (2, 0, pl.ds(0, 192))],
+    0: [(0, 1), (1, 1), (2, 0)],
+    2: [(0, 2)],
+    5: [(1, 2), (0, 3)],
+    7: [(2, 1)],
+    9: [(2, 2)],
     "end": [(1, 3), (2, 3)],
 }
 
@@ -617,7 +640,8 @@
     head = 2 * panels + 1
     grid = Grid(n_dp, n_fsdp)
     sizes = [(panels * 48, 384), (panels * 48, 384), (48, 384)]
-    jobs = job_list(sizes)
+    half = panels * 24
+    jobs = [(n, 0, pl.ds(at, half)) for n in range(2) for at in (0, half)] + [(2, 0, pl.ds(0, 48))]
     steps = slots // size
 
     def kernel(count_ref, q_ref, k_ref, v_ref, o_ref, do_ref, lse_ref, dy, z, h2, du, o_all, db, out_ref, *refs):
@@ -703,14 +727,17 @@
 
 
 BACKWARD_PLAN = {
-    (4, 0): [(0, 0)],
-    (6, 0): [(0, 1)],
-    (8, 0): [(1, 0), (0, 2)],
-    (9, 0): [(2, 0), (1, 1)],
-    (10, 0): [(0, 3)],
-    (10, 2): [(2, 1)],
-    (11, 2): [(1, 2), (2, 2)],
-    (12, 2): [(1, 3), (2, 3)],
+    (2, 0): [(0, 0)],
+    (4, 0): [(1, 0)],
+    (5, 0): [(0, 1)],
+    (7, 0): [(1, 1), (2, 0)],
+    (8, 0): [(3, 0), (0, 2)],
+    (9, 0): [(4, 0), (2, 1)],
+    (10, 0): [(1, 2), (0, 3), (3, 1)],
+    (11, 0): [(2, 2), (1, 3), (4, 1)],
+    (12, 0): [(3, 2), (2, 3)],
+    (13, 0): [(4, 2), (3, 3)],
+    (14, 0): [(4, 3)],
 }
 
 
@@ -784,14 +811,24 @@
     return [(z, x, y, c) for z in range(4) for x in range(2) for y in range(2) for c in range(2)]
 
 
-def owner_exchange(n_dp, n_fsdp, blocks_of, owners, flags, u, small, stats, roots, collective_id):
+def tile_values(g, tiles):
+    qkv, out, up, down = tiles
+    odd = (g.y * 2 + g.c) % 2 == 1
+    wide = jnp.float32
+    band = jnp.concatenate([qkv[0].astype(wide), qkv[1].astype(wide)], axis=1)
+    half = out[g.y].astype(wide)
+    return [jnp.where(odd, band[:, 192:], band[:, :576]), jnp.where(odd, half[:, 192:], half[:, :192]),
+            jnp.concatenate([up[0].astype(wide), up[1].astype(wide)], axis=1), down[...].astype(wide).T]
+
+
+def owner_exchange(n_dp, n_fsdp, blocks_of, owners, flags, u, small, stats, roots, masters, small_params, rates, collective_id):
     grid = Grid(n_dp, n_fsdp)
     count = n_dp * n_fsdp
     spread_lanes = 12
 
-    def kernel(of_ref, owners_ref, flags_ref, u_ref, small_ref, stats_hbm, roots_hbm,
-               all_small, qkv, out, up, down, s_qkv, s_out, s_up, s_down, new_stats_hbm,
-               slots, got, got_steps, u_steps, stats, roots, block, turned, local, send, recv):
+    def kernel(of_ref, owners_ref, flags_ref, u_ref, small_ref, w_qkv, w_out, w_up, w_down, params, stats_hbm, roots_hbm,
+               g_qkv, g_out, g_up, g_down, n_qkv, n_out, n_up, n_down, g_small, n_small, new_stats_hbm,
+               all_small, qkv, out, up, down, s_qkv, s_out, s_up, s_down, slots, got, got_steps, u_steps, stats, roots, block, turned, local, send, recv):
         g = grid.here()
         me, ranks, peers = meet_all(g, n_dp, n_fsdp)
         loads = [pltpu.make_async_copy(stats_hbm, stats, local.at[0]), pltpu.make_async_copy(roots_hbm, roots, local.at[1])]
@@ -845,6 +882,15 @@
             stats[side] = jnp.where(own, moved, stats[side])
         store = pltpu.make_async_copy(stats, new_stats_hbm, local.at[0])
         store.start()
+        spread.finish()
+        for ref, value in zip((g_qkv, g_out, g_up, g_down), tile_values(g, (qkv, out, up, down))):
+            ref[...] = value
+        arrived(small_copies)
+        lines = params.shape[0]
+        total = jnp.concatenate([all_small[n].astype(jnp.float32) for n in range(-(-lines // 16))], axis=0)[:lines]
+        g_small[...] = total
+        mean = jnp.sum(total * total) * (1.0 / (lines * 128))
+        n_small[...] = params[...] - rates[1] * total * lax.rsqrt(jnp.full((1, 128), mean + 1e-06, jnp.float32))
         arrived(step_copies)
 
         def pick(n, carry):
@@ -854,10 +900,11 @@
         lax.fori_loop(0, 12, pick, 0)
         back = Spread(g, u_steps, (s_qkv, s_out, s_up, s_down), send, recv, lane + spread_lanes)
         back.start()
-        spread.finish()
-        arrived(small_copies)
         sent(small_copies + step_copies)
         back.finish()
+        new = tile_values(g, (s_qkv, s_out, s_up, s_down))
+        for ref, master, value in zip((n_qkv, n_out, n_up, n_down), (w_qkv, w_out, w_up, w_down), new):
+            ref[...] = master[...] - rates[0] * value
         store.wait()
 
     lanes = 3 * (count - 1) + 2 * spread_lanes
@@ -865,11 +912,11 @@
     smem = pl.BlockSpec(memory_space=pltpu.SMEM)
     return pl.pallas_call(
         kernel,
-        out_shape=[jax.ShapeDtypeStruct((count,) + small.shape, jnp.float32)] + TILES + TILES
-        + [jax.ShapeDtypeStruct(stats.shape, jnp.float32)],
-        in_specs=[smem, smem, smem, VM, VM, ANY, ANY],
-        out_specs=[VM] * 9 + [ANY],
-        scratch_shapes=[pltpu.VMEM((count,) + PIECE, low), pltpu.VMEM((count,) + PIECE, low),
+        out_shape=[jax.ShapeDtypeStruct(a.shape, jnp.float32) for a in (*masters, *masters, small_params, small_params, stats)],
+        in_specs=[smem, smem, smem] + [VM] * 7 + [ANY, ANY],
+        out_specs=[VM] * 10 + [ANY],
+        scratch_shapes=[pltpu.VMEM((count,) + small.shape, low)] + [pltpu.VMEM(t.shape, low) for t in TILES * 2]
+        + [pltpu.VMEM((count,) + PIECE, low), pltpu.VMEM((count,) + PIECE, low),
                         pltpu.VMEM((count,) + PIECE, low), pltpu.VMEM((12,) + PIECE, low),
                         pltpu.VMEM(stats.shape, jnp.float32), pltpu.VMEM(roots.shape, jnp.float32),
                         pltpu.VMEM(stats.shape[1:], low), pltpu.VMEM(stats.shape[1:], low),
@@ -877,7 +924,7 @@
         compiler_params=pltpu.CompilerParams(collective_id=collective_id, has_side_effects=True,
                                              vmem_limit_bytes=56 * 1024 * 1024),
         name="owner_exchange",
-    )(blocks_of, owners, flags, u, small, stats, roots)
+    )(blocks_of, owners, flags, u, small, *masters, small_params, stats, roots)
 
 
 def block_grads_kernel(turned_blocks, left, right, out, sums, left_turned):
@@ -986,6 +1033,96 @@
         compiler_params=pltpu.CompilerParams(vmem_limit_bytes=60 * 1024 * 1024),
         name="middle_layer",
     )(tokens, attended, cotangent, out_w, up_w, down_w, rows, bias_up)
+
+
+def project_back(n_dp, n_fsdp, tokens, normed, projected_grad, weight, middle_grad, gain, others, collective_id, block=256):
+    grid = Grid(n_dp, n_fsdp)
+    count, d = tokens.shape
+    n_blocks = projected_grad.shape[0]
+    lines = others.shape[0]
+    sizes = [(48, 384)] * n_blocks + [(16, 128)]
+    jobs = job_list(sizes)
+    low, wide = jnp.bfloat16, jnp.float32
+
+    def kernel(x_h, normed_h, dp_h, weight_h, middle_h, gain_ref, others_ref, mine, small, input_grad_h, *refs):
+        x, h, dp, w, middle, out = refs[:6]
+        left, parts, small_parts, rows, packed, local = refs[6:12]
+        scratch = refs[12:]
+        g = grid.here()
+        g.barrier()
+        loads = [pltpu.make_async_copy(a, b, local.at[n])
+                 for n, (a, b) in enumerate(((normed_h, h), (dp_h, dp), (weight_h, w), (x_h, x), (middle_h, middle)))]
+        for load in loads:
+            load.start()
+        loads[0].wait()
+        left[...] = h[...].astype(wide).T.astype(low)
+        loads[1].wait()
+        work = scatter_jobs(g, ["j"] * (n_blocks + 1), jobs, [parts.at[n] for n in range(n_blocks)] + [small_parts], scratch)
+        for n in range(n_blocks):
+            values = dp[n]
+            grad = plain_dot(left[...], values).astype(low)
+            for z, px, y, c in places():
+                row, column = piece_rows(False, z, px, y, c)
+                parts[n, y, c, z, px] = grad[row : row + 48, column : column + 384]
+            work[n].step(0)
+        for line in range(lines):
+            rows[line : line + 1] = others_ref[line : line + 1]
+        rows[4:5] = jnp.sum(dp[0].astype(wide), axis=0, keepdims=True)
+        rows[5:6] = jnp.sum(dp[2].astype(wide), axis=0, keepdims=True)
+        for load in loads[2:]:
+            load.wait()
+
+        def back(n):
+            at = slice(n * block, (n + 1) * block)
+            dh = last_dot(dp[0, at], w[:, :d]) + last_dot(dp[1, at], w[:, d : 2 * d]) + last_dot(dp[2, at], w[:, 2 * d :])
+            unit, spread = centered(x[at].astype(wide))
+            out[at] = (middle[at] + norm_back(dh, unit, spread, gain_ref[...])).astype(low)
+            scaled, shifted = jnp.sum(dh * unit, axis=0, keepdims=True), jnp.sum(dh, axis=0, keepdims=True)
+            rows[0:1] = scaled if n == 0 else rows[0:1] + scaled
+            rows[1:2] = shifted if n == 0 else rows[1:2] + shifted
+
+        plan = {0: [(0, 1)], 1: [(1, 1), (2, 1)], 2: [(0, 2)], 3: [(1, 2), (2, 2)]}
+        for n in range(count // block):
+            for j, step in plan.get(n, []):
+                work[j].step(step)
+            back(n)
+        store = pltpu.make_async_copy(out, input_grad_h, local.at[0])
+        store.start()
+        packed[...] = jnp.zeros_like(packed)
+        for line in range(lines):
+            for part in range(d // 128):
+                at = line * (d // 128) + part
+                packed[at : at + 1] = rows[line : line + 1, part * 128 : (part + 1) * 128]
+        small_parts[...] = jnp.zeros_like(small_parts)
+        for n, (z, px, y, c) in enumerate(places()):
+            if n < packed.shape[0] // 16:
+                small_parts[y, c, z, px] = packed[16 * n : 16 * n + 16].astype(low)
+        work[n_blocks].step(0)
+        for j in range(n_blocks):
+            work[j].step(3)
+            work[n_blocks].step(j + 1)
+        for n in range(n_blocks):
+            mine[n] = work[n].total().astype(low)
+        small[...] = work[n_blocks].total().astype(low)
+        for job in work:
+            job.finish()
+        store.wait()
+
+    shape = jax.ShapeDtypeStruct
+    return pl.pallas_call(
+        kernel,
+        out_shape=[shape((n_blocks, 48, 384), low), shape((16, 128), low), shape((count, d), low)],
+        in_specs=[ANY] * 5 + [VM, VM],
+        out_specs=[VM, VM, ANY],
+        scratch_shapes=[pltpu.VMEM((count, d), low), pltpu.VMEM((count, d), low), pltpu.VMEM(projected_grad.shape, low),
+                        pltpu.VMEM(weight.shape, low), pltpu.VMEM((count, d), wide), pltpu.VMEM((count, d), low),
+                        pltpu.VMEM((d, count), low), pltpu.VMEM((n_blocks,) + grid.shape("j", 48, 384), low),
+                        pltpu.VMEM(grid.shape("j", 16, 128), low), pltpu.VMEM((16, d), wide), pltpu.VMEM((80, 128), wide),
+                        pltpu.SemaphoreType.DMA((5,))] + scatter_scratch(grid, sizes, jobs),
+        compiler_params=pltpu.CompilerParams(vmem_limit_bytes=60 * 1024 * 1024, collective_id=collective_id,
+                                             has_side_effects=True),
+        name="project_back",
+    )(tokens, normed, projected_grad, weight, middle_grad, gain, others)
 
 
 D = 768
@@ -1455,13 +1592,10 @@
     ) = unpack(small_params)
     orders = ("j", "j", "j", "i")
     qkv_pieces, *begun = gather_first(n_dp, n_fsdp, (qkv_low,) + later[:2], orders[:3], 0, 1)
-    qkv_full = whole_of(qkv_pieces)
-    inputs = tokens.astype(jnp.float32)
-    normed = layer_norm(inputs, gain_one, shift_one).astype(jnp.bfloat16)
     bias_qkv = jnp.concatenate([bias_query, jnp.zeros((D,), jnp.float32), bias_value])
-    projected = (row_dot(normed, qkv_full) + bias_qkv).astype(jnp.bfloat16)
-    attended, log_totals, out_pieces, up_pieces, down_pieces = attend_gather(
-        n_dp, n_fsdp, counts, projected, begun, later[2:], orders[1:], FORWARD_PLAN, 2
+    normed, projected, qkv_full, attended, log_totals, out_pieces, up_pieces, down_pieces = project_attend(
+        n_dp, n_fsdp, counts, tokens, qkv_pieces.reshape(n_fsdp, D, 3 * D // n_fsdp), jnp.stack([gain_one, shift_one]),
+        bias_qkv[None], begun, later[2:], orders[1:], FORWARD_PLAN, 2,
     )
     layer_rows, normed_two, active, hidden_grad, middle_grad, branch_grad, attended_grad, sums = middle_layer(
         tokens,
@@ -1473,58 +1607,32 @@
         jnp.stack([gain_two, shift_two, bias_out, bias_down]),
         bias_up.reshape(n_fsdp, FF // n_fsdp),
     )
-    grad_gain_two, grad_shift_two, grad_bias_down = sums[0], sums[1], sums[2]
     projected_grad, mine_down, mine_up, mine_out, grad_bias_up, grad_bias_out = grads_attend_back(
         n_dp, n_fsdp, counts, projected, attended, attended_grad, log_totals,
         cotangent, active, normed_two, hidden_grad, branch_grad, BACKWARD_PLAN, 3,
     )
-    split_qkv, grad_bias_qkv = block_grads(normed, projected_grad, False)
-    normed_grad = sum(
-        transposed_dot(projected_grad[part], qkv_full[:, part * D : (part + 1) * D]) for part in range(3)
-    )
-    unused_first, norm_one_pull = jax.vjp(layer_norm, inputs, gain_one, shift_one)
-    input_rows_grad, grad_gain_one, grad_shift_one = norm_one_pull(normed_grad)
-    input_grad = (middle_grad + input_rows_grad).astype(jnp.bfloat16)
-    small_grad = jnp.concatenate(
-        [
-            grad_gain_one,
-            grad_shift_one,
-            grad_gain_two,
-            grad_shift_two,
-            grad_bias_qkv[0, 0],
-            grad_bias_qkv[2, 0],
-            grad_bias_out.reshape(-1),
-            grad_bias_down,
-            grad_bias_up.reshape(-1),
-        ]
+    blank = jnp.zeros((2, D), jnp.float32)
+    others = jnp.concatenate(
+        [blank, sums[0:2], blank, grad_bias_out[0], sums[2:3], grad_bias_up[:, 0]], axis=0
+    )
+    mine_qkv, mine_small, input_grad = project_back(
+        n_dp, n_fsdp, tokens, normed, projected_grad, qkv_full, middle_grad, gain_one[None], others, 4
     )
     devices = n_dp * n_fsdp
-    small_split = jnp.pad(small_grad.astype(jnp.bfloat16).reshape(devices, -1), ((0, 0), (0, 2048 - 9216 // devices)))
-    small_split = small_split.reshape(4, 2, 2, 2, 16, 128).transpose(2, 3, 0, 1, 4, 5)
-    mine_qkv, mine_small = scatter_all(n_dp, n_fsdp, (split_qkv, small_split), ("j", "j"), 4)
-    mine = jnp.concatenate([mine_qkv.astype(jnp.bfloat16), mine_out, mine_up, mine_down], axis=0)
+    mine = jnp.concatenate([mine_qkv] + [part.reshape(-1, 48, 384) for part in (mine_out, mine_up, mine_down)], axis=0)
     numbers = jnp.arange(BLOCKS, dtype=jnp.int32)
     ranks = jnp.arange(devices, dtype=jnp.int32)
     blocks_of = jnp.sum(jnp.where(owners[None, :] == ranks[:, None], numbers[None, :], 0), axis=1).astype(jnp.int32)
     rank = lax.axis_index(("dp", "fsdp"))
     owning = jnp.any(owners == rank)
     flags = jnp.stack([owning, blocks_of[rank] >= 4 + FF // D]).astype(jnp.int32)
-    small_pieces, *tiles, new_statistics = owner_exchange(
-        n_dp, n_fsdp, blocks_of, owners, flags, mine.reshape(BLOCKS, 48, 384), mine_small[:8],
-        statistics[0], inverse_roots[0], 5,
-    )
-    grad_tiles, step_tiles = tiles[:4], tiles[4:]
-    column_index = lax.axis_index("fsdp")
-    shard_qkv, shard_out, shard_up, shard_down = tiles_of(grad_tiles, column_index)
-    tile_qkv, tile_out, tile_up, tile_down = tiles_of(step_tiles, column_index)
-    new_qkv = qkv_weight - step_rate * tile_qkv
-    new_out = out_weight - step_rate * tile_out
-    new_up = up_weight - step_rate * tile_up
-    new_down = down_weight - step_rate * tile_down
-    whole_small = small_pieces.reshape(devices, 1024)[:, : 9216 // devices].reshape(-1)
-    new_small = small_params - small_rate * whole_small * lax.rsqrt(
-        jnp.mean(whole_small * whole_small) + 1e-06
-    )
+    masters = (qkv_weight, out_weight, up_weight, down_weight)
+    *results, whole_small, new_small, new_statistics = owner_exchange(
+        n_dp, n_fsdp, blocks_of, owners, flags, mine, mine_small, statistics[0], inverse_roots[0],
+        masters, small_params.reshape(-1, 128), (step_rate, small_rate), 5,
+    )
+    shard_qkv, shard_out, shard_up, shard_down, new_qkv, new_out, new_up, new_down = results
+    whole_small, new_small = whole_small.reshape(-1), new_small.reshape(-1)
     return (
         layer_rows,
         input_grad,
@@ -1546,15 +1654,6 @@
     rows, columns = pieces.shape[-2:]
     folded = pieces.reshape(pieces.shape[0] * pieces.shape[1], -1, columns)
     return folded.transpose(1, 0, 2).reshape(folded.shape[1], -1)
-
-
-def tiles_of(tiles, column_index):
-    qkv, out, up, down = tiles
-    band = lambda halves: halves.astype(jnp.float32).transpose(1, 0, 2).reshape(96, D)
-    qkv, out = band(qkv), band(out)
-    qkv = jnp.where(column_index % 2 == 1, qkv[:, 192:], qkv[:, : D - 192])
-    out = lax.dynamic_slice_in_dim(out, column_index * 192, 192, 1)
-    return qkv, out, band(up), down.astype(jnp.float32).T
 
 
 def solution(mesh):

time: 419 us -> 386 us (0.921)
  other arithmetic: 26.2 us -> 11.3 us
  matrix products: 14 us -> 0 us
    dot_general x4 -> x0, matrix products: 14 us -> none  [the longest x1 7.54 us: row_dot(): return jnp.dot(left, right, preferred_element_type=jnp.float32)]
    pallas_call x1, Pallas kernels: 85.9 us -> 75.9 us  [grads_attend_back(): pl.pallas_call(kernel, out_shape=[jax.ShapeDtypeStruct((3, slots, d), low...]
    unnamed x84 -> x46, local copies, waits for them, and re-layouts: 8.17 us -> 16.8 us
    reduce_sum x4 -> x0, other arithmetic: 6.59 us -> none  [the longest x1 2.19 us: layer_norm(): return center * lax.rsqrt(spread + 1e-06) * scale_row + shift_row]
    reshape x2 -> x1, local copies, waits for them, and re-layouts: 7.84 us -> 1.68 us  [whole_of(): folded = pieces.reshape(pieces.shape[0] * pieces.shape[1], -1, columns)]
    pallas_call x4 -> x3, Pallas kernels: 177 us -> 183 us  [the longest x1 77.7 us: owner_exchange(): pl.pallas_call(kernel, out_shape=[jax.ShapeDtypeStruct(a.shape, jnp.float...]
    convert_element_type x3 -> x0, other arithmetic: 5.3 us -> none  [the longest x1 3.71 us: local_staged(): input_grad = (middle_grad + input_rows_grad).astype(jnp.bfloat16)]
where the time goes in v4:
time: 386 us; the launch traced here: 380 us
  Pallas kernels  340 us (88%)
  local copies, waits for them, and re-layouts  26.1 us (7%)
  other arithmetic  11.3 us (3%)
    pallas_call x1, Pallas kernels, owner_exchange(): pl.pallas_call(kernel, out_shape=[jax.ShapeDtypeStruct(a.shape, jnp.float...  77.7 us
    pallas_call x1, Pallas kernels, grads_attend_back(): pl.pallas_call(kernel, out_shape=[jax.ShapeDtypeStruct((3, slots, d), low...  75.9 us
    pallas_call x1, Pallas kernels, project_attend(): pl.pallas_call(kernel, out_shape=[jax.ShapeDtypeStruct((slots, d), low),...  61.1 us
    pallas_call x1, Pallas kernels, project_back(): pl.pallas_call(kernel, out_shape=[shape((n_blocks, 48, 384), low), shape(...  44.3 us
    pallas_call x1, Pallas kernels, gather_first(): pl.pallas_call(kernel, out_shape=[jax.ShapeDtypeStruct(grid.shape(o, *s.s...  42.7 us
    pallas_call x1, Pallas kernels, middle_layer(): pl.pallas_call(middle_kernel, out_shape=[shape((count, d), low), shape((c...  38.3 us
    unnamed x46, local copies, waits for them, and re-layouts  16.8 us

profile of v4, /device:TPU:27, one launch (start us, length us, event | category | flops | bytes accessed | tf_op | source)
XLA Modules:
  0.0 379.9 jit_solution(17116929573897107582)
XLA Ops:
  0.6 0.8 fusion
  2.7 1.6 convert_element_type.17.refs_2_
  4.3 1.6 convert_element_type.15.refs_0_
  6.0 1.5 convert_element_type.16.refs_1_
  7.5 42.7 %gather_first.1 = (bf16[2,2,4,2,96,576]{5,4,3,2,1,0:T(8,128)(2,1)}, bf16[2,2,4,2,96,192]{5,4,3,2,1,0:T(8,128)(2,1)}, bf16[2,2,4,2,96,768]{5,4,3,2,1,0:T(8,128)(2,1)}) custom-call(bf16[96,576]{1,0:T(8,128)(2,1)} %convert_element_type.15.refs_0_, bf16[96,192]{1,0:T(8,128)(2,1)} %convert_element_type.16.refs_1_, bf16[96,768]{1,0:T(8,128)(2,1)} %convert_element_type.17.refs_2_), custom_call_target="tpu_custom_call" | custom-call | tf_op jit(solution)/shard_map/gather_first/pallas_call | solution.py:344
  50.8 1.6 convert_bitcast_fusion.refs_2_
  52.5 61.1 %project_attend.1 = (bf16[1024,768]{1,0:T(8,128)(2,1)}, bf16[1024,2304]{1,0:T(8,128)(2,1)}, bf16[768,2304]{1,0:T(8,128)(2,1)}, bf16[1024,768]{1,0:T(8,128)(2,1)}...) custom-call(s32[1]{0:T(128)S(6)} %copy.55.count_ref, ...), custom_call_target="tpu_custom_call", output_to_operand_aliasing={{5}: (5, {}), {6}: (6, {})} | custom-call | tf_op jit(solution)/shard_map/project_attend/pallas_call | solution.py:597
  113.7 1.7 copy.35
  115.3 1.5 copy.36.out_w
  118.1 38.3 %middle_layer.1 = (bf16[1024,768]{1,0:T(8,128)(2,1)}, bf16[1024,768]{1,0:T(8,128)(2,1)}, bf16[1024,3072]{1,0:T(8,128)(2,1)}, bf16[1024,3072]{1,0:T(8,128)(2,1)},...) custom-call(bf16[1024,768]{1,0:T(8,128)(2,1)} %x_h.1, ...), custom_call_target="tpu_custom_call" | custom-call | tf_op jit(solution)/shard_map/middle_layer/pallas_call | solution.py:1026
  156.4 75.9 %grads_attend_back.1 = (bf16[3,1024,768]{2,1,0:T(8,128)(2,1)}, bf16[192,384]{1,0:T(8,128)(2,1)}, bf16[192,384]{1,0:T(8,128)(2,1)}, bf16[48,384]{1,0:T(8,128)(2,1...) custom-call(s32[1]{0:T(128)S(6)} %copy.55.count_ref, bf16[1024,2304]{1,0:T(8,128)(2,1)} %get-tuple-element.61.q_ref.k_ref.v_ref, ...), custom_call_target="tpu_custom_call" | custom-call | tf_op jit(solution)/shard_map/grads_attend_back/pallas_call | solution.py:707
  233.0 0.7 slice.53
  233.8 0.7 slice.54
  234.5 1.9 concatenate.10.others_ref
  236.5 44.3 %project_back.1 = (bf16[3,48,384]{2,1,0:T(8,128)(2,1)}, bf16[16,128]{1,0:T(8,128)(2,1)}, bf16[1024,768]{1,0:T(8,128)(2,1)}) custom-call(bf16[1024,768]{1,0:T(8,128)(2,1)} %x_h.1, bf16[1024,768]{1,0:T(8,128)(2,1)} %get-tuple-element.60.normed_h, bf16[3,1024,768]{2,1,0:T(8,128)(2,1)} %get-tuple-element.68.dp_h, bf16[768,2304]{1,0:T(8,128)(2,1)} %get-tuple-element.69.weight_h, ...), custom_call_target="tpu_custom_call" | custom-call | tf_op jit(solution)/shard_map/project_back/pallas_call | solution.py:1112
  280.8 1.7 pad_maximum_fusion.u_ref
  284.5 1.2 add_convert_fusion.flags_ref
  285.7 0.9 copy.37.w_down
  286.7 77.7 %owner_exchange.1 = (f32[96,576]{1,0:T(8,128)}, f32[96,192]{1,0:T(8,128)}, f32[96,768]{1,0:T(8,128)}, f32[384,192]{1,0:T(8,128)}, f32[96,576]{1,0:T(8,128)}, /*i...) custom-call(s32[32]{0:T(128)} %copy-done.15, ...), custom_call_target="tpu_custom_call" | custom-call | tf_op jit(solution)/shard_map/owner_exchange/pallas_call | solution.py:913
  364.5 1.9 copy.38
  366.4 1.9 copy.39
  368.2 1.1 copy.56
  370.7 0.7 copy.59
  372.1 4.9 %copy.61 = f32[1,2,768,768]{3,2,1,0:T(8,128)} copy(f32[1,2,768,768]{3,2,1,0:T(8,128)} %bitcast.27) | data formatting | bytes 9437184
  (58 shorter events, 9.2 us)
Async XLA Ops:
  1.5 112.2 %copy-start.13 = (f32[1,768]{1,0:T(1,128)}, f32[1,768]{1,0:T(1,128)S(1)}, u32[]{:S(2)}) copy-start(f32[1,768]{1,0:T(1,128)S(1)} %stack.31.gain_ref) | copy-start | bytes 9220
  113.6 3.8 %slice-start = ((f32[9216]{0:T(1024)}), f32[3072]{0:T(1024)S(1)}, s32[]{:S(2)}) async-start(f32[9216]{0:T(1024)} %param.18), calls=%async_computation | async-start | bytes 24576 | tf_op jit(solution)/shard_map/slice | solution.py:1155
  236.4 44.3 %copy-start.6 = (bf16[192,384]{1,0:T(8,128)(2,1)S(1)}, bf16[192,384]{1,0:T(8,128)(2,1)}, u32[]{:S(2)}) copy-start(bf16[192,384]{1,0:T(8,128)(2,1)} %get-tuple-element.78) | copy-start | bytes 442372
  236.5 44.3 %copy-start.7 = (bf16[192,384]{1,0:T(8,128)(2,1)S(1)}, bf16[192,384]{1,0:T(8,128)(2,1)}, u32[]{:S(2)}) copy-start(bf16[192,384]{1,0:T(8,128)(2,1)} %get-tuple-element.77) | copy-start | bytes 442372
  236.5 44.4 %copy-start.10 = (bf16[48,384]{1,0:T(8,128)(2,1)S(1)}, bf16[48,384]{1,0:T(8,128)(2,1)}, u32[]{:S(2)}) copy-start(bf16[48,384]{1,0:T(8,128)(2,1)} %get-tuple-element.76) | copy-start | bytes 110596
  236.5 46.1 %copy-start.14 = (s32[12]{0:T(128)S(1)}, s32[12]{0:T(128)}, u32[]{:S(2)}) copy-start(s32[12]{0:T(128)} %owners_ref.1) | copy-start | bytes 148
  236.5 49.3 %copy-start.1 = (f32[384,192]{0,1:T(8,128)S(1)}, f32[384,192]{0,1:T(8,128)}, u32[]{:S(2)}) copy-start(f32[384,192]{0,1:T(8,128)} %param.17) | copy-start | bytes 884740
  282.6 4.0 %copy-start.15 = (s32[32]{0:T(128)}, s32[32]{0:T(128)S(1)}, u32[]{:S(2)}) copy-start(s32[32]{0:T(128)S(1)} %select_reduce_fusion.of_ref) | copy-start | bytes 388
  286.7 81.6 %copy-start = (bf16[1024,768]{1,0:T(8,128)(2,1)S(1)}, bf16[1024,768]{1,0:T(8,128)(2,1)}, u32[]{:S(2)}) copy-start(bf16[1024,768]{1,0:T(8,128)(2,1)} %get-tuple-element.152) | copy-start | bytes 4718596
  364.4 5.0 %copy-start.5 = (f32[96,576]{1,0:T(8,128)S(1)}, f32[96,576]{1,0:T(8,128)}, u32[]{:S(2)}) copy-start(f32[96,576]{1,0:T(8,128)} %get-tuple-element.153) | copy-start | bytes 663556
  364.4 5.7 %copy-start.9 = (f32[96,192]{1,0:T(8,128)S(1)}, f32[96,192]{1,0:T(8,128)}, u32[]{:S(2)}) copy-start(f32[96,192]{1,0:T(8,128)} %get-tuple-element.154) | copy-start | bytes 221188
  364.4 6.3 %copy-start.3 = (f32[96,768]{1,0:T(8,128)S(1)}, f32[96,768]{1,0:T(8,128)}, u32[]{:S(2)}) copy-start(f32[96,768]{1,0:T(8,128)} %get-tuple-element.155) | copy-start | bytes 884740
  364.4 7.0 %copy-start.12 = (f32[72,128]{1,0:T(8,128)S(1)}, f32[72,128]{1,0:T(8,128)}, u32[]{:S(2)}) copy-start(f32[72,128]{1,0:T(8,128)} %get-tuple-element.84) | copy-start | bytes 110596
  372.1 4.9 %copy-start.4 = (f32[96,576]{1,0:T(8,128)S(1)}, f32[96,576]{1,0:T(8,128)}, u32[]{:S(2)}) copy-start(f32[96,576]{1,0:T(8,128)} %get-tuple-element.159) | copy-start | bytes 663556
  372.1 5.6 %copy-start.8 = (f32[96,192]{1,0:T(8,128)S(1)}, f32[96,192]{1,0:T(8,128)}, u32[]{:S(2)}) copy-start(f32[96,192]{1,0:T(8,128)} %get-tuple-element.160) | copy-start | bytes 221188
  372.1 6.2 %copy-start.2 = (f32[96,768]{1,0:T(8,128)S(1)}, f32[96,768]{1,0:T(8,128)}, u32[]{:S(2)}) copy-start(f32[96,768]{1,0:T(8,128)} %get-tuple-element.161) | copy-start | bytes 884740
  372.1 7.0 %copy-start.11 = (f32[72,128]{1,0:T(8,128)S(1)}, f32[72,128]{1,0:T(8,128)}, u32[]{:S(2)}) copy-start(f32[72,128]{1,0:T(8,128)} %get-tuple-element.90) | copy-start | bytes 110596

commit v5 on v4

--- a/solution.py
+++ b/solution.py
@@ -322,31 +322,33 @@
             for j, (n, path, rows) in enumerate(jobs)]
 
 
-def gather_first(n_dp, n_fsdp, shards, orders, share, collective_id):
+def gather_first(n_dp, n_fsdp, shards, orders, plan, collective_id):
     grid = Grid(n_dp, n_fsdp)
     count = len(shards)
-    jobs = job_list([shards[0].shape]) + [(n + 1, p, r) for n, p, r in job_list([s.shape for s in shards[1:]], share)]
+    jobs, order, wholes = plan
 
     def kernel(*refs):
         g = grid.here()
+        low = refs[2 * count : 3 * count]
+        low[0][...] = refs[0][...].astype(jnp.bfloat16)
         g.barrier()
-        whole, *others = gather_jobs(g, orders, jobs, refs[:count], refs[count : 2 * count], refs[2 * count :])
-        whole.step(0)
-        whole.step(1)
-        for job in others:
-            job.step(0)
-        whole.step(2)
-        whole.step(3)
-        for job in others:
+        work = gather_jobs(g, orders, jobs, low, refs[count : 2 * count], refs[3 * count :])
+        work[0].step(0)
+        for n in range(1, count):
+            low[n][...] = refs[n][...].astype(jnp.bfloat16)
+        for job, step in order:
+            work[job].step(step)
+        for job in work[wholes:]:
             job.pause()
-        whole.finish()
+        for job in work[:wholes]:
+            job.finish()
 
     return pl.pallas_call(
         kernel,
-        out_shape=[jax.ShapeDtypeStruct(grid.shape(o, *s.shape), s.dtype) for s, o in zip(shards, orders)],
-        in_specs=[ANY] * count,
+        out_shape=[jax.ShapeDtypeStruct(grid.shape(o, *s.shape), jnp.bfloat16) for s, o in zip(shards, orders)],
+        in_specs=[VM] * count,
         out_specs=[ANY] * count,
-        scratch_shapes=gather_scratch(grid, len(jobs)),
+        scratch_shapes=[pltpu.VMEM(s.shape, jnp.bfloat16) for s in shards] + gather_scratch(grid, len(jobs)),
         compiler_params=pltpu.CompilerParams(collective_id=collective_id, has_side_effects=True),
         name="gather_first",
     )(*shards)
@@ -535,13 +537,15 @@
     jobs = plan["jobs"]
     waits = [job[0] < begun for job in jobs]
     shapes = [jax.ShapeDtypeStruct(p.shape, p.dtype) for p in pieces]
-    shapes += [jax.ShapeDtypeStruct(grid.shape(o, *a.shape), a.dtype) for a, o in zip(fresh, orders[begun:])]
+    turned = [a.shape[::-1] for a in fresh]
+    shapes += [jax.ShapeDtypeStruct(grid.shape(o, *a), jnp.bfloat16) for a, o in zip(turned, orders[begun:])]
 
     def kernel(count_ref, x, w_pieces, rows, bias_ref, *refs):
         (h_ref, p_ref, w_ref, o_ref, lse_ref), outs = refs[count : count + 5], refs[count + 5 : 2 * count + 5]
         projected, q_heads, v_turned = refs[2 * count + 5 : 2 * count + 8]
+        low_fresh = refs[2 * count + 8 : 2 * count + 8 + len(fresh)]
         g = grid.here()
-        work = gather_jobs(g, orders, jobs, outs[:begun] + refs[begun:count], outs, refs[2 * count + 8 :])
+        work = gather_jobs(g, orders, jobs, outs[:begun] + low_fresh, outs, refs[2 * count + 8 + len(fresh) :])
         step = pl.program_id(0)
 
         def run(when):
@@ -553,6 +557,8 @@
 
         @pl.when(step == 0)
         def _():
+            for ref, master in zip(low_fresh, refs[begun:count]):
+                ref[...] = master[...].T.astype(jnp.bfloat16)
             g.barrier()
 
         for when in range(head + pairs):
@@ -601,12 +607,13 @@
                    jax.ShapeDtypeStruct((pairs, 2, slots), jnp.float32)] + shapes,
         grid_spec=pltpu.PrefetchScalarGridSpec(
             num_scalar_prefetch=1, grid=(head + pairs,),
-            in_specs=[row(d), whole(weight_pieces), whole(norm_rows), whole(bias)] + [ANY] * count,
+            in_specs=[row(d), whole(weight_pieces), whole(norm_rows), whole(bias)] + [ANY] * begun + [whole(a) for a in fresh],
             out_specs=[row(d), row(width), pl.BlockSpec((d, width), lambda s, n: (0, 0)),
                        pl.BlockSpec((slots, PAIR), lambda s, n: (0, pair_at(s))),
                        pl.BlockSpec((1, 2, slots), lambda s, n: (pair_at(s), 0, 0))] + [ANY] * count,
             scratch_shapes=[pltpu.VMEM((slots, width), low), pltpu.VMEM((2, slots, PAIR), low),
-                            pltpu.VMEM((2, PAIR, slots), low)] + gather_scratch(grid, len(jobs))),
+                            pltpu.VMEM((2, PAIR, slots), low)] + [pltpu.VMEM(a, low) for a in turned]
+            + gather_scratch(grid, len(jobs))),
         input_output_aliases={5 + n: 5 + n for n in range(begun)},
         compiler_params=pltpu.CompilerParams(vmem_limit_bytes=56 * 1024 * 1024, collective_id=collective_id,
                                              has_side_effects=True),
@@ -614,14 +621,18 @@
     )(counts, tokens, weight_pieces, norm_rows, bias, *pieces, *fresh)
 
 
+FIRST_PLAN = (
+    [(0, 0, pl.ds(0, 48)), (0, 0, pl.ds(48, 48)), (1, 0, pl.ds(0, 96)), (2, 0, pl.ds(0, 64)), (2, 1, pl.ds(64, 32))],
+    [(0, 1), (1, 0), (0, 2), (1, 1), (2, 0), (3, 0), (4, 0), (0, 3), (1, 2), (1, 3)],
+    2,
+)
 FORWARD_PLAN = {
-    "jobs": [(0, 0, pl.ds(0, 96)), (1, 0, pl.ds(0, 96)), (2, 0, pl.ds(0, 192))],
-    0: [(0, 1), (1, 1), (2, 0)],
-    2: [(0, 2)],
-    5: [(1, 2), (0, 3)],
-    7: [(2, 1)],
-    9: [(2, 2)],
-    "end": [(1, 3), (2, 3)],
+    "jobs": [(0, 0, pl.ds(0, 96)), (1, 0, pl.ds(0, 64)), (1, 1, pl.ds(64, 32)), (2, 0, pl.ds(0, 192))],
+    0: [(0, 1), (1, 1), (3, 0), (2, 1)],
+    3: [(0, 2)],
+    5: [(1, 2), (0, 3), (2, 2)],
+    7: [(3, 1)],
+    "end": [(1, 3), (3, 2), (2, 3), (3, 3)],
 }
 
 
@@ -640,8 +651,7 @@
     head = 2 * panels + 1
     grid = Grid(n_dp, n_fsdp)
     sizes = [(panels * 48, 384), (panels * 48, 384), (48, 384)]
-    half = panels * 24
-    jobs = [(n, 0, pl.ds(at, half)) for n in range(2) for at in (0, half)] + [(2, 0, pl.ds(0, 48))]
+    jobs = plan["jobs"]
     steps = slots // size
 
     def kernel(count_ref, q_ref, k_ref, v_ref, o_ref, do_ref, lse_ref, dy, z, h2, du, o_all, db, out_ref, *refs):
@@ -727,6 +737,7 @@
 
 
 BACKWARD_PLAN = {
+    "jobs": [(n, 0, pl.ds(at, 96)) for n in range(2) for at in (0, 96)] + [(2, 0, pl.ds(0, 48))],
     (2, 0): [(0, 0)],
     (4, 0): [(1, 0)],
     (5, 0): [(0, 1)],
@@ -821,20 +832,34 @@
             jnp.concatenate([up[0].astype(wide), up[1].astype(wide)], axis=1), down[...].astype(wide).T]
 
 
-def owner_exchange(n_dp, n_fsdp, blocks_of, owners, flags, u, small, stats, roots, masters, small_params, rates, collective_id):
+def owner_exchange(n_dp, n_fsdp, owners, mine, small, roots, collective_id):
     grid = Grid(n_dp, n_fsdp)
     count = n_dp * n_fsdp
+    n_blocks = owners.shape[0]
+    d = roots.shape[1]
     spread_lanes = 12
 
-    def kernel(of_ref, owners_ref, flags_ref, u_ref, small_ref, w_qkv, w_out, w_up, w_down, params, stats_hbm, roots_hbm,
-               g_qkv, g_out, g_up, g_down, n_qkv, n_out, n_up, n_down, g_small, n_small, new_stats_hbm,
-               all_small, qkv, out, up, down, s_qkv, s_out, s_up, s_down, slots, got, got_steps, u_steps, stats, roots, block, turned, local, send, recv):
+    def kernel(owners_ref, qkv_ref, out_ref, up_ref, down_ref, small_ref, roots_hbm,
+               qkv, out, up, down, s_qkv, s_out, s_up, s_down, all_small, block, turned,
+               u, slots, got, got_steps, u_steps, roots, local, send, recv):
         g = grid.here()
         me, ranks, peers = meet_all(g, n_dp, n_fsdp)
-        loads = [pltpu.make_async_copy(stats_hbm, stats, local.at[0]), pltpu.make_async_copy(roots_hbm, roots, local.at[1])]
+        load = pltpu.make_async_copy(roots_hbm, roots, local.at[0])
+        load.start()
+        first = 0
+        for ref in (qkv_ref, out_ref, up_ref, down_ref):
+            part = ref.shape[0] // 48
+            u[first : first + part] = ref[...].reshape(part, 48, 384)
+            first += part
+
+        def owned(n):
+            found = 0
+            for b in range(n_blocks):
+                found = jnp.where(owners_ref[b] == n, b, found)
+            return found
 
         def fill(n, carry):
-            slots[n] = u_ref[of_ref[n]]
+            slots[n] = u[owned(n)]
             return carry
 
         lax.fori_loop(0, count, fill, 0)
@@ -846,25 +871,20 @@
             step_copies.append(remote(slots.at[rank], got_steps.at[me], send, recv, lane + 2, peer))
             lane += 3
         start_all(copies)
-        for load in loads:
-            load.start()
         got[me] = slots[me]
         all_small[me] = small_ref[...]
-        for load in loads:
-            load.wait()
+        load.wait()
+        kind = jnp.where(owned(me) >= 8, 1, 0)
         arrived(copies)
         sent(copies)
-        spread = Spread(g, u_ref, (qkv, out, up, down), send, recv, lane)
+        spread = Spread(g, u, (qkv, out, up, down), send, recv, lane)
         spread.start()
         start_all(small_copies)
-
-        own, kind = flags_ref[0] == 1, flags_ref[1]
         for turn in range(2):
             for n, place in enumerate(places()):
                 row, column = piece_rows(turn, *place)
                 (turned if turn else block)[row : row + 48, column : column + 384] = got[n]
         block[...] = jnp.where(kind == 1, turned[...], block[...])
-        turned[...] = block[...].astype(jnp.float32).T.astype(jnp.bfloat16)
         left = plain_dot(roots[kind].astype(jnp.bfloat16), block[...]).astype(jnp.bfloat16)
         step = plain_dot(left, roots[1 - kind].astype(jnp.bfloat16)).astype(jnp.bfloat16)
         for n, place in enumerate(places()):
@@ -874,92 +894,95 @@
                                  step[row : row + 48, column : column + 384])
         start_all(step_copies)
         got_steps[me] = slots[me]
-        rows_by = last_dot(block[...], block[...])
-        columns_by = last_dot(turned[...], turned[...])
-        for side in range(2):
-            mine, other = (rows_by, columns_by) if side == 0 else (columns_by, rows_by)
-            moved = 0.5 * stats[side] + 0.5 * jnp.where(kind == 1, other, mine)
-            stats[side] = jnp.where(own, moved, stats[side])
-        store = pltpu.make_async_copy(stats, new_stats_hbm, local.at[0])
-        store.start()
+        wide = block[...].astype(jnp.float32)
+        wide_turned = wide.T
+        block[...] = jnp.where(kind == 1, wide_turned, wide).astype(jnp.bfloat16)
+        turned[...] = jnp.where(kind == 1, wide, wide_turned).astype(jnp.bfloat16)
         spread.finish()
-        for ref, value in zip((g_qkv, g_out, g_up, g_down), tile_values(g, (qkv, out, up, down))):
-            ref[...] = value
         arrived(small_copies)
-        lines = params.shape[0]
-        total = jnp.concatenate([all_small[n].astype(jnp.float32) for n in range(-(-lines // 16))], axis=0)[:lines]
-        g_small[...] = total
-        mean = jnp.sum(total * total) * (1.0 / (lines * 128))
-        n_small[...] = params[...] - rates[1] * total * lax.rsqrt(jnp.full((1, 128), mean + 1e-06, jnp.float32))
         arrived(step_copies)
 
         def pick(n, carry):
             u_steps[n] = got_steps[owners_ref[n]]
             return carry
 
-        lax.fori_loop(0, 12, pick, 0)
+        lax.fori_loop(0, n_blocks, pick, 0)
         back = Spread(g, u_steps, (s_qkv, s_out, s_up, s_down), send, recv, lane + spread_lanes)
         back.start()
         sent(small_copies + step_copies)
         back.finish()
-        new = tile_values(g, (s_qkv, s_out, s_up, s_down))
-        for ref, master, value in zip((n_qkv, n_out, n_up, n_down), (w_qkv, w_out, w_up, w_down), new):
-            ref[...] = master[...] - rates[0] * value
-        store.wait()
 
     lanes = 3 * (count - 1) + 2 * spread_lanes
     low = jnp.bfloat16
-    smem = pl.BlockSpec(memory_space=pltpu.SMEM)
+    pieces = pltpu.VMEM((count,) + PIECE, low)
     return pl.pallas_call(
         kernel,
-        out_shape=[jax.ShapeDtypeStruct(a.shape, jnp.float32) for a in (*masters, *masters, small_params, small_params, stats)],
-        in_specs=[smem, smem, smem] + [VM] * 7 + [ANY, ANY],
-        out_specs=[VM] * 10 + [ANY],
-        scratch_shapes=[pltpu.VMEM((count,) + small.shape, low)] + [pltpu.VMEM(t.shape, low) for t in TILES * 2]
-        + [pltpu.VMEM((count,) + PIECE, low), pltpu.VMEM((count,) + PIECE, low),
-                        pltpu.VMEM((count,) + PIECE, low), pltpu.VMEM((12,) + PIECE, low),
-                        pltpu.VMEM(stats.shape, jnp.float32), pltpu.VMEM(roots.shape, jnp.float32),
-                        pltpu.VMEM(stats.shape[1:], low), pltpu.VMEM(stats.shape[1:], low),
-                        pltpu.SemaphoreType.DMA((2,)), pltpu.SemaphoreType.DMA((lanes,)), pltpu.SemaphoreType.DMA((lanes,))],
+        out_shape=TILES + TILES + [jax.ShapeDtypeStruct((count,) + small.shape, low), jax.ShapeDtypeStruct((d, d), low),
+                                   jax.ShapeDtypeStruct((d, d), low)],
+        in_specs=[pl.BlockSpec(memory_space=pltpu.SMEM)] + [VM] * 5 + [ANY],
+        out_specs=[VM] * 11,
+        scratch_shapes=[pltpu.VMEM((n_blocks,) + PIECE, low), pieces, pieces, pieces, pltpu.VMEM((n_blocks,) + PIECE, low),
+                        pltpu.VMEM(roots.shape, jnp.float32), pltpu.SemaphoreType.DMA((1,)),
+                        pltpu.SemaphoreType.DMA((lanes,)), pltpu.SemaphoreType.DMA((lanes,))],
         compiler_params=pltpu.CompilerParams(collective_id=collective_id, has_side_effects=True,
                                              vmem_limit_bytes=56 * 1024 * 1024),
         name="owner_exchange",
-    )(blocks_of, owners, flags, u, small, *masters, small_params, stats, roots)
-
-
-def block_grads_kernel(turned_blocks, left, right, out, sums, left_turned):
-    @pl.when(pl.program_id(0) == 0)
-    def _():
-        left_turned[...] = left[...].astype(jnp.float32).T.astype(jnp.bfloat16)
-
-    values = right[...].reshape(right.shape[-2:])
-    grad = plain_dot(left_turned[...], values).astype(jnp.bfloat16)
-    for z, x, y, c in places():
-        row, column = piece_rows(turned_blocks, z, x, y, c)
-        out[y, c, z, x] = grad[row : row + 48, column : column + 384]
-    sums[...] = jnp.sum(values.astype(jnp.float32), axis=0).reshape(sums.shape)
-
-
-def block_grads(left, right, turned_blocks):
-    rows, d = left.shape
-    if right.ndim == 3:
-        count = right.shape[0]
-        spec = pl.BlockSpec((1, rows, d), lambda b: (b, 0, 0))
-    else:
-        count = right.shape[1] // d
-        spec = pl.BlockSpec((rows, d), lambda b: (0, b))
+    )(owners, *mine, small, roots)
+
+
+def finish_step(n_dp, n_fsdp, owners, exchanged, masters, small_params, stats, rates, parts=4):
+    grid = Grid(n_dp, n_fsdp)
+    tiles, all_small, block, turned = exchanged[:8], *exchanged[8:]
+    d = block.shape[0]
+    rows = d // parts
+
+    def kernel(owners_ref, qkv, out, up, down, s_qkv, s_out, s_up, s_down, all_small, block, turned,
+               w_qkv, w_out, w_up, w_down, params, stats_ref,
+               g_qkv, g_out, g_up, g_down, n_qkv, n_out, n_up, n_down, g_small, n_small, new_stats):
+        g = grid.here()
+        step = pl.program_id(0)
+        me = (g.z * g.X + g.x) * n_fsdp + g.y * 2 + g.c
+        own = owners_ref[0] == me
+        for n in range(1, owners.shape[0]):
+            own = own | (owners_ref[n] == me)
+
+        @pl.when(step == 0)
+        def _():
+            values = tile_values(g, (qkv, out, up, down))
+            for ref, value in zip((g_qkv, g_out, g_up, g_down), values):
+                ref[...] = value
+            steps = tile_values(g, (s_qkv, s_out, s_up, s_down))
+            for ref, master, value in zip((n_qkv, n_out, n_up, n_down), (w_qkv, w_out, w_up, w_down), steps):
+                ref[...] = master[...] - rates[0] * value
+            lines = params.shape[0]
+            total = jnp.concatenate([all_small[n].astype(jnp.float32) for n in range(-(-lines // 16))], axis=0)[:lines]
+            g_small[...] = total
+            mean = jnp.sum(total * total) * (1.0 / (lines * 128))
+            n_small[...] = params[...] - rates[1] * total * lax.rsqrt(jnp.full((1, 128), mean + 1e-06, jnp.float32))
+
+        @pl.when(own)
+        def _():
+            at = pl.ds(pl.multiple_of(step * rows, rows), rows)
+            new_stats[0] = 0.5 * stats_ref[0] + 0.5 * last_dot(block[at, :], block[...])
+            new_stats[1] = 0.5 * stats_ref[1] + 0.5 * last_dot(turned[at, :], turned[...])
+
+        @pl.when(jnp.logical_not(own))
+        def _():
+            new_stats[...] = stats_ref[...]
+
+    whole = lambda a: pl.BlockSpec(a.shape, lambda s, n: (0,) * len(a.shape))
+    banded = pl.BlockSpec((2, rows, d), lambda s, n: (0, s, 0))
+    results = [jax.ShapeDtypeStruct(a.shape, jnp.float32) for a in (*masters, *masters, small_params, small_params)]
     return pl.pallas_call(
-        partial(block_grads_kernel, turned_blocks),
-        out_shape=[jax.ShapeDtypeStruct((2, 2, 4, 2, count * 48, 384), jnp.bfloat16),
-                   jax.ShapeDtypeStruct((count, 1, d), jnp.float32)],
-        grid=(count,),
-        in_specs=[pl.BlockSpec((rows, d), lambda b: (0, 0)), spec],
-        out_specs=[pl.BlockSpec((2, 2, 4, 2, 48, 384), lambda b: (0, 0, 0, 0, b, 0)),
-                   pl.BlockSpec((1, 1, d), lambda b: (b, 0, 0))],
-        scratch_shapes=[pltpu.VMEM((d, rows), jnp.bfloat16)],
+        kernel,
+        out_shape=results + [jax.ShapeDtypeStruct(stats.shape, jnp.float32)],
+        grid_spec=pltpu.PrefetchScalarGridSpec(
+            num_scalar_prefetch=1, grid=(parts,),
+            in_specs=[whole(a) for a in (*exchanged, *masters, small_params)] + [banded],
+            out_specs=[whole(a) for a in results] + [banded]),
         compiler_params=pltpu.CompilerParams(vmem_limit_bytes=56 * 1024 * 1024),
-        name="block_grads",
-    )(left, right)
+        name="finish_step",
+    )(owners, *exchanged, *masters, small_params, stats)
 
 
 def centered(values):
@@ -975,8 +998,14 @@
     return (scaled - mean - unit * along) * spread
 
 
-def middle_kernel(x, attended, dy, out_w, up_w, down_w, rows, bias_up,
-                  layer, h2, active, hidden_grad, middle_grad, branch_grad, attended_grad, sums):
+def middle_kernel(x, attended, dy, out_pieces, up_w, down_w, rows, bias_up,
+                  layer, h2, active, hidden_grad, middle_grad, branch_grad, attended_grad, sums, out_w):
+    @pl.when(pl.program_id(0) == 0)
+    def _():
+        part = out_pieces.shape[2]
+        for n in range(out_pieces.shape[0]):
+            out_w[:, n * part : (n + 1) * part] = out_pieces[n]
+
     gain, shift, bias_out, bias_down = rows[0:1], rows[1:2], rows[2:3], rows[3:4]
     middle = x[...].astype(jnp.float32) + (plain_dot(attended[...], out_w[...]) + bias_out)
     unit, spread = centered(middle)
@@ -1030,21 +1059,23 @@
         grid=(count // block,),
         in_specs=[row(d), row(d), row(d)] + [whole(a) for a in (out_w, up_w, down_w, rows, bias_up)],
         out_specs=[row(d), row(d), row(ff), row(ff), row(d), row(d), row(d), pl.BlockSpec((8, d), lambda r: (0, 0))],
+        scratch_shapes=[pltpu.VMEM((d, d), low)],
         compiler_params=pltpu.CompilerParams(vmem_limit_bytes=60 * 1024 * 1024),
         name="middle_layer",
     )(tokens, attended, cotangent, out_w, up_w, down_w, rows, bias_up)
 
 
-def project_back(n_dp, n_fsdp, tokens, normed, projected_grad, weight, middle_grad, gain, others, collective_id, block=256):
+def project_back(n_dp, n_fsdp, tokens, normed, projected_grad, weight, middle_grad, gain, sums, bias_out, bias_up, plan,
+                 collective_id, block=256):
     grid = Grid(n_dp, n_fsdp)
     count, d = tokens.shape
     n_blocks = projected_grad.shape[0]
-    lines = others.shape[0]
+    lines = 8 + bias_up.shape[0]
     sizes = [(48, 384)] * n_blocks + [(16, 128)]
-    jobs = job_list(sizes)
+    jobs = plan["jobs"]
     low, wide = jnp.bfloat16, jnp.float32
 
-    def kernel(x_h, normed_h, dp_h, weight_h, middle_h, gain_ref, others_ref, mine, small, input_grad_h, *refs):
+    def kernel(x_h, normed_h, dp_h, weight_h, middle_h, gain_ref, sums_ref, bias_out_ref, bias_up_ref, mine, small, input_grad_h, *refs):
         x, h, dp, w, middle, out = refs[:6]
         left, parts, small_parts, rows, packed, local = refs[6:12]
         scratch = refs[12:]
@@ -1064,9 +1095,14 @@
             for z, px, y, c in places():
                 row, column = piece_rows(False, z, px, y, c)
                 parts[n, y, c, z, px] = grad[row : row + 48, column : column + 384]
-            work[n].step(0)
-        for line in range(lines):
-            rows[line : line + 1] = others_ref[line : line + 1]
+            for j, job in enumerate(jobs):
+                if job[0] == n:
+                    work[j].step(0)
+        rows[2:4] = sums_ref[0:2]
+        rows[6:7] = bias_out_ref[0]
+        rows[7:8] = sums_ref[2:3]
+        for n in range(lines - 8):
+            rows[8 + n : 9 + n] = bias_up_ref[n]
         rows[4:5] = jnp.sum(dp[0].astype(wide), axis=0, keepdims=True)
         rows[5:6] = jnp.sum(dp[2].astype(wide), axis=0, keepdims=True)
         for load in loads[2:]:
@@ -1081,7 +1117,6 @@
             rows[0:1] = scaled if n == 0 else rows[0:1] + scaled
             rows[1:2] = shifted if n == 0 else rows[1:2] + shifted
 
-        plan = {0: [(0, 1)], 1: [(1, 1), (2, 1)], 2: [(0, 2)], 3: [(1, 2), (2, 2)]}
         for n in range(count // block):
             for j, step in plan.get(n, []):
                 work[j].step(step)
@@ -1097,13 +1132,13 @@
         for n, (z, px, y, c) in enumerate(places()):
             if n < packed.shape[0] // 16:
                 small_parts[y, c, z, px] = packed[16 * n : 16 * n + 16].astype(low)
-        work[n_blocks].step(0)
-        for j in range(n_blocks):
-            work[j].step(3)
-            work[n_blocks].step(j + 1)
-        for n in range(n_blocks):
-            mine[n] = work[n].total().astype(low)
-        small[...] = work[n_blocks].total().astype(low)
+        for j, step in plan["end"]:
+            work[j].step(step)
+        for job, (n, path, at) in zip(work, jobs):
+            if n < n_blocks:
+                mine[n, at, :] = job.total().astype(low)
+            else:
+                small[...] = job.total().astype(low)
         for job in work:
             job.finish()
         store.wait()
@@ -1112,7 +1147,7 @@
     return pl.pallas_call(
         kernel,
         out_shape=[shape((n_blocks, 48, 384), low), shape((16, 128), low), shape((count, d), low)],
-        in_specs=[ANY] * 5 + [VM, VM],
+        in_specs=[ANY] * 5 + [VM] * 4,
         out_specs=[VM, VM, ANY],
         scratch_shapes=[pltpu.VMEM((count, d), low), pltpu.VMEM((count, d), low), pltpu.VMEM(projected_grad.shape, low),
                         pltpu.VMEM(weight.shape, low), pltpu.VMEM((count, d), wide), pltpu.VMEM((count, d), low),
@@ -1122,7 +1157,17 @@
         compiler_params=pltpu.CompilerParams(vmem_limit_bytes=60 * 1024 * 1024, collective_id=collective_id,
                                              has_side_effects=True),
         name="project_back",
-    )(tokens, normed, projected_grad, weight, middle_grad, gain, others)
+    )(tokens, normed, projected_grad, weight, middle_grad, gain, sums, bias_out, bias_up)
+
+
+TAIL_PLAN = {
+    "jobs": [(0, 0, pl.ds(0, 48)), (1, 0, pl.ds(0, 48)), (2, 0, pl.ds(0, 48)), (3, 0, pl.ds(0, 16))],
+    0: [(0, 1)],
+    1: [(1, 1), (0, 2)],
+    2: [(2, 1)],
+    3: [(1, 2), (0, 3)],
+    "end": [(3, 0), (2, 2), (3, 1), (1, 3), (3, 2), (2, 3), (3, 3)],
+}
 
 
 D = 768
@@ -1573,12 +1618,6 @@
     owners,
 ):
     n_dp, n_fsdp = sizes
-    qkv_low = qkv_weight.astype(jnp.bfloat16)
-    later = (
-        out_weight.astype(jnp.bfloat16),
-        up_weight.astype(jnp.bfloat16),
-        down_weight.astype(jnp.bfloat16).T,
-    )
     (
         gain_one,
         shift_one,
@@ -1591,17 +1630,17 @@
         bias_up,
     ) = unpack(small_params)
     orders = ("j", "j", "j", "i")
-    qkv_pieces, *begun = gather_first(n_dp, n_fsdp, (qkv_low,) + later[:2], orders[:3], 0, 1)
+    qkv_pieces, *begun = gather_first(n_dp, n_fsdp, (qkv_weight, out_weight, up_weight), orders[:3], FIRST_PLAN, 1)
     bias_qkv = jnp.concatenate([bias_query, jnp.zeros((D,), jnp.float32), bias_value])
     normed, projected, qkv_full, attended, log_totals, out_pieces, up_pieces, down_pieces = project_attend(
         n_dp, n_fsdp, counts, tokens, qkv_pieces.reshape(n_fsdp, D, 3 * D // n_fsdp), jnp.stack([gain_one, shift_one]),
-        bias_qkv[None], begun, later[2:], orders[1:], FORWARD_PLAN, 2,
+        bias_qkv[None], begun, (down_weight,), orders[1:], FORWARD_PLAN, 2,
     )
     layer_rows, normed_two, active, hidden_grad, middle_grad, branch_grad, attended_grad, sums = middle_layer(
         tokens,
         attended,
         cotangent,
-        whole_of(out_pieces),
+        out_pieces.reshape(n_fsdp, D, D // n_fsdp),
         up_pieces.reshape(n_fsdp, D, FF // n_fsdp),
         down_pieces.reshape(n_dp, D, FF // n_dp),
         jnp.stack([gain_two, shift_two, bias_out, bias_down]),
@@ -1611,25 +1650,16 @@
         n_dp, n_fsdp, counts, projected, attended, attended_grad, log_totals,
         cotangent, active, normed_two, hidden_grad, branch_grad, BACKWARD_PLAN, 3,
     )
-    blank = jnp.zeros((2, D), jnp.float32)
-    others = jnp.concatenate(
-        [blank, sums[0:2], blank, grad_bias_out[0], sums[2:3], grad_bias_up[:, 0]], axis=0
-    )
     mine_qkv, mine_small, input_grad = project_back(
-        n_dp, n_fsdp, tokens, normed, projected_grad, qkv_full, middle_grad, gain_one[None], others, 4
-    )
-    devices = n_dp * n_fsdp
-    mine = jnp.concatenate([mine_qkv] + [part.reshape(-1, 48, 384) for part in (mine_out, mine_up, mine_down)], axis=0)
-    numbers = jnp.arange(BLOCKS, dtype=jnp.int32)
-    ranks = jnp.arange(devices, dtype=jnp.int32)
-    blocks_of = jnp.sum(jnp.where(owners[None, :] == ranks[:, None], numbers[None, :], 0), axis=1).astype(jnp.int32)
-    rank = lax.axis_index(("dp", "fsdp"))
-    owning = jnp.any(owners == rank)
-    flags = jnp.stack([owning, blocks_of[rank] >= 4 + FF // D]).astype(jnp.int32)
+        n_dp, n_fsdp, tokens, normed, projected_grad, qkv_full, middle_grad, gain_one[None],
+        sums, grad_bias_out, grad_bias_up, TAIL_PLAN, 4
+    )
+    exchanged = owner_exchange(
+        n_dp, n_fsdp, owners, (mine_qkv.reshape(-1, 384), mine_out, mine_up, mine_down), mine_small, inverse_roots[0], 5
+    )
     masters = (qkv_weight, out_weight, up_weight, down_weight)
-    *results, whole_small, new_small, new_statistics = owner_exchange(
-        n_dp, n_fsdp, blocks_of, owners, flags, mine, mine_small, statistics[0], inverse_roots[0],
-        masters, small_params.reshape(-1, 128), (step_rate, small_rate), 5,
+    *results, whole_small, new_small, new_statistics = finish_step(
+        n_dp, n_fsdp, owners, exchanged, masters, small_params.reshape(-1, 128), statistics[0], (step_rate, small_rate)
     )
     shard_qkv, shard_out, shard_up, shard_down, new_qkv, new_out, new_up, new_down = results
     whole_small, new_small = whole_small.reshape(-1), new_small.reshape(-1)
@@ -1648,12 +1678,6 @@
         new_down,
         new_small,
     )
-
-
-def whole_of(pieces):
-    rows, columns = pieces.shape[-2:]
-    folded = pieces.reshape(pieces.shape[0] * pieces.shape[1], -1, columns)
-    return folded.transpose(1, 0, 2).reshape(folded.shape[1], -1)
 
 
 def solution(mesh):

time: 386 us -> 358 us (0.927)
  local copies, waits for them, and re-layouts: 26.1 us -> 9.51 us
  other arithmetic: 11.3 us -> 1.23 us
    pallas_call x1 -> x2, Pallas kernels: 77.7 us -> 90.8 us  [the longest x1 82.3 us: owner_exchange(): pl.pallas_call(kernel, out_shape=TILES + TILES + [jax.ShapeDtypeStruct((c...]
    unnamed x46 -> x8, local copies, waits for them, and re-layouts: 16.8 us -> 6.75 us
    pallas_call x1, Pallas kernels: 44.3 us -> 36.3 us  [project_back(): pl.pallas_call(kernel, out_shape=[shape((n_blocks, 48, 384), low), shape(...]
    convert_element_type x4 -> x0, other arithmetic: 5.99 us -> none  [the longest x1 1.64 us: local_staged(): up_weight.astype(jnp.bfloat16)]
    pallas_call x1, Pallas kernels: 42.7 us -> 37.9 us  [gather_first(): pl.pallas_call(kernel, out_shape=[jax.ShapeDtypeStruct(grid.shape(o, *s.s...]
where the time goes in v5:
time: 358 us; the launch traced here: 351 us
  Pallas kernels  339 us (95%)
  local copies, waits for them, and re-layouts  9.51 us (3%)
    pallas_call x1, Pallas kernels, owner_exchange(): pl.pallas_call(kernel, out_shape=TILES + TILES + [jax.ShapeDtypeStruct((c...  82.3 us
    pallas_call x1, Pallas kernels, grads_attend_back(): pl.pallas_call(kernel, out_shape=[jax.ShapeDtypeStruct((3, slots, d), low...  75.1 us
    pallas_call x1, Pallas kernels, project_attend(): pl.pallas_call(kernel, out_shape=[jax.ShapeDtypeStruct((slots, d), low),...  60.3 us
    pallas_call x1, Pallas kernels, middle_layer(): pl.pallas_call(middle_kernel, out_shape=[shape((count, d), low), shape((c...  38.8 us
    pallas_call x1, Pallas kernels, gather_first(): pl.pallas_call(kernel, out_shape=[jax.ShapeDtypeStruct(grid.shape(o, *s.s...  37.9 us
    pallas_call x1, Pallas kernels, project_back(): pl.pallas_call(kernel, out_shape=[shape((n_blocks, 48, 384), low), shape(...  36.3 us
    pallas_call x1, Pallas kernels, finish_step(): pl.pallas_call(kernel, out_shape=results + [jax.ShapeDtypeStruct(stats.sh...  8.43 us

profile of v5, /device:TPU:27, one launch (start us, length us, event | category | flops | bytes accessed | tf_op | source)
XLA Modules:
  0.0 351.5 jit_solution(15326161549089311336)
XLA Ops:
  1.3 0.7 slice.45
  2.0 0.6 slice.46.bias_up
  2.6 0.8 fusion
  3.4 0.0 copy-start.1
  3.5 0.6 pad_maximum_fusion.1.rows
  4.1 0.6 pad_maximum_fusion.2.rows
  4.7 0.6 broadcast_in_dim.11.bias_ref
  5.3 1.9 copy.26.refs_2_.w_down
  7.2 37.9 %gather_first.1 = (bf16[2,2,4,2,96,576]{5,4,3,2,1,0:T(8,128)(2,1)}, bf16[2,2,4,2,96,192]{5,4,3,2,1,0:T(8,128)(2,1)}, bf16[2,2,4,2,96,768]{5,4,3,2,1,0:T(8,128)(2,1)}) custom-call(f32[96,576]{1,0:T(8,128)} %w_qkv.1, f32[96,192]{1,0:T(8,128)} %w_out.1, f32[96,768]{1,0:T(8,128)} %w_up.1), custom_call_target="tpu_custom_call" | custom-call | tf_op jit(solution)/shard_map/gather_first/pallas_call | solution.py:346
  45.1 60.3 %project_attend.1 = (bf16[1024,768]{1,0:T(8,128)(2,1)}, bf16[1024,2304]{1,0:T(8,128)(2,1)}, bf16[768,2304]{1,0:T(8,128)(2,1)}, bf16[1024,768]{1,0:T(8,128)(2,1)}...) custom-call(s32[1]{0:T(128)S(6)} %copy.33.count_ref, ...), custom_call_target="tpu_custom_call", output_to_operand_aliasing={{5}: (5, {}), {6}: (6, {})} | custom-call | tf_op jit(solution)/shard_map/project_attend/pallas_call | solution.py:603
  105.4 0.0 copy-done.1
  105.4 38.8 %middle_layer.1 = (bf16[1024,768]{1,0:T(8,128)(2,1)}, bf16[1024,768]{1,0:T(8,128)(2,1)}, bf16[1024,3072]{1,0:T(8,128)(2,1)}, bf16[1024,3072]{1,0:T(8,128)(2,1)},...) custom-call(bf16[1024,768]{1,0:T(8,128)(2,1)} %x_h.1, ...), custom_call_target="tpu_custom_call" | custom-call | tf_op jit(solution)/shard_map/middle_layer/pallas_call | solution.py:1055
  144.2 75.1 %grads_attend_back.1 = (bf16[3,1024,768]{2,1,0:T(8,128)(2,1)}, bf16[192,384]{1,0:T(8,128)(2,1)}, bf16[192,384]{1,0:T(8,128)(2,1)}, bf16[48,384]{1,0:T(8,128)(2,1...) custom-call(s32[1]{0:T(128)S(6)} %copy.33.count_ref, bf16[1024,2304]{1,0:T(8,128)(2,1)} %get-tuple-element.72.q_ref.k_ref.v_ref, ...), custom_call_target="tpu_custom_call" | custom-call | tf_op jit(solution)/shard_map/grads_attend_back/pallas_call | solution.py:717
  219.3 36.3 %project_back.1 = (bf16[3,48,384]{2,1,0:T(8,128)(2,1)}, bf16[16,128]{1,0:T(8,128)(2,1)}, bf16[1024,768]{1,0:T(8,128)(2,1)}) custom-call(bf16[1024,768]{1,0:T(8,128)(2,1)} %x_h.1, bf16[1024,768]{1,0:T(8,128)(2,1)} %get-tuple-element.71.normed_h, bf16[3,1024,768]{2,1,0:T(8,128)(2,1)} %get-tuple-element.79.dp_h, bf16[768,2304]{1,0:T(8,128)(2,1)} %get-tuple-element.80.weight_h, ...), custom_call_target="tpu_custom_call" | custom-call | tf_op jit(solution)/shard_map/project_back/pallas_call | solution.py:1147
  255.6 82.3 %owner_exchange.1 = (bf16[2,96,384]{2,1,0:T(8,128)(2,1)}, bf16[2,96,384]{2,1,0:T(8,128)(2,1)}, bf16[2,96,384]{2,1,0:T(8,128)(2,1)}, bf16[192,384]{1,0:T(8,128)(2...) custom-call(s32[12]{0:T(128)} %owners_ref.3, ...), custom_call_target="tpu_custom_call" | custom-call | tf_op jit(solution)/shard_map/owner_exchange/pallas_call | solution.py:918
  337.9 0.0 copy-start
  337.9 8.4 %finish_step.1 = (f32[96,576]{1,0:T(8,128)}, f32[96,192]{1,0:T(8,128)}, f32[96,768]{1,0:T(8,128)}, f32[384,192]{1,0:T(8,128)}, f32[96,576]{1,0:T(8,128)}, /*inde...) custom-call(s32[12]{0:T(128)} %owners_ref.3, ...), custom_call_target="tpu_custom_call" | custom-call | tf_op jit(solution)/shard_map/finish_step/pallas_call | solution.py:976
  346.4 1.9 copy.28
  348.2 1.9 copy.29
  350.1 0.0 copy-done
  350.1 1.1 copy.34
  (8 shorter events, 0.0 us)
Async XLA Ops:
  3.4 102.0 %copy-start.1 = (f32[1,768]{1,0:T(1,128)}, f32[1,768]{1,0:T(1,128)S(1)}, u32[]{:S(2)}) copy-start(f32[1,768]{1,0:T(1,128)S(1)} %stack.24.gain_ref) | copy-start | bytes 9220
  337.9 12.2 %copy-start = (bf16[1024,768]{1,0:T(8,128)(2,1)S(1)}, bf16[1024,768]{1,0:T(8,128)(2,1)}, u32[]{:S(2)}) copy-start(bf16[1024,768]{1,0:T(8,128)(2,1)} %get-tuple-element.148) | copy-start | bytes 4718596

commit v6 on v5

--- a/solution.py
+++ b/solution.py
@@ -55,11 +55,13 @@
         out += [{"dp": self.z * self.X + self.x, "fsdp": self.y * 2 + 1 - self.c}]
         return out
 
-    def barrier(self):
+    def barrier(self, between=None):
         sem = pltpu.get_barrier_semaphore()
         peers = self.peers()
         for peer in peers:
             pl.semaphore_signal(sem, inc=1, device_id=peer, device_id_type=MESH)
+        if between is not None:
+            between()
         pl.semaphore_wait(sem, len(peers))
 
 
@@ -330,8 +332,11 @@
     def kernel(*refs):
         g = grid.here()
         low = refs[2 * count : 3 * count]
-        low[0][...] = refs[0][...].astype(jnp.bfloat16)
-        g.barrier()
+
+        def first():
+            low[0][...] = refs[0][...].astype(jnp.bfloat16)
+
+        g.barrier(first)
         work = gather_jobs(g, orders, jobs, low, refs[count : 2 * count], refs[3 * count :])
         work[0].step(0)
         for n in range(1, count):
@@ -526,7 +531,7 @@
     out_ref[2] = dv_sum[...].astype(jnp.bfloat16)
 
 
-def project_attend(n_dp, n_fsdp, counts, tokens, weight_pieces, norm_rows, bias, pieces, fresh, orders, plan, collective_id,
+def project_attend(n_dp, n_fsdp, counts, tokens, weight_pieces, small_rows, pieces, fresh, orders, plan, collective_id,
                    size=512, block=256):
     slots, d = tokens.shape
     width = weight_pieces.shape[0] * weight_pieces.shape[2]
@@ -537,10 +542,9 @@
     jobs = plan["jobs"]
     waits = [job[0] < begun for job in jobs]
     shapes = [jax.ShapeDtypeStruct(p.shape, p.dtype) for p in pieces]
-    turned = [a.shape[::-1] for a in fresh]
-    shapes += [jax.ShapeDtypeStruct(grid.shape(o, *a), jnp.bfloat16) for a, o in zip(turned, orders[begun:])]
-
-    def kernel(count_ref, x, w_pieces, rows, bias_ref, *refs):
+    shapes += [jax.ShapeDtypeStruct(grid.shape(o, *a.shape), jnp.bfloat16) for a, o in zip(fresh, orders[begun:])]
+
+    def kernel(count_ref, x, w_pieces, rows, *refs):
         (h_ref, p_ref, w_ref, o_ref, lse_ref), outs = refs[count : count + 5], refs[count + 5 : 2 * count + 5]
         projected, q_heads, v_turned = refs[2 * count + 5 : 2 * count + 8]
         low_fresh = refs[2 * count + 8 : 2 * count + 8 + len(fresh)]
@@ -557,9 +561,11 @@
 
         @pl.when(step == 0)
         def _():
-            for ref, master in zip(low_fresh, refs[begun:count]):
-                ref[...] = master[...].T.astype(jnp.bfloat16)
-            g.barrier()
+            def first():
+                for ref, master in zip(low_fresh, refs[begun:count]):
+                    ref[...] = master[...].astype(jnp.bfloat16)
+
+            g.barrier(first)
 
         for when in range(head + pairs):
             if when in plan:
@@ -576,7 +582,8 @@
             unit, spread = centered(x[...].astype(jnp.float32))
             low = (unit * rows[0:1] + rows[1:2]).astype(jnp.bfloat16)
             h_ref[...] = low
-            result = (plain_dot(low, w_ref[...]) + bias_ref[...]).astype(jnp.bfloat16)
+            bias = jnp.concatenate([rows[4:5], jnp.zeros((1, d), jnp.float32), rows[5:6]], axis=1)
+            result = (plain_dot(low, w_ref[...]) + bias).astype(jnp.bfloat16)
             p_ref[...] = result
             projected[pl.ds(pl.multiple_of(step * block, block), block), :] = result
 
@@ -607,18 +614,18 @@
                    jax.ShapeDtypeStruct((pairs, 2, slots), jnp.float32)] + shapes,
         grid_spec=pltpu.PrefetchScalarGridSpec(
             num_scalar_prefetch=1, grid=(head + pairs,),
-            in_specs=[row(d), whole(weight_pieces), whole(norm_rows), whole(bias)] + [ANY] * begun + [whole(a) for a in fresh],
+            in_specs=[row(d), whole(weight_pieces), whole(small_rows)] + [ANY] * begun + [whole(a) for a in fresh],
             out_specs=[row(d), row(width), pl.BlockSpec((d, width), lambda s, n: (0, 0)),
                        pl.BlockSpec((slots, PAIR), lambda s, n: (0, pair_at(s))),
                        pl.BlockSpec((1, 2, slots), lambda s, n: (pair_at(s), 0, 0))] + [ANY] * count,
             scratch_shapes=[pltpu.VMEM((slots, width), low), pltpu.VMEM((2, slots, PAIR), low),
-                            pltpu.VMEM((2, PAIR, slots), low)] + [pltpu.VMEM(a, low) for a in turned]
+                            pltpu.VMEM((2, PAIR, slots), low)] + [pltpu.VMEM(a.shape, low) for a in fresh]
             + gather_scratch(grid, len(jobs))),
-        input_output_aliases={5 + n: 5 + n for n in range(begun)},
+        input_output_aliases={4 + n: 5 + n for n in range(begun)},
         compiler_params=pltpu.CompilerParams(vmem_limit_bytes=56 * 1024 * 1024, collective_id=collective_id,
                                              has_side_effects=True),
         name="project_attend",
-    )(counts, tokens, weight_pieces, norm_rows, bias, *pieces, *fresh)
+    )(counts, tokens, weight_pieces, small_rows, *pieces, *fresh)
 
 
 FIRST_PLAN = (
@@ -800,7 +807,7 @@
 TILES = [jax.ShapeDtypeStruct((2, 96, 384), jnp.bfloat16)] * 3 + [jax.ShapeDtypeStruct((192, 384), jnp.bfloat16)]
 
 
-def meet_all(g, n_dp, n_fsdp):
+def meet_all(g, n_dp, n_fsdp, between):
     count = n_dp * n_fsdp
     me = (g.z * g.X + g.x) * n_fsdp + g.y * 2 + g.c
     sem = pltpu.get_barrier_semaphore()
@@ -808,6 +815,7 @@
     peers = [{"dp": rank // n_fsdp, "fsdp": rank % n_fsdp} for rank in ranks]
     for peer in peers:
         pl.semaphore_signal(sem, inc=1, device_id=peer, device_id_type=MESH)
+    between(me)
     pl.semaphore_wait(sem, count - 1)
     return me, ranks, peers
 
@@ -829,7 +837,7 @@
     band = jnp.concatenate([qkv[0].astype(wide), qkv[1].astype(wide)], axis=1)
     half = out[g.y].astype(wide)
     return [jnp.where(odd, band[:, 192:], band[:, :576]), jnp.where(odd, half[:, 192:], half[:, :192]),
-            jnp.concatenate([up[0].astype(wide), up[1].astype(wide)], axis=1), down[...].astype(wide).T]
+            jnp.concatenate([up[0].astype(wide), up[1].astype(wide)], axis=1), down[...].astype(wide)]
 
 
 def owner_exchange(n_dp, n_fsdp, owners, mine, small, roots, collective_id):
@@ -843,14 +851,7 @@
                qkv, out, up, down, s_qkv, s_out, s_up, s_down, all_small, block, turned,
                u, slots, got, got_steps, u_steps, roots, local, send, recv):
         g = grid.here()
-        me, ranks, peers = meet_all(g, n_dp, n_fsdp)
         load = pltpu.make_async_copy(roots_hbm, roots, local.at[0])
-        load.start()
-        first = 0
-        for ref in (qkv_ref, out_ref, up_ref, down_ref):
-            part = ref.shape[0] // 48
-            u[first : first + part] = ref[...].reshape(part, 48, 384)
-            first += part
 
         def owned(n):
             found = 0
@@ -858,11 +859,23 @@
                 found = jnp.where(owners_ref[b] == n, b, found)
             return found
 
-        def fill(n, carry):
-            slots[n] = u[owned(n)]
-            return carry
-
-        lax.fori_loop(0, count, fill, 0)
+        def first(me):
+            load.start()
+            at = 0
+            for ref in (qkv_ref, out_ref, up_ref, down_ref):
+                part = ref.shape[0] // 48
+                u[at : at + part] = ref[...].reshape(part, 48, 384)
+                at += part
+
+            def fill(n, carry):
+                slots[n] = u[owned(n)]
+                return carry
+
+            lax.fori_loop(0, count, fill, 0)
+            got[me] = slots[me]
+            all_small[me] = small_ref[...]
+
+        me, ranks, peers = meet_all(g, n_dp, n_fsdp, first)
         lane = 0
         copies, small_copies, step_copies = [], [], []
         for rank, peer in zip(ranks, peers):
@@ -871,8 +884,6 @@
             step_copies.append(remote(slots.at[rank], got_steps.at[me], send, recv, lane + 2, peer))
             lane += 3
         start_all(copies)
-        got[me] = slots[me]
-        all_small[me] = small_ref[...]
         load.wait()
         kind = jnp.where(owned(me) >= 8, 1, 0)
         arrived(copies)
@@ -998,7 +1009,7 @@
     return (scaled - mean - unit * along) * spread
 
 
-def middle_kernel(x, attended, dy, out_pieces, up_w, down_w, rows, bias_up,
+def middle_kernel(x, attended, dy, out_pieces, up_w, down_w, rows,
                   layer, h2, active, hidden_grad, middle_grad, branch_grad, attended_grad, sums, out_w):
     @pl.when(pl.program_id(0) == 0)
     def _():
@@ -1006,7 +1017,7 @@
         for n in range(out_pieces.shape[0]):
             out_w[:, n * part : (n + 1) * part] = out_pieces[n]
 
-    gain, shift, bias_out, bias_down = rows[0:1], rows[1:2], rows[2:3], rows[3:4]
+    gain, shift, bias_out, bias_down = rows[2:3], rows[3:4], rows[6:7], rows[7:8]
     middle = x[...].astype(jnp.float32) + (plain_dot(attended[...], out_w[...]) + bias_out)
     unit, spread = centered(middle)
     normed = (unit * gain + shift).astype(jnp.bfloat16)
@@ -1018,7 +1029,7 @@
     y = jnp.zeros_like(middle)
     dh = jnp.zeros_like(middle)
     for panel in range(panels):
-        hidden = plain_dot(normed, up_w[panel]) + bias_up[panel : panel + 1]
+        hidden = plain_dot(normed, up_w[panel]) + rows[8 + panel : 9 + panel]
         passed = 0.5 + 0.5 * lax.erf(hidden * (0.5**0.5))
         z = (hidden * passed).astype(jnp.bfloat16)
         slope = passed + hidden * (jnp.exp(-0.5 * hidden * hidden) * 0.3989422804014327)
@@ -1045,7 +1056,7 @@
     sums[2:3] += jnp.sum(wide, axis=0, keepdims=True)
 
 
-def middle_layer(tokens, attended, cotangent, out_w, up_w, down_w, rows, bias_up, block=256):
+def middle_layer(tokens, attended, cotangent, out_w, up_w, down_w, rows, block=256):
     count, d = tokens.shape
     ff = up_w.shape[0] * up_w.shape[2]
     row = lambda width: pl.BlockSpec((block, width), lambda r: (r, 0))
@@ -1057,12 +1068,12 @@
         out_shape=[shape((count, d), low), shape((count, d), low), shape((count, ff), low), shape((count, ff), low),
                    shape((count, d), wide), shape((count, d), low), shape((count, d), low), shape((8, d), wide)],
         grid=(count // block,),
-        in_specs=[row(d), row(d), row(d)] + [whole(a) for a in (out_w, up_w, down_w, rows, bias_up)],
+        in_specs=[row(d), row(d), row(d)] + [whole(a) for a in (out_w, up_w, down_w, rows)],
         out_specs=[row(d), row(d), row(ff), row(ff), row(d), row(d), row(d), pl.BlockSpec((8, d), lambda r: (0, 0))],
         scratch_shapes=[pltpu.VMEM((d, d), low)],
         compiler_params=pltpu.CompilerParams(vmem_limit_bytes=60 * 1024 * 1024),
         name="middle_layer",
-    )(tokens, attended, cotangent, out_w, up_w, down_w, rows, bias_up)
+    )(tokens, attended, cotangent, out_w, up_w, down_w, rows)
 
 
 def project_back(n_dp, n_fsdp, tokens, normed, projected_grad, weight, middle_grad, gain, sums, bias_out, bias_up, plan,
@@ -1080,13 +1091,16 @@
         left, parts, small_parts, rows, packed, local = refs[6:12]
         scratch = refs[12:]
         g = grid.here()
-        g.barrier()
         loads = [pltpu.make_async_copy(a, b, local.at[n])
                  for n, (a, b) in enumerate(((normed_h, h), (dp_h, dp), (weight_h, w), (x_h, x), (middle_h, middle)))]
-        for load in loads:
-            load.start()
-        loads[0].wait()
-        left[...] = h[...].astype(wide).T.astype(low)
+
+        def first():
+            for load in loads:
+                load.start()
+            loads[0].wait()
+            left[...] = h[...].astype(wide).T.astype(low)
+
+        g.barrier(first)
         loads[1].wait()
         work = scatter_jobs(g, ["j"] * (n_blocks + 1), jobs, [parts.at[n] for n in range(n_blocks)] + [small_parts], scratch)
         for n in range(n_blocks):
@@ -1112,7 +1126,7 @@
             at = slice(n * block, (n + 1) * block)
             dh = last_dot(dp[0, at], w[:, :d]) + last_dot(dp[1, at], w[:, d : 2 * d]) + last_dot(dp[2, at], w[:, 2 * d :])
             unit, spread = centered(x[at].astype(wide))
-            out[at] = (middle[at] + norm_back(dh, unit, spread, gain_ref[...])).astype(low)
+            out[at] = (middle[at] + norm_back(dh, unit, spread, gain_ref[0:1])).astype(low)
             scaled, shifted = jnp.sum(dh * unit, axis=0, keepdims=True), jnp.sum(dh, axis=0, keepdims=True)
             rows[0:1] = scaled if n == 0 else rows[0:1] + scaled
             rows[1:2] = shifted if n == 0 else rows[1:2] + shifted
@@ -1618,23 +1632,13 @@
     owners,
 ):
     n_dp, n_fsdp = sizes
-    (
-        gain_one,
-        shift_one,
-        gain_two,
-        shift_two,
-        bias_query,
-        bias_value,
-        bias_out,
-        bias_down,
-        bias_up,
-    ) = unpack(small_params)
+    small_rows = small_params.reshape(-1, D)
+    down_turned = down_weight.T
     orders = ("j", "j", "j", "i")
     qkv_pieces, *begun = gather_first(n_dp, n_fsdp, (qkv_weight, out_weight, up_weight), orders[:3], FIRST_PLAN, 1)
-    bias_qkv = jnp.concatenate([bias_query, jnp.zeros((D,), jnp.float32), bias_value])
     normed, projected, qkv_full, attended, log_totals, out_pieces, up_pieces, down_pieces = project_attend(
-        n_dp, n_fsdp, counts, tokens, qkv_pieces.reshape(n_fsdp, D, 3 * D // n_fsdp), jnp.stack([gain_one, shift_one]),
-        bias_qkv[None], begun, (down_weight,), orders[1:], FORWARD_PLAN, 2,
+        n_dp, n_fsdp, counts, tokens, qkv_pieces.reshape(n_fsdp, D, 3 * D // n_fsdp), small_rows,
+        begun, (down_turned,), orders[1:], FORWARD_PLAN, 2,
     )
     layer_rows, normed_two, active, hidden_grad, middle_grad, branch_grad, attended_grad, sums = middle_layer(
         tokens,
@@ -1643,21 +1647,20 @@
         out_pieces.reshape(n_fsdp, D, D // n_fsdp),
         up_pieces.reshape(n_fsdp, D, FF // n_fsdp),
         down_pieces.reshape(n_dp, D, FF // n_dp),
-        jnp.stack([gain_two, shift_two, bias_out, bias_down]),
-        bias_up.reshape(n_fsdp, FF // n_fsdp),
+        small_rows,
     )
     projected_grad, mine_down, mine_up, mine_out, grad_bias_up, grad_bias_out = grads_attend_back(
         n_dp, n_fsdp, counts, projected, attended, attended_grad, log_totals,
         cotangent, active, normed_two, hidden_grad, branch_grad, BACKWARD_PLAN, 3,
     )
     mine_qkv, mine_small, input_grad = project_back(
-        n_dp, n_fsdp, tokens, normed, projected_grad, qkv_full, middle_grad, gain_one[None],
+        n_dp, n_fsdp, tokens, normed, projected_grad, qkv_full, middle_grad, small_rows,
         sums, grad_bias_out, grad_bias_up, TAIL_PLAN, 4
     )
     exchanged = owner_exchange(
         n_dp, n_fsdp, owners, (mine_qkv.reshape(-1, 384), mine_out, mine_up, mine_down), mine_small, inverse_roots[0], 5
     )
-    masters = (qkv_weight, out_weight, up_weight, down_weight)
+    masters = (qkv_weight, out_weight, up_weight, down_turned)
     *results, whole_small, new_small, new_statistics = finish_step(
         n_dp, n_fsdp, owners, exchanged, masters, small_params.reshape(-1, 128), statistics[0], (step_rate, small_rate)
     )
@@ -1669,13 +1672,13 @@
         shard_qkv,
         shard_out,
         shard_up,
-        shard_down,
+        shard_down.T,
         whole_small,
         new_statistics[None],
         new_qkv,
         new_out,
         new_up,
-        new_down,
+        new_down.T,
         new_small,
     )
 

time: 358 us -> 347 us (0.969)
  local copies, waits for them, and re-layouts: 9.51 us -> 2.55 us
    unnamed x8 -> x3, local copies, waits for them, and re-layouts: 6.75 us -> 1.15 us
where the time goes in v6:
time: 347 us; the launch traced here: 340 us
  Pallas kernels  336 us (97%)
    pallas_call x1, Pallas kernels, owner_exchange(): pl.pallas_call(kernel, out_shape=TILES + TILES + [jax.ShapeDtypeStruct((c...  81.8 us
    pallas_call x1, Pallas kernels, grads_attend_back(): pl.pallas_call(kernel, out_shape=[jax.ShapeDtypeStruct((3, slots, d), low...  75 us
    pallas_call x1, Pallas kernels, project_attend(): pl.pallas_call(kernel, out_shape=[jax.ShapeDtypeStruct((slots, d), low),...  60.1 us
    pallas_call x1, Pallas kernels, middle_layer(): pl.pallas_call(middle_kernel, out_shape=[shape((count, d), low), shape((c...  38.7 us
    pallas_call x1, Pallas kernels, gather_first(): pl.pallas_call(kernel, out_shape=[jax.ShapeDtypeStruct(grid.shape(o, *s.s...  37.9 us
    pallas_call x1, Pallas kernels, project_back(): pl.pallas_call(kernel, out_shape=[shape((n_blocks, 48, 384), low), shape(...  34 us
    pallas_call x1, Pallas kernels, finish_step(): pl.pallas_call(kernel, out_shape=results + [jax.ShapeDtypeStruct(stats.sh...  8.25 us

profile of v6, /device:TPU:27, one launch (start us, length us, event | category | flops | bytes accessed | tf_op | source)
XLA Modules:
  0.0 340.1 jit_solution(17235531242167679835)
XLA Ops:
  1.3 1.4 reshape.54.rows.gain_ref
  2.7 37.9 %gather_first.1 = (bf16[2,2,4,2,96,576]{5,4,3,2,1,0:T(8,128)(2,1)}, bf16[2,2,4,2,96,192]{5,4,3,2,1,0:T(8,128)(2,1)}, bf16[2,2,4,2,96,768]{5,4,3,2,1,0:T(8,128)(2,1)}) custom-call(f32[96,576]{1,0:T(8,128)} %w_qkv.1, f32[96,192]{1,0:T(8,128)} %w_out.1, f32[96,768]{1,0:T(8,128)} %w_up.1), custom_call_target="tpu_custom_call" | custom-call | tf_op jit(solution)/shard_map/gather_first/pallas_call | solution.py:351
  40.6 60.1 %project_attend.1 = (bf16[1024,768]{1,0:T(8,128)(2,1)}, bf16[1024,2304]{1,0:T(8,128)(2,1)}, bf16[768,2304]{1,0:T(8,128)(2,1)}, bf16[1024,768]{1,0:T(8,128)(2,1)}...) custom-call(s32[1]{0:T(128)S(6)} %copy.29.count_ref, ...), custom_call_target="tpu_custom_call", output_to_operand_aliasing={{5}: (4, {}), {6}: (5, {})} | custom-call | tf_op jit(solution)/shard_map/project_attend/pallas_call | solution.py:610
  100.7 38.7 %middle_layer.1 = (bf16[1024,768]{1,0:T(8,128)(2,1)}, bf16[1024,768]{1,0:T(8,128)(2,1)}, bf16[1024,3072]{1,0:T(8,128)(2,1)}, bf16[1024,3072]{1,0:T(8,128)(2,1)},...) custom-call(bf16[1024,768]{1,0:T(8,128)(2,1)} %x_h.1, ...), custom_call_target="tpu_custom_call" | custom-call | tf_op jit(solution)/shard_map/middle_layer/pallas_call | solution.py:1066
  139.4 75.0 %grads_attend_back.1 = (bf16[3,1024,768]{2,1,0:T(8,128)(2,1)}, bf16[192,384]{1,0:T(8,128)(2,1)}, bf16[192,384]{1,0:T(8,128)(2,1)}, bf16[48,384]{1,0:T(8,128)(2,1...) custom-call(s32[1]{0:T(128)S(6)} %copy.29.count_ref, bf16[1024,2304]{1,0:T(8,128)(2,1)} %get-tuple-element.72.q_ref.k_ref.v_ref, ...), custom_call_target="tpu_custom_call" | custom-call | tf_op jit(solution)/shard_map/grads_attend_back/pallas_call | solution.py:724
  214.4 34.0 %project_back.1 = (bf16[3,48,384]{2,1,0:T(8,128)(2,1)}, bf16[16,128]{1,0:T(8,128)(2,1)}, bf16[1024,768]{1,0:T(8,128)(2,1)}) custom-call(bf16[1024,768]{1,0:T(8,128)(2,1)} %x_h.1, bf16[1024,768]{1,0:T(8,128)(2,1)} %get-tuple-element.71.normed_h, bf16[3,1024,768]{2,1,0:T(8,128)(2,1)} %get-tuple-element.79.dp_h, bf16[768,2304]{1,0:T(8,128)(2,1)} %get-tuple-element.80.weight_h, ...), custom_call_target="tpu_custom_call" | custom-call | tf_op jit(solution)/shard_map/project_back/pallas_call | solution.py:1161
  248.4 81.8 %owner_exchange.1 = (bf16[2,96,384]{2,1,0:T(8,128)(2,1)}, bf16[2,96,384]{2,1,0:T(8,128)(2,1)}, bf16[2,96,384]{2,1,0:T(8,128)(2,1)}, bf16[192,384]{1,0:T(8,128)(2...) custom-call(s32[12]{0:T(128)} %owners_ref.3, ...), custom_call_target="tpu_custom_call" | custom-call | tf_op jit(solution)/shard_map/owner_exchange/pallas_call | solution.py:929
  330.2 0.0 copy-start
  330.2 8.2 %finish_step.1 = (f32[96,576]{1,0:T(8,128)}, f32[96,192]{1,0:T(8,128)}, f32[96,768]{1,0:T(8,128)}, f32[192,384]{1,0:T(8,128)}, f32[96,576]{1,0:T(8,128)}, /*inde...) custom-call(s32[12]{0:T(128)} %owners_ref.3, ...), custom_call_target="tpu_custom_call" | custom-call | tf_op jit(solution)/shard_map/finish_step/pallas_call | solution.py:987
  338.5 0.0 copy-done
  338.5 1.1 copy.30
Async XLA Ops:
  330.2 8.3 %copy-start = (bf16[1024,768]{1,0:T(8,128)(2,1)S(1)}, bf16[1024,768]{1,0:T(8,128)(2,1)}, u32[]{:S(2)}) copy-start(bf16[1024,768]{1,0:T(8,128)(2,1)} %get-tuple-element.127) | copy-start | bytes 4718596

commit v7 on v6

--- a/solution.py
+++ b/solution.py
@@ -629,9 +629,10 @@
 
 
 FIRST_PLAN = (
-    [(0, 0, pl.ds(0, 48)), (0, 0, pl.ds(48, 48)), (1, 0, pl.ds(0, 96)), (2, 0, pl.ds(0, 64)), (2, 1, pl.ds(64, 32))],
-    [(0, 1), (1, 0), (0, 2), (1, 1), (2, 0), (3, 0), (4, 0), (0, 3), (1, 2), (1, 3)],
-    2,
+    [(0, 0, pl.ds(0, 32)), (0, 0, pl.ds(32, 32)), (0, 0, pl.ds(64, 32)), (1, 0, pl.ds(0, 96)), (2, 0, pl.ds(0, 64)),
+     (2, 1, pl.ds(64, 32))],
+    [(1, 0), (0, 1), (2, 0), (1, 1), (0, 2), (2, 1), (3, 0), (4, 0), (5, 0), (1, 2), (0, 3), (2, 2), (1, 3), (2, 3)],
+    3,
 )
 FORWARD_PLAN = {
     "jobs": [(0, 0, pl.ds(0, 96)), (1, 0, pl.ds(0, 64)), (1, 1, pl.ds(64, 32)), (2, 0, pl.ds(0, 192))],
@@ -941,7 +942,7 @@
     )(owners, *mine, small, roots)
 
 
-def finish_step(n_dp, n_fsdp, owners, exchanged, masters, small_params, stats, rates, parts=4):
+def finish_step(n_dp, n_fsdp, owners, exchanged, masters, small_params, stats, rates, parts=2):
     grid = Grid(n_dp, n_fsdp)
     tiles, all_small, block, turned = exchanged[:8], *exchanged[8:]
     d = block.shape[0]

time: 347 us -> 347 us (level)
    pallas_call x1, Pallas kernels: 81.8 us -> 87.3 us  [owner_exchange(): pl.pallas_call(kernel, out_shape=TILES + TILES + [jax.ShapeDtypeStruct((c...]
where the time goes in v7:
time: 347 us; the launch traced here: 341 us
  Pallas kernels  337 us (97%)
    pallas_call x1, Pallas kernels, owner_exchange(): pl.pallas_call(kernel, out_shape=TILES + TILES + [jax.ShapeDtypeStruct((c...  87.3 us
    pallas_call x1, Pallas kernels, grads_attend_back(): pl.pallas_call(kernel, out_shape=[jax.ShapeDtypeStruct((3, slots, d), low...  75.2 us
    pallas_call x1, Pallas kernels, project_attend(): pl.pallas_call(kernel, out_shape=[jax.ShapeDtypeStruct((slots, d), low),...  57.7 us
    pallas_call x1, Pallas kernels, middle_layer(): pl.pallas_call(middle_kernel, out_shape=[shape((count, d), low), shape((c...  38.7 us
    pallas_call x1, Pallas kernels, gather_first(): pl.pallas_call(kernel, out_shape=[jax.ShapeDtypeStruct(grid.shape(o, *s.s...  36.2 us
    pallas_call x1, Pallas kernels, project_back(): pl.pallas_call(kernel, out_shape=[shape((n_blocks, 48, 384), low), shape(...  33.6 us
    pallas_call x1, Pallas kernels, finish_step(): pl.pallas_call(kernel, out_shape=results + [jax.ShapeDtypeStruct(stats.sh...  8.63 us

profile of v7, /device:TPU:27, one launch (start us, length us, event | category | flops | bytes accessed | tf_op | source)
XLA Modules:
  0.0 341.4 jit_solution(9684152968493349914)
XLA Ops:
  1.3 1.4 reshape.54.rows.gain_ref
  2.7 36.2 %gather_first.1 = (bf16[2,2,4,2,96,576]{5,4,3,2,1,0:T(8,128)(2,1)}, bf16[2,2,4,2,96,192]{5,4,3,2,1,0:T(8,128)(2,1)}, bf16[2,2,4,2,96,768]{5,4,3,2,1,0:T(8,128)(2,1)}) custom-call(f32[96,576]{1,0:T(8,128)} %w_qkv.1, f32[96,192]{1,0:T(8,128)} %w_out.1, f32[96,768]{1,0:T(8,128)} %w_up.1), custom_call_target="tpu_custom_call" | custom-call | tf_op jit(solution)/shard_map/gather_first/pallas_call | solution.py:351
  38.9 57.7 %project_attend.1 = (bf16[1024,768]{1,0:T(8,128)(2,1)}, bf16[1024,2304]{1,0:T(8,128)(2,1)}, bf16[768,2304]{1,0:T(8,128)(2,1)}, bf16[1024,768]{1,0:T(8,128)(2,1)}...) custom-call(s32[1]{0:T(128)S(6)} %copy.29.count_ref, ...), custom_call_target="tpu_custom_call", output_to_operand_aliasing={{5}: (4, {}), {6}: (5, {})} | custom-call | tf_op jit(solution)/shard_map/project_attend/pallas_call | solution.py:610
  96.6 38.7 %middle_layer.1 = (bf16[1024,768]{1,0:T(8,128)(2,1)}, bf16[1024,768]{1,0:T(8,128)(2,1)}, bf16[1024,3072]{1,0:T(8,128)(2,1)}, bf16[1024,3072]{1,0:T(8,128)(2,1)},...) custom-call(bf16[1024,768]{1,0:T(8,128)(2,1)} %x_h.1, ...), custom_call_target="tpu_custom_call" | custom-call | tf_op jit(solution)/shard_map/middle_layer/pallas_call | solution.py:1067
  135.3 75.2 %grads_attend_back.1 = (bf16[3,1024,768]{2,1,0:T(8,128)(2,1)}, bf16[192,384]{1,0:T(8,128)(2,1)}, bf16[192,384]{1,0:T(8,128)(2,1)}, bf16[48,384]{1,0:T(8,128)(2,1...) custom-call(s32[1]{0:T(128)S(6)} %copy.29.count_ref, bf16[1024,2304]{1,0:T(8,128)(2,1)} %get-tuple-element.72.q_ref.k_ref.v_ref, ...), custom_call_target="tpu_custom_call" | custom-call | tf_op jit(solution)/shard_map/grads_attend_back/pallas_call | solution.py:725
  210.5 33.6 %project_back.1 = (bf16[3,48,384]{2,1,0:T(8,128)(2,1)}, bf16[16,128]{1,0:T(8,128)(2,1)}, bf16[1024,768]{1,0:T(8,128)(2,1)}) custom-call(bf16[1024,768]{1,0:T(8,128)(2,1)} %x_h.1, bf16[1024,768]{1,0:T(8,128)(2,1)} %get-tuple-element.71.normed_h, bf16[3,1024,768]{2,1,0:T(8,128)(2,1)} %get-tuple-element.79.dp_h, bf16[768,2304]{1,0:T(8,128)(2,1)} %get-tuple-element.80.weight_h, ...), custom_call_target="tpu_custom_call" | custom-call | tf_op jit(solution)/shard_map/project_back/pallas_call | solution.py:1162
  244.1 87.3 %owner_exchange.1 = (bf16[2,96,384]{2,1,0:T(8,128)(2,1)}, bf16[2,96,384]{2,1,0:T(8,128)(2,1)}, bf16[2,96,384]{2,1,0:T(8,128)(2,1)}, bf16[192,384]{1,0:T(8,128)(2...) custom-call(s32[12]{0:T(128)} %owners_ref.3, ...), custom_call_target="tpu_custom_call" | custom-call | tf_op jit(solution)/shard_map/owner_exchange/pallas_call | solution.py:930
  331.4 0.0 copy-start
  331.4 8.6 %finish_step.1 = (f32[96,576]{1,0:T(8,128)}, f32[96,192]{1,0:T(8,128)}, f32[96,768]{1,0:T(8,128)}, f32[192,384]{1,0:T(8,128)}, f32[96,576]{1,0:T(8,128)}, /*inde...) custom-call(s32[12]{0:T(128)} %owners_ref.3, ...), custom_call_target="tpu_custom_call" | custom-call | tf_op jit(solution)/shard_map/finish_step/pallas_call | solution.py:988
  340.0 0.0 copy-done
  340.0 1.1 copy.30
Async XLA Ops:
  331.4 8.6 %copy-start = (bf16[1024,768]{1,0:T(8,128)(2,1)S(1)}, bf16[1024,768]{1,0:T(8,128)(2,1)}, u32[]{:S(2)}) copy-start(bf16[1024,768]{1,0:T(8,128)(2,1)} %get-tuple-element.127) | copy-start | bytes 4718596
